TPU v7x, 32 devices: a whole 2x2x4 slice. The times are simulated.
32 devices in a mesh: seq: 8 (over y, x, core), fsdp: 4 (over z).
Axes of the slice: x: 2, y: 2, z: 4, core: 2. Of those that a mesh axis runs over, the one named last changes fastest.
Arguments:
- tokens: bfloat16 [8192, 2048], P(('seq', 'fsdp')), may hold values from -6 to 6
- cotangent: bfloat16 [8192, 2048], P(('seq', 'fsdp')), may hold values from -6 to 6
- lengths: int32 [4], replicated, may hold values from 1 to 8192, as said below
- offsets: int32 [4], replicated, may hold values from 0 to 63, as said below
- deal: int32 [64], replicated, may hold values from 0 to 63, as said below
- norm_gain1: float32 [2048], P(('seq', 'fsdp')), may hold values from 0.1 to 1.9
- w_branch: float32 [2048, 2560], P(('seq', 'fsdp')), may hold values from -0.125 to 0.125
- w_input: float32 [2048, 2560], P(('seq', 'fsdp')), may hold values from -0.125 to 0.125
- conv_kernel: float32 [4, 2560], P(None, ('seq', 'fsdp')), may hold values from -3 to 3
- conv_bias: float32 [2560], P(('seq', 'fsdp')), may hold values from -3 to 3
- gate_rec: float32 [2560, 160], P(('seq', 'fsdp')), may hold values from -0.5 to 0.5
- bias_rec: float32 [2560], P(('seq', 'fsdp')), may hold values from -4 to 4
- gate_in: float32 [2560, 160], P(('seq', 'fsdp')), may hold values from -0.5 to 0.5
- bias_in: float32 [2560], P(('seq', 'fsdp')), may hold values from -4 to 4
- decay_param: float32 [2560], P(('seq', 'fsdp')), may hold values from 5 to 16
- w_out: float32 [2560, 2048], P(('seq', 'fsdp')), may hold values from -0.25 to 0.25
- norm_gain2: float32 [2048], P(('seq', 'fsdp')), may hold values from 0.1 to 1.9
- w_gate: float32 [2048, 6144], P(('seq', 'fsdp')), may hold values from -0.125 to 0.125
- w_up: float32 [2048, 6144], P(('seq', 'fsdp')), may hold values from -0.125 to 0.125
- w_down: float32 [6144, 2048], P(('seq', 'fsdp')), may hold values from -0.109375 to 0.109375
Outputs:
- mixed: bfloat16 [8192, 2048], P(('seq', 'fsdp'))
- tokens_grad: bfloat16 [8192, 2048], P(('seq', 'fsdp'))
- grad_norm_gain1: float32 [2048], P(('seq', 'fsdp'))
- grad_w_branch: float32 [2048, 2560], P(('seq', 'fsdp'))
- grad_w_input: float32 [2048, 2560], P(('seq', 'fsdp'))
- grad_conv_kernel: float32 [4, 2560], P(None, ('seq', 'fsdp'))
- grad_conv_bias: float32 [2560], P(('seq', 'fsdp'))
- grad_gate_rec: float32 [2560, 160], P(('seq', 'fsdp'))
- grad_bias_rec: float32 [2560], P(('seq', 'fsdp'))
- grad_gate_in: float32 [2560, 160], P(('seq', 'fsdp'))
- grad_bias_in: float32 [2560], P(('seq', 'fsdp'))
- grad_decay_param: float32 [2560], P(('seq', 'fsdp'))
- grad_w_out: float32 [2560, 2048], P(('seq', 'fsdp'))
- grad_norm_gain2: float32 [2048], P(('seq', 'fsdp'))
- grad_w_gate: float32 [2048, 6144], P(('seq', 'fsdp'))
- grad_w_up: float32 [2048, 6144], P(('seq', 'fsdp'))
- grad_w_down: float32 [6144, 2048], P(('seq', 'fsdp'))
Inputs may be any that keep to these rules, and one draw needn't show every extreme that they name: deal is a permutation that keeps each block in its row: deal[b] // 8 == b // 8. Sequence s fills logical tokens offsets[s] * 128 to offsets[s] * 128 + lengths[s] - 1 and ends in its last block; offsets rise with s and no two sequences share a block. One sequence, which one varies, begins in the first 8 logical blocks and ends in the last 8. `offsets`: see lengths; a block may belong to no sequence.
All inputs are finite; a program needn't handle non-finite values.
Results may differ from a plain program's by a relative error of at most 0.008.
The roundings to bfloat16 on the way count: a program that leaves them out, or rounds other values in their place, can miss the bound.
Values may be sent and summed in bfloat16 or wider, within the bound.
No kernel may reach another device: no remote copies, remote signals or barrier semaphores. Data moves between devices by JAX's collectives and lax.ppermute only.
A program may use at most 448 MiB of HBM per device.

v0:
```python
import jax
import jax.numpy as jnp
from jax import lax
from jax.sharding import PartitionSpec as P

BLOCK = 128


NORM_EPSILON = 1e-06
GATE_SCALE = 8.0
PRECISE = lax.Precision.HIGHEST


def entering(value, axis, join, neutral, backward):
    count, mine = (lax.axis_size(axis), lax.axis_index(axis))
    pieces = jax.tree.map(lambda part: lax.all_gather(part, axis), value)
    if backward:
        pieces = jax.tree.map(lambda part: part[::-1], pieces)
        mine = count - 1 - mine
    total = jax.tree.map(
        lambda part, zero: jnp.full_like(part, 0) + jnp.asarray(zero, part.dtype), value, neutral
    )

    def turn(position, total):
        longer = join(total, jax.tree.map(lambda part: part[position], pieces))
        return jax.tree.map(lambda new, old: jnp.where(position < mine, new, old), longer, total)

    return lax.fori_loop(0, count - 1, turn, total)


def rms_norm(values, gain_vec):
    inv_scale = lax.rsqrt(jnp.mean(values * values, axis=-1, keepdims=True) + NORM_EPSILON)
    return values * inv_scale * gain_vec


def lru_terms(pre_rec, pre_in, xc_value, decay_value, reset_mask):
    rate_gate = jax.nn.sigmoid(pre_rec)
    entry_gate = jax.nn.sigmoid(pre_in)
    log_keep = -GATE_SCALE * rate_gate * jax.nn.softplus(-decay_value)
    keep_rate = jnp.exp(log_keep) * reset_mask
    drive_in = jnp.sqrt(-jnp.expm1(2.0 * log_keep)) * entry_gate * xc_value
    return (keep_rate, drive_in)


def gated_unit(gate_pre, up_pre):
    return jax.nn.gelu(gate_pre) * up_pre


def chain_join(earlier, later):
    return (earlier[0] * later[0], later[0] * earlier[1] + later[1])


def newest(earlier, later):
    return (jnp.maximum(earlier[0], later[0]), jnp.where(later[0] > 0, later[1], earlier[1]))


def transposed_left(left, right):
    return lax.dot_general(
        left, right, (((0,), (0,)), ((), ())), preferred_element_type=jnp.float32
    )


def transposed_right(left, right):
    return lax.dot_general(
        left, right, (((1,), (1,)), ((), ())), preferred_element_type=jnp.float32
    )


def select_rows(picker, table):
    return jnp.einsum("ak,k...->a...", picker, table, precision=PRECISE)


def as_low(values):
    return values.astype(jnp.bfloat16)


def row_pieces(values):
    return lax.all_gather(values, "fsdp", axis=0, tiled=True)


def forward_chain(pair, combine, identity):
    return entering(pair, "seq", combine, identity, False)


def backward_chain(pair, combine, identity):
    return entering(pair, "seq", combine, identity, True)


def token_places(logical, lengths, offsets):
    within = jnp.arange(BLOCK, dtype=jnp.int32)
    token_place = (logical[:, None] * BLOCK + within[None, :]).reshape(-1)
    starts = offsets * BLOCK
    inside = (token_place[:, None] >= starts[None, :]) & (
        token_place[:, None] < (starts + lengths)[None, :]
    )
    live_rows = jnp.any(inside, axis=1).astype(jnp.float32)
    seq_depth = jnp.sum(jnp.where(inside, token_place[:, None] - starts[None, :], 0), axis=1)
    return (live_rows, seq_depth)


def shards(
    tokens,
    cotangent,
    lengths,
    offsets,
    deal,
    norm_gain1,
    w_branch,
    w_input,
    conv_kernel,
    conv_bias,
    gate_rec,
    bias_rec,
    gate_in,
    bias_in,
    decay_param,
    w_out,
    norm_gain2,
    w_gate,
    w_up,
    w_down,
):
    row_count = tokens.shape[0]
    blocks_here = row_count // BLOCK
    row_blocks = blocks_here * lax.axis_size("fsdp")
    device = lax.axis_index(("seq", "fsdp"))
    row_first = lax.axis_index("seq") * row_blocks
    own_blocks = lax.dynamic_slice_in_dim(deal, device * blocks_here, blocks_here)
    row_logical = lax.dynamic_slice_in_dim(deal, row_first, row_blocks) - row_first
    own_local = own_blocks - row_first
    live_rows, seq_depth = token_places(own_blocks, lengths, offsets)
    rank_index = jnp.arange(row_blocks, dtype=jnp.int32)
    order_row = (row_logical[None, :] == rank_index[:, None]).astype(jnp.float32)
    before_pick = (row_logical[None, :] == own_local[:, None] - 1).astype(jnp.float32)
    after_pick = (row_logical[None, :] == own_local[:, None] + 1).astype(jnp.float32)
    own_pick = (rank_index[None, :] == own_local[:, None]).astype(jnp.float32)
    at_first = (own_local == 0).astype(jnp.float32)[:, None, None]
    at_last = (own_local == row_blocks - 1).astype(jnp.float32)[:, None, None]
    mix_fwd = (
        lax.all_gather(as_low(norm_gain1), ("seq", "fsdp"), axis=0, tiled=True),
        lax.all_gather(as_low(w_branch), ("seq", "fsdp"), axis=0, tiled=True),
        lax.all_gather(as_low(w_input), ("seq", "fsdp"), axis=0, tiled=True),
        lax.all_gather(as_low(conv_kernel), ("seq", "fsdp"), axis=1, tiled=True),
        lax.all_gather(as_low(conv_bias), ("seq", "fsdp"), axis=0, tiled=True),
        lax.all_gather(as_low(gate_rec), ("seq", "fsdp"), axis=0, tiled=True),
        lax.all_gather(as_low(bias_rec), ("seq", "fsdp"), axis=0, tiled=True),
        lax.all_gather(as_low(gate_in), ("seq", "fsdp"), axis=0, tiled=True),
        lax.all_gather(as_low(bias_in), ("seq", "fsdp"), axis=0, tiled=True),
        lax.all_gather(as_low(decay_param), ("seq", "fsdp"), axis=0, tiled=True),
        lax.all_gather(as_low(w_out), ("seq", "fsdp"), axis=0, tiled=True),
        lax.all_gather(as_low(norm_gain2), ("seq", "fsdp"), axis=0, tiled=True),
    )
    (
        gain_one,
        branch_w,
        input_w,
        kernel_w,
        kernel_b,
        rec_w,
        rec_b,
        in_w,
        in_b,
        decay_w,
        out_w,
        gain_two,
    ) = mix_fwd
    resid_in = tokens.astype(jnp.float32)
    gain_one_value = gain_one.astype(jnp.float32)
    normed_one = rms_norm(resid_in, gain_one_value).astype(jnp.bfloat16)
    branch_pre = jnp.dot(normed_one, branch_w, preferred_element_type=jnp.float32)
    u_value = jnp.dot(normed_one, input_w, preferred_element_type=jnp.float32)
    state_width = u_value.shape[1]
    u_blocks = u_value.reshape(blocks_here, BLOCK, state_width)
    flag_one = jnp.ones((1, 1), jnp.float32)
    flag_zero = jnp.zeros((1, 1), jnp.float32)
    edge_zero = jnp.zeros((3, state_width), jnp.float32)
    row_tails = row_pieces(u_blocks[:, BLOCK - 3 :, :])
    last_tail = select_rows(order_row[row_blocks - 1 :], row_tails)[0]
    prev_flag, prev_tail = forward_chain((flag_one, last_tail), newest, (flag_zero, edge_zero))
    pred_tail = select_rows(before_pick, row_tails) + at_first * prev_tail[None]
    extended = jnp.concatenate([pred_tail, u_blocks], axis=1)
    depth_blocks = seq_depth.reshape(blocks_here, BLOCK, 1)
    tap_valid = [(depth_blocks >= tap_index).astype(jnp.float32) for tap_index in range(4)]
    kernel_fwd = kernel_w.astype(jnp.float32)
    conv_pre = jnp.zeros((blocks_here, BLOCK, state_width), jnp.float32) + kernel_b.astype(
        jnp.float32
    )
    for tap_index in range(4):
        conv_pre = (
            conv_pre
            + kernel_fwd[tap_index]
            * extended[:, 3 - tap_index : 3 - tap_index + BLOCK, :]
            * tap_valid[tap_index]
        )
    conv_low = conv_pre.reshape(row_count, state_width).astype(jnp.bfloat16)
    gate_width = rec_w.shape[1]
    groups = state_width // gate_width
    conv_heads = conv_low.reshape(row_count, groups, gate_width)
    pre_rec = jnp.einsum(
        "thb,hbc->thc",
        conv_heads,
        rec_w.reshape(groups, gate_width, gate_width),
        preferred_element_type=jnp.float32,
    ).reshape(row_count, state_width) + rec_b.astype(jnp.float32)
    pre_in = jnp.einsum(
        "thb,hbc->thc",
        conv_heads,
        in_w.reshape(groups, gate_width, gate_width),
        preferred_element_type=jnp.float32,
    ).reshape(row_count, state_width) + in_b.astype(jnp.float32)
    reset_mask = (seq_depth > 0).astype(jnp.float32)[:, None]
    (keep_rate, drive_in), lru_back = jax.vjp(
        lru_terms,
        pre_rec,
        pre_in,
        conv_low.astype(jnp.float32),
        decay_w.astype(jnp.float32),
        reset_mask,
    )
    keep_blocks = keep_rate.reshape(blocks_here, BLOCK, state_width)
    drive_blocks = drive_in.reshape(blocks_here, BLOCK, state_width)
    cum_keep, local_state = lax.associative_scan(chain_join, (keep_blocks, drive_blocks), axis=1)
    row_summary = row_pieces(jnp.stack([cum_keep[:, BLOCK - 1], local_state[:, BLOCK - 1]], axis=1))
    keep_sorted = select_rows(order_row, row_summary[:, 0])
    state_sorted = select_rows(order_row, row_summary[:, 1])
    incl_keep, incl_state = lax.associative_scan(chain_join, (keep_sorted, state_sorted), axis=0)
    ones_row = jnp.ones((1, state_width), jnp.float32)
    zeros_row = jnp.zeros((1, state_width), jnp.float32)
    excl_keep = jnp.concatenate([ones_row, incl_keep[:-1]], axis=0)
    excl_state = jnp.concatenate([zeros_row, incl_state[:-1]], axis=0)
    ones_vec = jnp.ones((state_width,), jnp.float32)
    zeros_vec = jnp.zeros((state_width,), jnp.float32)
    enter_keep, enter_row = forward_chain(
        (incl_keep[row_blocks - 1], incl_state[row_blocks - 1]), chain_join, (ones_vec, zeros_vec)
    )
    enter_sorted = excl_keep * enter_row[None, :] + excl_state
    enter_own = select_rows(own_pick, enter_sorted)
    state_blocks = local_state + cum_keep * enter_own[:, None, :]
    hidden_state = state_blocks.reshape(row_count, state_width)
    branch_act = jax.nn.gelu(branch_pre)
    gated_state = (hidden_state * branch_act).astype(jnp.bfloat16)
    resid_mid = resid_in + jnp.dot(gated_state, out_w, preferred_element_type=jnp.float32)
    gain_two_value = gain_two.astype(jnp.float32)
    normed_two = rms_norm(resid_mid, gain_two_value).astype(jnp.bfloat16)
    live_col = live_rows[:, None]
    grad_top = live_col * cotangent.astype(jnp.float32)
    grad_top_low = grad_top.astype(jnp.bfloat16)
    gate_w, up_w, down_w = (
        lax.all_gather(as_low(w_gate), ("seq", "fsdp"), axis=0, tiled=True),
        lax.all_gather(as_low(w_up), ("seq", "fsdp"), axis=0, tiled=True),
        lax.all_gather(as_low(w_down), ("seq", "fsdp"), axis=0, tiled=True),
    )
    gate_pre = jnp.dot(normed_two, gate_w, preferred_element_type=jnp.float32)
    up_pre = jnp.dot(normed_two, up_w, preferred_element_type=jnp.float32)
    hidden = gated_unit(gate_pre, up_pre).astype(jnp.bfloat16)
    mlp_out = jnp.dot(hidden, down_w, preferred_element_type=jnp.float32)
    grad_down = transposed_left(hidden, grad_top_low)
    grad_hidden = transposed_right(grad_top_low, down_w)
    unit_value, unit_back = jax.vjp(gated_unit, gate_pre, up_pre)
    grad_gate_full, grad_up_full = unit_back(grad_hidden)
    grad_gate_low = grad_gate_full.astype(jnp.bfloat16)
    grad_up_low = grad_up_full.astype(jnp.bfloat16)
    grad_gate = transposed_left(normed_two, grad_gate_low)
    grad_up = transposed_left(normed_two, grad_up_low)
    grad_normed_two = transposed_right(grad_gate_low, gate_w) + transposed_right(grad_up_low, up_w)
    grad_gate_home, grad_up_home, grad_down_home = (
        lax.psum_scatter(grad_gate, ("seq", "fsdp"), scatter_dimension=0, tiled=True),
        lax.psum_scatter(grad_up, ("seq", "fsdp"), scatter_dimension=0, tiled=True),
        lax.psum_scatter(grad_down, ("seq", "fsdp"), scatter_dimension=0, tiled=True),
    )
    mixed = (live_col * (resid_mid + mlp_out)).astype(jnp.bfloat16)
    norm_two_value, norm_two_back = jax.vjp(rms_norm, resid_mid, gain_two_value)
    grad_mid_norm, grad_gain_two = norm_two_back(grad_normed_two)
    grad_mid = grad_top + grad_mid_norm
    grad_out_low = grad_mid.astype(jnp.bfloat16)
    grad_out = transposed_left(gated_state, grad_out_low)
    grad_gated = transposed_right(grad_out_low, out_w)
    grad_state_direct = grad_gated * branch_act
    gelu_value, gelu_back = jax.vjp(jax.nn.gelu, branch_pre)
    grad_branch_low = gelu_back(grad_gated * hidden_state)[0].astype(jnp.bfloat16)
    grad_branch = transposed_left(normed_one, grad_branch_low)
    direct_blocks = grad_state_direct.reshape(blocks_here, BLOCK, state_width)
    next_keep = jnp.concatenate(
        [keep_blocks[:, 1:], jnp.ones((blocks_here, 1, state_width), jnp.float32)], axis=1
    )
    flip_keep, flip_grad = lax.associative_scan(
        chain_join, (next_keep[:, ::-1], direct_blocks[:, ::-1]), axis=1
    )
    tail_keep = flip_keep[:, ::-1]
    local_grad = flip_grad[:, ::-1]
    send_back = keep_blocks[:, 0] * local_grad[:, 0]
    row_back = row_pieces(send_back[:, None, :])[:, 0]
    back_sorted = select_rows(order_row, row_back)
    rev_keep, rev_grad = lax.associative_scan(
        chain_join, (keep_sorted[::-1], back_sorted[::-1]), axis=0
    )
    suffix_keep = jnp.concatenate([rev_keep[::-1][1:], ones_row], axis=0)
    suffix_grad = jnp.concatenate([rev_grad[::-1][1:], zeros_row], axis=0)
    leave_keep, leave_row = backward_chain(
        (rev_keep[row_blocks - 1], rev_grad[row_blocks - 1]), chain_join, (ones_vec, zeros_vec)
    )
    carry_sorted = suffix_keep * leave_row[None, :] + suffix_grad
    carry_own = select_rows(own_pick, carry_sorted)
    grad_blocks = local_grad + tail_keep * carry_own[:, None, :]
    state_before = jnp.concatenate([enter_own[:, None, :], state_blocks[:, :-1]], axis=1)
    grad_keep = (grad_blocks * state_before).reshape(row_count, state_width)
    grad_drive = grad_blocks.reshape(row_count, state_width)
    grad_rec_full, grad_in_full, grad_conv_direct, grad_decay, grad_reset = lru_back(
        (grad_keep, grad_drive)
    )
    grad_rec_low = grad_rec_full.astype(jnp.bfloat16)
    grad_in_low = grad_in_full.astype(jnp.bfloat16)
    rec_heads_low = grad_rec_low.reshape(row_count, groups, gate_width)
    in_heads_low = grad_in_low.reshape(row_count, groups, gate_width)
    grad_rec_w = jnp.einsum(
        "thb,thc->hbc", conv_heads, rec_heads_low, preferred_element_type=jnp.float32
    ).reshape(state_width, gate_width)
    grad_in_w = jnp.einsum(
        "thb,thc->hbc", conv_heads, in_heads_low, preferred_element_type=jnp.float32
    ).reshape(state_width, gate_width)
    grad_rec_bias = jnp.sum(grad_rec_low.astype(jnp.float32), axis=0)
    grad_in_bias = jnp.sum(grad_in_low.astype(jnp.float32), axis=0)
    grad_conv = grad_conv_direct + jnp.einsum(
        "thc,hbc->thb",
        rec_heads_low,
        rec_w.reshape(groups, gate_width, gate_width),
        preferred_element_type=jnp.float32,
    ).reshape(row_count, state_width)
    grad_conv = grad_conv + jnp.einsum(
        "thc,hbc->thb",
        in_heads_low,
        in_w.reshape(groups, gate_width, gate_width),
        preferred_element_type=jnp.float32,
    ).reshape(row_count, state_width)
    conv_grad_blocks = grad_conv.reshape(blocks_here, BLOCK, state_width)
    grad_ext = jnp.zeros((blocks_here, BLOCK + 3, state_width), jnp.float32)
    kernel_rows = []
    for tap_index in range(4):
        weighted = conv_grad_blocks * tap_valid[tap_index]
        kernel_rows.append(
            jnp.sum(weighted * extended[:, 3 - tap_index : 3 - tap_index + BLOCK, :], axis=(0, 1))
        )
        grad_ext = grad_ext + jnp.pad(
            weighted * kernel_fwd[tap_index], ((0, 0), (3 - tap_index, tap_index), (0, 0))
        )
    grad_kernel = jnp.stack(kernel_rows, axis=0)
    grad_kernel_bias = jnp.sum(grad_conv, axis=0)
    row_heads = row_pieces(grad_ext[:, :3, :])
    first_head = select_rows(order_row[:1], row_heads)[0]
    next_flag, next_head = backward_chain((flag_one, first_head), newest, (flag_zero, edge_zero))
    tail_grad = select_rows(after_pick, row_heads) + at_last * next_head[None]
    grad_u_blocks = grad_ext[:, 3:, :] + jnp.pad(tail_grad, ((0, 0), (BLOCK - 3, 0), (0, 0)))
    grad_u_low = grad_u_blocks.reshape(row_count, state_width).astype(jnp.bfloat16)
    grad_input = transposed_left(normed_one, grad_u_low)
    grad_normed_one = transposed_right(grad_branch_low, branch_w) + transposed_right(
        grad_u_low, input_w
    )
    norm_one_value, norm_one_back = jax.vjp(rms_norm, resid_in, gain_one_value)
    grad_in_norm, grad_gain_one = norm_one_back(grad_normed_one)
    tokens_grad = (grad_mid + grad_in_norm).astype(jnp.bfloat16)
    mix_sums = (
        lax.psum_scatter(grad_gain_one, ("seq", "fsdp"), scatter_dimension=0, tiled=True),
        lax.psum_scatter(grad_branch, ("seq", "fsdp"), scatter_dimension=0, tiled=True),
        lax.psum_scatter(grad_input, ("seq", "fsdp"), scatter_dimension=0, tiled=True),
        lax.psum_scatter(grad_kernel, ("seq", "fsdp"), scatter_dimension=1, tiled=True),
        lax.psum_scatter(grad_kernel_bias, ("seq", "fsdp"), scatter_dimension=0, tiled=True),
        lax.psum_scatter(grad_rec_w, ("seq", "fsdp"), scatter_dimension=0, tiled=True),
        lax.psum_scatter(grad_rec_bias, ("seq", "fsdp"), scatter_dimension=0, tiled=True),
        lax.psum_scatter(grad_in_w, ("seq", "fsdp"), scatter_dimension=0, tiled=True),
        lax.psum_scatter(grad_in_bias, ("seq", "fsdp"), scatter_dimension=0, tiled=True),
        lax.psum_scatter(grad_decay, ("seq", "fsdp"), scatter_dimension=0, tiled=True),
        lax.psum_scatter(grad_out, ("seq", "fsdp"), scatter_dimension=0, tiled=True),
        lax.psum_scatter(grad_gain_two, ("seq", "fsdp"), scatter_dimension=0, tiled=True),
    )
    return (
        mixed,
        tokens_grad,
        mix_sums[0],
        mix_sums[1],
        mix_sums[2],
        mix_sums[3],
        mix_sums[4],
        mix_sums[5],
        mix_sums[6],
        mix_sums[7],
        mix_sums[8],
        mix_sums[9],
        mix_sums[10],
        mix_sums[11],
        grad_gate_home,
        grad_up_home,
        grad_down_home,
    )


def solution(mesh):
    return jax.shard_map(
        shards,
        mesh=mesh,
        in_specs=(
            P(("seq", "fsdp"), None),
            P(("seq", "fsdp"), None),
            P(),
            P(),
            P(),
            P(("seq", "fsdp")),
            P(("seq", "fsdp"), None),
            P(("seq", "fsdp"), None),
            P(None, ("seq", "fsdp")),
            P(("seq", "fsdp")),
            P(("seq", "fsdp"), None),
            P(("seq", "fsdp")),
            P(("seq", "fsdp"), None),
            P(("seq", "fsdp")),
            P(("seq", "fsdp")),
            P(("seq", "fsdp"), None),
            P(("seq", "fsdp")),
            P(("seq", "fsdp"), None),
            P(("seq", "fsdp"), None),
            P(("seq", "fsdp"), None),
        ),
        out_specs=(
            P(("seq", "fsdp"), None),
            P(("seq", "fsdp"), None),
            P(("seq", "fsdp")),
            P(("seq", "fsdp"), None),
            P(("seq", "fsdp"), None),
            P(None, ("seq", "fsdp")),
            P(("seq", "fsdp")),
            P(("seq", "fsdp"), None),
            P(("seq", "fsdp")),
            P(("seq", "fsdp"), None),
            P(("seq", "fsdp")),
            P(("seq", "fsdp")),
            P(("seq", "fsdp"), None),
            P(("seq", "fsdp")),
            P(("seq", "fsdp"), None),
            P(("seq", "fsdp"), None),
            P(("seq", "fsdp"), None),
        ),
        check_vma=False,
    )
```

profile of v0, /device:TPU:0, one launch (start us, length us, event | category | flops | bytes accessed | tf_op | source)
XLA Modules:
  0.0 4243.9 jit_solution(1516317738197780760)
XLA Ops:
  18.2 70.6 %all-gather.2 = bf16[32,80,4]{1,2,0:T(4,128)(2,1)S(1)} all-gather(bf16[1,80,4]{1,2,0:T(4,128)(2,1)S(1)} %convert_bitcast_fusion), channel_id=1, replica_groups=mesh['seq'=8,'fsdp'=4] {'seq','fsdp'}, dimensions={0}, use_global_device_ids=true | all-gather | bytes 21120 | tf_op jit(solution)/shard_map/all_gather | solution.py:143
  90.1 12.2 all-reduce.93
  103.9 37.8 all-reduce.105
  148.4 97.4 %all_gather.86 = bf16[2560,160]{1,0:T(8,128)(2,1)} all-gather(bf16[80,160]{1,0:T(8,128)(2,1)S(1)} %convert_element_type.260), channel_id=1, replica_groups=mesh['seq'=8,'fsdp'=4] {'seq','fsdp'}, dimensions={0}, use_global_device_ids=true | all-gather | bytes 844800 | tf_op jit(solution)/shard_map/all_gather | solution.py:145
  245.8 98.0 %all_gather.89 = bf16[2560,160]{1,0:T(8,128)(2,1)} all-gather(bf16[80,160]{1,0:T(8,128)(2,1)S(1)} %convert_element_type.265), channel_id=1, replica_groups=mesh['seq'=8,'fsdp'=4] {'seq','fsdp'}, dimensions={0}, use_global_device_ids=true | all-gather | bytes 844800 | tf_op jit(solution)/shard_map/all_gather | solution.py:147
  349.9 16.7 all_gather.83
  375.2 9.1 while.56
  619.2 13.5 all_gather.91
  655.6 9.8 all-gather.5
  674.8 11.1 slice.800
  713.5 9.8 fusion.31
  729.8 15.2 fusion.174
  745.0 14.9 fusion.175
  759.9 17.1 all-gather.26.cloned.1.call-done
  777.1 21.8 multiply_convert_fusion
  798.8 13.5 fusion.176
  812.3 15.2 multiply_reduce_fusion.5
  830.7 9.5 fusion.47
  846.7 10.8 slice.802
  857.4 10.7 slice.804
  957.2 10.8 slice.852
  980.3 13.2 all_gather.101
  1002.2 9.4 all-gather.7
  1033.1 13.1 rev.25
  1046.3 21.0 rev.24
  1067.6 8.8 convert_reduce_fusion.1
  1093.5 9.3 fusion.27
  1114.5 8.6 multiply_reduce_fusion
  1134.8 11.3 multiply_reduce_fusion.3
  1153.8 14.8 all_gather.103
  1169.0 9.8 all-gather.8
  1179.7 14.4 while.59
  1200.6 8.9 fusion.145
  1211.2 9.9 fusion.50
  1221.2 10.1 fusion.147
  1231.4 21.2 fusion.180
  1252.7 21.2 fusion.181
  1274.5 21.9 fusion.54
  1312.1 39.4 all-reduce.104
  1358.4 13.0 fusion.34
  1372.8 49.8 %reduce-scatter.16.cloned.1.call-done = f32[80,160]{1,0:T(8,128)} async-done(((f32[2560,160]{1,0:T(8,128)}), f32[80,160]{1,0:T(8,128)}) %reduce-scatter.16.cloned.1.call-update) | async-done | bytes 51216 | tf_op jit(solution)/shard_map/reduce_scatter | solution.py:367
  1422.6 141.8 %reduce-scatter.18.cloned.1.call-done = f32[80,160]{1,0:T(8,128)} async-done(((f32[2560,160]{1,0:T(8,128)}), f32[80,160]{1,0:T(8,128)}) %reduce-scatter.18.cloned.1.call-update) | async-done | bytes 51216 | tf_op jit(solution)/shard_map/reduce_scatter | solution.py:369
  1564.4 452.0 %reduce-scatter.14.cloned.1.call-done = f32[64,2560]{1,0:T(8,128)} async-done(((f32[2048,2560]{1,0:T(8,128)}), f32[64,2560]{1,0:T(8,128)}) %reduce-scatter.14.cloned.1.call-update) | async-done | bytes 655376 | tf_op jit(solution)/shard_map/reduce_scatter | solution.py:364
  2016.5 452.4 %reduce-scatter.20.cloned.1.call-done = f32[80,2048]{1,0:T(8,128)} async-done(((f32[2560,2048]{1,0:T(8,128)}), f32[80,2048]{1,0:T(8,128)}) %reduce-scatter.20.cloned.1.call-update) | async-done | bytes 655376 | tf_op jit(solution)/shard_map/reduce_scatter | solution.py:372
  2468.9 452.3 %reduce-scatter.12.cloned.1.call-done = f32[64,2560]{1,0:T(8,128)} async-done(((f32[2048,2560]{1,0:T(8,128)}), f32[64,2560]{1,0:T(8,128)}) %reduce-scatter.12.cloned.1.call-update) | async-done | bytes 655376 | tf_op jit(solution)/shard_map/reduce_scatter | solution.py:363
  2921.2 438.6 %reduce-scatter.22.cloned.1.call-done = f32[64,6144]{1,0:T(8,128)} async-done(((f32[2048,6144]{1,0:T(8,128)}), f32[64,6144]{1,0:T(8,128)}) %reduce-scatter.22.cloned.1.call-update) | async-done | bytes 1572880 | tf_op jit(solution)/shard_map/reduce_scatter | solution.py:267
  3359.8 438.7 %reduce-scatter.24.cloned.1.call-done = f32[64,6144]{1,0:T(8,128)} async-done(((f32[2048,6144]{1,0:T(8,128)}), f32[64,6144]{1,0:T(8,128)}) %reduce-scatter.24.cloned.1.call-update) | async-done | bytes 1572880 | tf_op jit(solution)/shard_map/reduce_scatter | solution.py:268
  3798.5 438.6 %reduce-scatter.26.cloned.1.call-done = f32[192,2048]{1,0:T(8,128)} async-done(((f32[6144,2048]{1,0:T(8,128)}), f32[192,2048]{1,0:T(8,128)}) %reduce-scatter.26.cloned.1.call-update) | async-done | bytes 1572880 | tf_op jit(solution)/shard_map/reduce_scatter | solution.py:269
  (847 shorter events, 581.8 us)
Async XLA Ops:
  7.2 336.7 %all-gather.16.cloned.1.call-start = ((), (), s32[]{:S(2)}) async-start(), calls=%async_computation.9 | async-start | bytes 10813440 | tf_op jit(solution)/shard_map/all_gather | solution.py:142
  9.2 704.2 %all-gather.18.cloned.1.call-start = ((), (), s32[]{:S(2)}) async-start(), calls=%async_computation.10 | async-start | bytes 10813440 | tf_op jit(solution)/shard_map/all_gather | solution.py:141
  11.2 712.1 %all-gather.20.cloned.1.call-start = ((), (), s32[]{:S(2)}) async-start(), calls=%async_computation.11 | async-start | bytes 10813440 | tf_op jit(solution)/shard_map/all_gather | solution.py:150
  13.2 716.6 %all-gather.22.cloned.1.call-start = ((), (), s32[]{:S(2)}) async-start(), calls=%async_computation.12 | async-start | bytes 25952256 | tf_op jit(solution)/shard_map/all_gather | solution.py:249
  14.2 74.6 %copy-start.154 = (u32[32]{0:T(128)S(1)}, u32[32]{0:T(128)}, u32[]{:S(2)}) copy-start(u32[32]{0:T(128)} %constant.387) | copy-start | bytes 388
  14.2 730.8 %all-gather.24.cloned.1.call-start = ((), (), s32[]{:S(2)}) async-start(), calls=%async_computation.13 | async-start | bytes 25952256 | tf_op jit(solution)/shard_map/all_gather | solution.py:250
  15.3 87.1 %copy-start.147 = (f32[80]{0:T(128)S(1)}, f32[80]{0:T(128)}, u32[]{:S(2)}) copy-start(f32[80]{0:T(128)} %param.37) | copy-start | bytes 964
  15.3 87.1 %copy-start.148 = (f32[80]{0:T(128)S(1)}, f32[80]{0:T(128)}, u32[]{:S(2)}) copy-start(f32[80]{0:T(128)} %param.39) | copy-start | bytes 964
  15.3 87.1 %copy-start.149 = (f32[80]{0:T(128)S(1)}, f32[80]{0:T(128)}, u32[]{:S(2)}) copy-start(f32[80]{0:T(128)} %param.42) | copy-start | bytes 964
  15.3 87.2 %copy-start.150 = (f32[80]{0:T(128)S(1)}, f32[80]{0:T(128)}, u32[]{:S(2)}) copy-start(f32[80]{0:T(128)} %param.41) | copy-start | bytes 964
  15.3 87.2 %copy-start.151 = (f32[64]{0:T(128)S(1)}, f32[64]{0:T(128)}, u32[]{:S(2)}) copy-start(f32[64]{0:T(128)} %param.33) | copy-start | bytes 772
  15.3 87.2 %copy-start.152 = (f32[64]{0:T(128)S(1)}, f32[64]{0:T(128)}, u32[]{:S(2)}) copy-start(f32[64]{0:T(128)} %param.44) | copy-start | bytes 772
  15.3 127.9 %copy-start.91 = (f32[80,160]{1,0:T(8,128)S(1)}, f32[80,160]{1,0:T(8,128)}, u32[]{:S(2)}) copy-start(f32[80,160]{1,0:T(8,128)} %param.38) | copy-start | bytes 153604
  15.3 127.9 %copy-start.92 = (f32[80,160]{1,0:T(8,128)S(1)}, f32[80,160]{1,0:T(8,128)}, u32[]{:S(2)}) copy-start(f32[80,160]{1,0:T(8,128)} %param.40) | copy-start | bytes 153604
  15.3 127.9 %copy-start.143 = (s32[64]{0:T(128)S(1)}, s32[64]{0:T(128)}, u32[]{:S(2)}) copy-start(s32[64]{0:T(128)} %param.32) | copy-start | bytes 772
  15.3 128.0 %copy-start.145 = (s32[4]{0:T(128)S(1)}, s32[4]{0:T(128)}, u32[]{:S(2)}) copy-start(s32[4]{0:T(128)} %param.30) | copy-start | bytes 52
  15.3 128.0 %copy-start.146 = (s32[4]{0:T(128)S(1)}, s32[4]{0:T(128)}, u32[]{:S(2)}) copy-start(s32[4]{0:T(128)} %param.31) | copy-start | bytes 52
  15.4 131.6 %copy-start.12 = (bf16[256,2048]{1,0:T(8,128)(2,1)S(1)}, bf16[256,2048]{1,0:T(8,128)(2,1)}, u32[]{:S(2)}) copy-start(bf16[256,2048]{1,0:T(8,128)(2,1)} %param.28) | copy-start | bytes 3145732
  15.4 761.7 %all-gather.26.cloned.1.call-start = ((), (), s32[]{:S(2)}) async-start(), calls=%async_computation.14 | async-start | bytes 25952256 | tf_op jit(solution)/shard_map/all_gather | solution.py:251
  18.1 1353.3 %reduce-scatter.28.cloned.1.call-start = ((), (), s32[]{:S(2)}) async-start(), calls=%async_computation.23 | async-start | bytes 1351680
  141.6 278.3 %copy-start.65 = (f32[2560]{0:T(1024)}, f32[2560]{0:T(1024)S(1)}, u32[]{:S(2)}) copy-start(f32[2560]{0:T(1024)S(1)} %convert_element_type.267) | copy-start | bytes 30724
  142.3 277.6 %copy-start.67 = (f32[2560]{0:T(1024)}, f32[2560]{0:T(1024)S(1)}, u32[]{:S(2)}) copy-start(f32[2560]{0:T(1024)S(1)} %convert_element_type.262) | copy-start | bytes 30724
  143.0 570.4 %copy-start.56 = (f32[2048]{0:T(1024)}, f32[2048]{0:T(1024)S(1)}, u32[]{:S(2)}) copy-start(f32[2048]{0:T(1024)S(1)} %convert_element_type.246) | copy-start | bytes 24580
  144.1 205.7 %copy-start.78 = (f32[2560]{0:T(1024)}, f32[2560]{0:T(1024)S(1)}, u32[]{:S(2)}) copy-start(f32[2560]{0:T(1024)S(1)} %get-tuple-element.654) | copy-start | bytes 30724
  144.1 275.8 %copy-start.63 = (f32[2560]{0:T(1024)}, f32[2560]{0:T(1024)S(1)}, u32[]{:S(2)}) copy-start(f32[2560]{0:T(1024)S(1)} %get-tuple-element.655) | copy-start | bytes 30724
  146.2 228.7 %copy-start.115 = (s32[8]{0:T(128)}, s32[8]{0:T(128)S(1)}, u32[]{:S(2)}) copy-start(s32[8]{0:T(128)S(1)} %dynamic-slice_subtract_fusion) | copy-start | bytes 100
  146.8 203.1 %copy-start.133 = (s32[2]{0:T(128)}, s32[2]{0:T(128)S(1)}, u32[]{:S(2)}) copy-start(s32[2]{0:T(128)S(1)} %get-tuple-element.542) | copy-start | bytes 28
  147.0 237.5 %copy-start.80 = (f32[2560]{0:T(1024)}, f32[2560]{0:T(1024)S(1)}, u32[]{:S(2)}) copy-start(f32[2560]{0:T(1024)S(1)} %get-tuple-element.479) | copy-start | bytes 30724
  147.0 237.5 %copy-start.82 = (f32[2560]{0:T(1024)}, f32[2560]{0:T(1024)S(1)}, u32[]{:S(2)}) copy-start(f32[2560]{0:T(1024)S(1)} %get-tuple-element.480) | copy-start | bytes 30724
  147.0 237.5 %copy-start.84 = (f32[2560]{0:T(1024)}, f32[2560]{0:T(1024)S(1)}, u32[]{:S(2)}) copy-start(f32[2560]{0:T(1024)S(1)} %get-tuple-element.481) | copy-start | bytes 30724
  147.0 237.5 %copy-start.86 = (f32[2560]{0:T(1024)}, f32[2560]{0:T(1024)S(1)}, u32[]{:S(2)}) copy-start(f32[2560]{0:T(1024)S(1)} %get-tuple-element.482) | copy-start | bytes 30724
  147.3 202.6 %copy-start.130 = (f32[256]{0:T(256)}, f32[256]{0:T(256)S(1)}, u32[]{:S(2)}) copy-start(f32[256]{0:T(256)S(1)} %fusion.42) | copy-start | bytes 3076
  147.8 218.8 %copy-start.138 = (pred[8,8]{1,0:T(8,128)(4,1)}, pred[8,8]{1,0:T(8,128)(4,1)S(1)}, u32[]{:S(2)}) copy-start(pred[8,8]{1,0:T(8,128)(4,1)S(1)} %iota_compare_fusion) | copy-start | bytes 196
  147.8 565.6 %copy-start.104 = (f32[256]{0:T(256)}, f32[256]{0:T(256)S(1)}, u32[]{:S(2)}) copy-start(f32[256]{0:T(256)S(1)} %fusion.130) | copy-start | bytes 3076
  148.4 236.0 %copy-start.120 = (f32[2,128]{1,0:T(2,128)}, f32[2,128]{1,0:T(2,128)S(1)}, u32[]{:S(2)}) copy-start(f32[2,128]{1,0:T(2,128)S(1)} %get-tuple-element.658) | copy-start | bytes 3076
  148.4 236.1 %copy-start.122 = (f32[2,128]{1,0:T(2,128)}, f32[2,128]{1,0:T(2,128)S(1)}, u32[]{:S(2)}) copy-start(f32[2,128]{1,0:T(2,128)S(1)} %get-tuple-element.659) | copy-start | bytes 3076
  148.4 236.1 %copy-start.124 = (f32[2,128]{1,0:T(2,128)}, f32[2,128]{1,0:T(2,128)S(1)}, u32[]{:S(2)}) copy-start(f32[2,128]{1,0:T(2,128)S(1)} %get-tuple-element.660) | copy-start | bytes 3076
  148.4 236.1 %copy-start.126 = (f32[2,128]{1,0:T(2,128)}, f32[2,128]{1,0:T(2,128)S(1)}, u32[]{:S(2)}) copy-start(f32[2,128]{1,0:T(2,128)S(1)} %get-tuple-element.661) | copy-start | bytes 3076
  148.4 271.5 %copy-start.128 = (f32[2,128]{1,0:T(2,128)}, f32[2,128]{1,0:T(2,128)S(1)}, u32[]{:S(2)}) copy-start(f32[2,128]{1,0:T(2,128)S(1)} %get-tuple-element.657) | copy-start | bytes 3076
  729.5 98.0 %copy-start.27 = (f32[256,2048]{1,0:T(8,128)}, f32[256,2048]{1,0:T(8,128)S(1)}, u32[]{:S(2)}) copy-start(f32[256,2048]{1,0:T(8,128)S(1)} %get-tuple-element.669) | copy-start | bytes 6291460
  1147.8 274.8 %reduce-scatter.16.cloned.1.call-start = ((), (), s32[]{:S(2)}) async-start(), calls=%async_computation.17 | async-start | bytes 2703360 | tf_op jit(solution)/shard_map/reduce_scatter | solution.py:367
  1179.6 384.8 %reduce-scatter.18.cloned.1.call-start = ((), (), s32[]{:S(2)}) async-start(), calls=%async_computation.18 | async-start | bytes 2703360 | tf_op jit(solution)/shard_map/reduce_scatter | solution.py:369
  1194.2 822.3 %reduce-scatter.14.cloned.1.call-start = ((), (), s32[]{:S(2)}) async-start(), calls=%async_computation.16 | async-start | bytes 21626880 | tf_op jit(solution)/shard_map/reduce_scatter | solution.py:364
  1209.6 1259.3 %reduce-scatter.20.cloned.1.call-start = ((), (), s32[]{:S(2)}) async-start(), calls=%async_computation.19 | async-start | bytes 21626880 | tf_op jit(solution)/shard_map/reduce_scatter | solution.py:372
  1221.1 1700.1 %reduce-scatter.12.cloned.1.call-start = ((), (), s32[]{:S(2)}) async-start(), calls=%async_computation.15 | async-start | bytes 21626880 | tf_op jit(solution)/shard_map/reduce_scatter | solution.py:363
  1231.3 2128.5 %reduce-scatter.22.cloned.1.call-start = ((), (), s32[]{:S(2)}) async-start(), calls=%async_computation.20 | async-start | bytes 51904512 | tf_op jit(solution)/shard_map/reduce_scatter | solution.py:267
  1252.6 2545.9 %reduce-scatter.24.cloned.1.call-start = ((), (), s32[]{:S(2)}) async-start(), calls=%async_computation.21 | async-start | bytes 51904512 | tf_op jit(solution)/shard_map/reduce_scatter | solution.py:268
  1273.9 2963.3 %reduce-scatter.26.cloned.1.call-start = ((), (), s32[]{:S(2)}) async-start(), calls=%async_computation.22 | async-start | bytes 51904512 | tf_op jit(solution)/shard_map/reduce_scatter | solution.py:269
  (123 other events, 1103.3 us)
Sparse Core Ops, SparseCore 0:
  11.4 89.5 all-gather.15
  103.9 94.2 all-gather.17
  201.1 98.0 all-gather.19
  302.5 162.5 all-gather.21
  467.9 152.8 all-gather.23
  623.5 153.5 all-gather.25
  1148.0 134.3 reduce-scatter.27
  1285.3 137.2 reduce-scatter.15
  1425.6 138.8 reduce-scatter.17
  1567.3 449.1 reduce-scatter.13
  2019.5 449.4 reduce-scatter.19
  2471.8 449.4 reduce-scatter.11
  2929.4 430.4 reduce-scatter.21
  3367.8 430.6 reduce-scatter.23
  3806.5 430.6 reduce-scatter.25
where the time goes:
time: 4260 us; the launch traced here: 4240 us
  waiting for transfers between devices  2880 us (68%)
  blocking collectives  467 us (11%)
  local copies, waits for them, and re-layouts  433 us (10%)
  matrix products  255 us (6%)
  other arithmetic  189 us (4%)
    reduce_scatter x1, waiting for transfers between devices, shards(): lax.psum_scatter(grad_out, ('seq', 'fsdp'), scatter_dimension=0, tiled=True)  452 us
    reduce_scatter x1, waiting for transfers between devices, shards(): lax.psum_scatter(grad_branch, ('seq', 'fsdp'), scatter_dimension=0, tiled...  452 us
    reduce_scatter x1, waiting for transfers between devices, shards(): lax.psum_scatter(grad_input, ('seq', 'fsdp'), scatter_dimension=0, tiled=...  452 us
    reduce_scatter x1, waiting for transfers between devices, shards(): lax.psum_scatter(grad_up, ('seq', 'fsdp'), scatter_dimension=0, tiled=True)  439 us
    reduce_scatter x1, waiting for transfers between devices, shards(): lax.psum_scatter(grad_down, ('seq', 'fsdp'), scatter_dimension=0, tiled=T...  439 us
    reduce_scatter x1, waiting for transfers between devices, shards(): lax.psum_scatter(grad_gate, ('seq', 'fsdp'), scatter_dimension=0, tiled=T...  439 us
    reduce_scatter x1, waiting for transfers between devices, shards(): lax.psum_scatter(grad_in_w, ('seq', 'fsdp'), scatter_dimension=0, tiled=T...  142 us
    slice x49, local copies, waits for them, and re-layouts, shards(): lax.associative_scan(chain_join, (next_keep[:, ::-1], direct_blocks[:, ::...  123 us
  transfers between devices with their start and end apart: 15, of which 9 were waited for; matrix products, arithmetic and copies ran while one was open for 12% of the time, Pallas kernels for 0%

commit v1 on v0

v1 whole, which is shorter than its diff:
```python
import jax
import jax.numpy as jnp
from jax import lax
from jax.experimental import pallas as pl
from jax.experimental.pallas import tpu as pltpu
from jax.sharding import PartitionSpec as P

BLOCK = 128
LANES = 128
TAPS = 4
UNROLL = 8
NORM_EPSILON = 1e-06
GATE_SCALE = 8.0
VMEM_LIMIT = 48 * 1024 * 1024
GELU_C = 0.7978845608028654
GELU_A = 0.044715


def as_low(values):
    return values.astype(jnp.bfloat16)


def as_wide(values):
    return values.astype(jnp.float32)


def mm(left, right, out=jnp.float32):
    return jnp.dot(left, right, preferred_element_type=jnp.float32).astype(out)


def mm_tn(left, right, out=jnp.float32):
    return lax.dot_general(
        left, right, (((0,), (0,)), ((), ())), preferred_element_type=jnp.float32
    ).astype(out)


def mm_nt(left, right, out=jnp.float32):
    return lax.dot_general(
        left, right, (((1,), (1,)), ((), ())), preferred_element_type=jnp.float32
    ).astype(out)


def swap(values, axis, flip):
    count = lax.axis_size(axis)
    return lax.ppermute(values, axis, [(i, i ^ flip) for i in range(count)])


def gather_plane(own):
    count = lax.axis_size("seq")
    if count == 8:
        half = own.shape[0] // 2
        near, side = swap(own, "seq", 2), swap(own, "seq", 4)
        far = (swap(side[:half], "seq", 2), swap(near[half:], "seq", 4))
        even = [(own,), (near,), (side,), far]
    else:
        even = [(own,)] + [(swap(own, "seq", k),) for k in range(2, count, 2)]
    odd = [tuple(swap(part, "seq", 1) for part in slot) for slot in even]
    return even + odd


def scatter_plane(product, hold=lambda value: value):
    count = lax.axis_size("seq")
    other = swap(hold(as_low(product(True))), "seq", 1)
    pair = product(False) + as_wide(other)
    rows = pair.shape[0] // (count // 2)
    if count != 8:
        total = pair[:rows]
        for index, k in enumerate(range(2, count, 2), start=1):
            total = total + as_wide(swap(as_low(pair[index * rows : (index + 1) * rows]), "seq", k))
        return total
    half = rows // 2

    def part(slot, lower):
        start = slot * rows + (half if lower else 0)
        return pair[start : start + half]

    far_top = swap(as_low(part(3, False)), "seq", 2)
    far_low = swap(as_low(part(3, True)), "seq", 4)
    near_top = swap(as_low(part(1, False)), "seq", 2)
    side_low = swap(as_low(part(2, True)), "seq", 4)
    near_low = swap(as_low(part(1, True) + as_wide(far_low)), "seq", 2)
    side_top = swap(as_low(part(2, False) + as_wide(far_top)), "seq", 4)
    top = part(0, False) + as_wide(near_top) + as_wide(side_top)
    low = part(0, True) + as_wide(near_low) + as_wide(side_low)
    return jnp.concatenate([top, low], axis=0)


def spread_z(value):
    count = lax.axis_size("fsdp")
    return jnp.stack([value] + [swap(value, "fsdp", j) for j in range(1, count)], axis=0)


def gelu_parts(values):
    inner = GELU_C * (values + GELU_A * values * values * values)
    bend = jnp.tanh(inner)
    return (0.5 * values * (1.0 + bend), bend)


def gelu_slope(values, bend):
    return 0.5 * (1.0 + bend) + 0.5 * values * (1.0 - bend * bend) * GELU_C * (
        1.0 + 3.0 * GELU_A * values * values
    )


def expm1_small(values):
    series = values * (1.0 / 120.0) + 1.0 / 24.0
    for scale in (1.0 / 6.0, 0.5, 1.0):
        series = series * values + scale
    return series * values


def block_rows(index):
    return pl.ds(pl.multiple_of(index * BLOCK, BLOCK), BLOCK)


def lane_tiles(width):
    return [(low, min(LANES, width - low)) for low in range(0, width, LANES)]


def stack_step(refs, slots):
    step = pl.program_id(0)
    steps = pl.num_programs(0)
    rows, at = [], 0
    for parts in slots:
        if parts == 1:
            rows.append(refs[at][...])
        else:
            rows.append(jnp.where(step < steps // 2, refs[at][...], refs[at + 1][...]))
        at += parts
    return jnp.concatenate(rows, axis=0)


def slot_specs(pieces, steps):
    specs = []
    for slot in pieces:
        chunk = sum(part.shape[0] for part in slot) // steps
        model = slot[0].shape[1]
        if len(slot) == 1:
            specs.append(pl.BlockSpec((chunk, model), lambda i: (i, 0)))
        else:
            last = steps // 2 - 1
            specs.append(pl.BlockSpec((chunk, model), lambda i, last=last: (jnp.minimum(i, last), 0)))
            specs.append(pl.BlockSpec((chunk, model), lambda i, last=last: (jnp.maximum(i - last - 1, 0), 0)))
    return specs


def stack(pieces, name, gain=None, weights=(), steps=8):
    slots = tuple(len(slot) for slot in pieces)
    count = len(pieces)
    flat = [part for slot in pieces for part in slot]
    rows = sum(part.shape[0] for part in pieces[0])
    model = flat[0].shape[1]
    chunk = rows // steps
    extra = ([gain] if gain is not None else []) + list(weights)

    def kernel(*refs):
        pieces_in, refs = refs[: len(flat)], refs[len(flat) :]
        values = stack_step(pieces_in, slots)
        if gain is not None:
            gain_ref, refs = refs[0], refs[1:]
            wide = values.astype(jnp.float32)
            scale = lax.rsqrt(jnp.mean(wide * wide, axis=-1, keepdims=True) + NORM_EPSILON)
            values = (wide * scale * gain_ref[...]).astype(jnp.bfloat16)
        weight_refs, refs = refs[: len(weights)], refs[len(weights) :]
        refs[0][...] = values.reshape(count, chunk, model)
        for weight_ref, out_ref in zip(weight_refs, refs[1:]):
            out = jnp.dot(values, weight_ref[...], preferred_element_type=jnp.float32)
            out_ref[...] = out.reshape(count, chunk, out.shape[1])

    widths = [weight.shape[1] for weight in weights]
    outs = [shaped((count, rows, model), jnp.bfloat16)] + [shaped((count, rows, w)) for w in widths]
    done = pl.pallas_call(
        kernel,
        grid=(steps,),
        in_specs=slot_specs(pieces, steps) + [pl.BlockSpec(e.shape, lambda i: (0, 0)) for e in extra],
        out_specs=[pl.BlockSpec((count, chunk, w), lambda i: (0, i, 0)) for w in [model] + widths],
        out_shape=outs,
        compiler_params=pltpu.CompilerParams(vmem_limit_bytes=VMEM_LIMIT),
        name=name,
    )(*flat, *extra)
    return [out.reshape(count * rows, out.shape[2]) for out in done]


def dead_mask(rows, live_count):
    return (rows < live_count).astype(jnp.float32)


def lru_forward_kernel(
    live_ref,
    first_ref,
    pred_ref,
    u_ref,
    tail_ref,
    vec_ref,
    rec_ref,
    in_ref,
    xc_ref,
    keep_ref,
    drive_ref,
    rate_ref,
    entry_ref,
    sum_ref,
    ext_ref,
):
    blocks = u_ref.shape[0] // BLOCK
    tiles = lane_tiles(u_ref.shape[1])
    rows = lax.broadcasted_iota(jnp.int32, (BLOCK, LANES), 0)

    def block(index, carry):
        at = block_rows(index)
        first = first_ref[index]
        pred = pred_ref[index]
        live = dead_mask(rows, live_ref[index])
        before = jnp.maximum(pred, 0)
        joined = jnp.where((pred >= 0) & (first == 0), 1.0, 0.0)
        for low, size in tiles:
            lanes = slice(low, low + size)
            u_value = u_ref[at, lanes]
            ext_ref[0:8, :size] = tail_ref[before, :, lanes] * joined
            ext_ref[8 : 8 + BLOCK, :size] = u_value
            later = vec_ref[1:2, lanes] * ext_ref[7 : 7 + BLOCK, :size]
            for tap in range(2, TAPS):
                later = later + vec_ref[tap : tap + 1, lanes] * ext_ref[8 - tap : 8 - tap + BLOCK, :size]
            conv = vec_ref[4:5, lanes] + vec_ref[0:1, lanes] * u_value + later * live[:, :size]
            xc_ref[at, lanes] = conv.astype(jnp.bfloat16)
        low_rows = xc_ref[at, :]
        pre_rec = jnp.dot(low_rows, rec_ref[...], preferred_element_type=jnp.float32)
        pre_in = jnp.dot(low_rows, in_ref[...], preferred_element_type=jnp.float32)
        for tile, (low, size) in enumerate(tiles):
            lanes = slice(low, low + size)
            rate = jax.nn.sigmoid(pre_rec[:, lanes] + vec_ref[5:6, lanes])
            entry = jax.nn.sigmoid(pre_in[:, lanes] + vec_ref[6:7, lanes])
            minus = expm1_small(rate * vec_ref[7:8, lanes])
            rate_ref[tile, at, :size] = rate
            entry_ref[tile, at, :size] = entry
            keep_ref[tile, at, :size] = (1.0 + minus) * live[:, :size]
            drive_ref[tile, at, :size] = (
                jnp.sqrt(-minus * (2.0 + minus)) * entry * low_rows[:, lanes].astype(jnp.float32)
            )

        @pl.when(first > 0)
        def _():
            top = pl.ds(pl.multiple_of(index * BLOCK, BLOCK), 8)
            after = (rows[:8] > 0).astype(jnp.float32)
            for tile in range(len(tiles)):
                keep_ref[tile, top, :] = keep_ref[tile, top, :] * after

        return carry

    lax.fori_loop(0, blocks, block, 0)

    def step(place, carry):
        at = pl.ds(place, blocks, stride=BLOCK)
        after = []
        for tile, (total, state) in enumerate(carry):
            keep = keep_ref[tile, at, :]
            after.append((total * keep, keep * state + drive_ref[tile, at, :]))
        return tuple(after)

    ones = jnp.ones((blocks, LANES), jnp.float32)
    start = tuple((ones, jnp.zeros_like(ones)) for _ in tiles)
    ends = lax.fori_loop(0, BLOCK, step, start, unroll=UNROLL)
    for tile, (total, state) in enumerate(ends):
        sum_ref[0, tile] = total
        sum_ref[1, tile] = state


def lru_state_kernel(pos_ref, all_ref, keep_ref, drive_ref, ypre_ref, h_ref, hy_ref, enter_ref, line_ref):
    tiles = lane_tiles(ypre_ref.shape[1])
    turns, _, _, blocks, _ = all_ref.shape

    def chain(place, states):
        slot = pos_ref[place]
        turn, index = slot // blocks, slot % blocks
        after = []
        for tile, state in enumerate(states):
            line_ref[tile, pl.ds(slot, 1), :] = state
            keep = all_ref[turn, 0, tile, pl.ds(index, 1), :]
            after.append(keep * state + all_ref[turn, 1, tile, pl.ds(index, 1), :])
        return tuple(after)

    zero = jnp.zeros((1, LANES), jnp.float32)
    lax.fori_loop(0, turns * blocks, chain, tuple(zero for _ in tiles))
    for tile in range(len(tiles)):
        enter_ref[tile] = line_ref[tile, 0:blocks, :]

    def step(place, states):
        at = pl.ds(place, blocks, stride=BLOCK)
        after = []
        for tile, state in enumerate(states):
            state = keep_ref[tile, at, :] * state + drive_ref[tile, at, :]
            h_ref[tile, at, :] = state
            after.append(state)
        return tuple(after)

    start = tuple(line_ref[tile, 0:blocks, :] for tile in range(len(tiles)))
    lax.fori_loop(0, BLOCK, step, start, unroll=UNROLL)

    def block(index, carry):
        at = block_rows(index)
        for tile, (low, size) in enumerate(tiles):
            lanes = slice(low, low + size)
            act = gelu_parts(ypre_ref[at, lanes])[0]
            hy_ref[at, lanes] = (h_ref[tile, at, :size] * act).astype(jnp.bfloat16)
        return carry

    lax.fori_loop(0, blocks, block, 0)


def lru_back(pieces, out_w, state, branch_pre, keep, steps=8):
    slots = tuple(len(slot) for slot in pieces)
    count = len(pieces)
    flat = [part for slot in pieces for part in slot]
    rows = sum(part.shape[0] for part in pieces[0])
    model = flat[0].shape[1]
    width = out_w.shape[0]
    tiles = lane_tiles(width)
    chunk = rows // steps
    blocks = count * rows // BLOCK

    def kernel(*refs):
        values = stack_step(refs[: len(flat)], slots)
        w_ref, h_ref, ypre_ref, keep_ref, out_ref, dy_ref, dh_ref, send_ref = refs[len(flat) :]
        here = pl.program_id(0)
        out_ref[...] = values.reshape(count, chunk, model)
        grads = lax.dot_general(
            values, w_ref[...], (((1,), (1,)), ((), ())), preferred_element_type=jnp.float32
        )
        for slot in range(count):
            span = pl.ds(pl.multiple_of(slot * rows + here * chunk, chunk), chunk)
            for tile, (low, size) in enumerate(tiles):
                lanes = slice(low, low + size)
                value = ypre_ref[slot, :, lanes]
                act, bend = gelu_parts(value)
                grad = grads[slot * chunk : (slot + 1) * chunk, lanes]
                slope = gelu_slope(value, bend)
                dy_ref[slot, :, lanes] = (grad * h_ref[tile, slot, :, :size] * slope).astype(jnp.bfloat16)
                dh_ref[tile, span, :size] = grad * act

        @pl.when(here == steps - 1)
        def _():
            def step(turn, carry):
                at = pl.ds(BLOCK - 1 - turn, blocks, stride=BLOCK)
                return tuple(
                    keep_ref[tile, at, :] * (dh_ref[tile, at, :] + value)
                    for tile, value in enumerate(carry)
                )

            zero = jnp.zeros((blocks, LANES), jnp.float32)
            ends = lax.fori_loop(0, BLOCK, step, tuple(zero for _ in tiles), unroll=UNROLL)
            for tile, value in enumerate(ends):
                send_ref[tile] = value

    depth = len(tiles)
    total = count * rows
    out, dy, dh, send = pl.pallas_call(
        kernel,
        grid=(steps,),
        in_specs=slot_specs(pieces, steps)
        + [
            pl.BlockSpec((width, model), lambda i: (0, 0)),
            pl.BlockSpec((depth, count, chunk, LANES), lambda i: (0, 0, i, 0)),
            pl.BlockSpec((count, chunk, width), lambda i: (0, i, 0)),
            pl.BlockSpec((depth, total, LANES), lambda i: (0, 0, 0)),
        ],
        out_specs=[
            pl.BlockSpec((count, chunk, model), lambda i: (0, i, 0)),
            pl.BlockSpec((count, chunk, width), lambda i: (0, i, 0)),
            pl.BlockSpec((depth, total, LANES), lambda i: (0, 0, 0)),
            pl.BlockSpec((depth, blocks, LANES), lambda i: (0, 0, 0)),
        ],
        out_shape=[
            shaped((count, rows, model), jnp.bfloat16),
            shaped((count, rows, width), jnp.bfloat16),
            shaped((depth, total, LANES)),
            shaped((depth, blocks, LANES)),
        ],
        compiler_params=pltpu.CompilerParams(vmem_limit_bytes=VMEM_LIMIT),
        name="lru_back",
    )(
        *flat,
        out_w,
        state.reshape(depth, count, rows, LANES),
        branch_pre.reshape(count, rows, width),
        keep,
    )
    return out.reshape(total, model), dy.reshape(total, width), dh, send


def fold_rows(values):
    return values.reshape(BLOCK // 8, 8, values.shape[1]).sum(axis=0)


def lru_grad_kernel(
    live_ref,
    first_ref,
    pred_ref,
    pos_ref,
    all_ref,
    back_ref,
    dh_ref,
    keep_ref,
    drive_ref,
    rate_ref,
    entry_ref,
    h_ref,
    enter_ref,
    xc_ref,
    u_ref,
    tail_ref,
    vec_ref,
    rec_ref,
    in_ref,
    drec_ref,
    din_ref,
    du_ref,
    last_ref,
    head_ref,
    total_ref,
    line_ref,
    g_ref,
    ext_ref,
    acc_ref,
    direct_ref,
):
    blocks = u_ref.shape[0] // BLOCK
    width = u_ref.shape[1]
    tiles = lane_tiles(width)
    every = back_ref.shape[0] * blocks
    rows = lax.broadcasted_iota(jnp.int32, (BLOCK, LANES), 0)

    def chain(count, carry):
        slot = pos_ref[every - 1 - count]
        turn, index = slot // blocks, slot % blocks
        after = []
        for tile, value in enumerate(carry):
            line_ref[tile, pl.ds(slot, 1), :] = value
            keep = all_ref[turn, 0, tile, pl.ds(index, 1), :]
            after.append(keep * value + back_ref[turn, tile, pl.ds(index, 1), :])
        return tuple(after)

    zero = jnp.zeros((1, LANES), jnp.float32)
    lax.fori_loop(0, every, chain, tuple(zero for _ in tiles))

    def step(turn, carry):
        at = pl.ds(BLOCK - 1 - turn, blocks, stride=BLOCK)
        after = []
        for tile, value in enumerate(carry):
            grad = dh_ref[tile, at, :] + value
            g_ref[tile, at, :] = grad
            after.append(keep_ref[tile, at, :] * grad)
        return tuple(after)

    start = tuple(line_ref[tile, 0:blocks, :] for tile in range(len(tiles)))
    lax.fori_loop(0, BLOCK, step, start, unroll=UNROLL)
    acc_ref[...] = jnp.zeros_like(acc_ref)
    contract = (((1,), (1,)), ((), ()))

    def block(index, carry):
        at = block_rows(index)
        first = first_ref[index]
        pred = pred_ref[index]
        live = dead_mask(rows, live_ref[index])
        before = jnp.maximum(pred, 0)
        joined = jnp.where((pred >= 0) & (first == 0), 1.0, 0.0)
        for tile, (low, size) in enumerate(tiles):
            lanes = slice(low, low + size)
            grad = g_ref[tile, at, :size]
            rate = rate_ref[tile, at, :size]
            entry = entry_ref[tile, at, :size]
            decay = vec_ref[7:8, lanes]
            minus = expm1_small(rate * decay)
            twice = minus * (2.0 + minus)
            ext_ref[7:8, :size] = enter_ref[tile, pl.ds(index, 1), :size]
            ext_ref[8 : 8 + BLOCK, :size] = h_ref[tile, at, :size]
            d_log = grad * (
                keep_ref[tile, at, :size] * ext_ref[7 : 7 + BLOCK, :size]
                + drive_ref[tile, at, :size] * ((1.0 + twice) / twice)
            )
            slow = rate * d_log
            acc_ref[7, :, lanes] += fold_rows(slow)
            d_rec = (decay * slow * (1.0 - rate)).astype(jnp.bfloat16)
            scaled = grad * jnp.sqrt(-twice) * entry
            d_in = scaled * xc_ref[at, lanes].astype(jnp.float32) * (1.0 - entry)
            d_in = d_in.astype(jnp.bfloat16)
            drec_ref[at, lanes] = d_rec
            din_ref[at, lanes] = d_in
            acc_ref[5, :, lanes] += fold_rows(d_rec.astype(jnp.float32))
            acc_ref[6, :, lanes] += fold_rows(d_in.astype(jnp.float32))
            direct_ref[:, lanes] = scaled
        direct_ref[...] += lax.dot_general(
            drec_ref[at, :], rec_ref[...], contract, preferred_element_type=jnp.float32
        ) + lax.dot_general(
            din_ref[at, :], in_ref[...], contract, preferred_element_type=jnp.float32
        )
        for low, size in tiles:
            lanes = slice(low, low + size)
            dxc = direct_ref[:, lanes]
            u_value = u_ref[at, lanes]
            ext_ref[0:8, :size] = tail_ref[before, :, lanes] * joined
            ext_ref[8 : 8 + BLOCK, :size] = u_value
            acc_ref[4, :, lanes] += fold_rows(dxc)
            acc_ref[0, :, lanes] += fold_rows(dxc * u_value)
            part = dxc * live[:, :size]
            for tap in range(1, TAPS):
                acc_ref[tap, :, lanes] += fold_rows(part * ext_ref[8 - tap : 8 - tap + BLOCK, :size])
            zero_tile = jnp.zeros((8, size), jnp.float32)
            ext_ref[0:8, :size] = zero_tile
            ext_ref[8 : 8 + BLOCK, :size] = part
            ext_ref[8 + BLOCK : 16 + BLOCK, :size] = zero_tile
            du_value = dxc * vec_ref[0:1, lanes]
            head = zero_tile
            for tap in range(1, TAPS):
                weight = vec_ref[tap : tap + 1, lanes]
                du_value = du_value + weight * ext_ref[8 + tap : 8 + tap + BLOCK, :size]
                head = head + weight * ext_ref[tap : tap + 8, :size]
            du_ref[at, lanes] = du_value.astype(jnp.bfloat16)
            last_ref[index, :, lanes] = du_value[BLOCK - 8 :]
            head_ref[index, :, lanes] = head * joined
        return carry

    lax.fori_loop(0, blocks, block, 0)
    for index in range(8):
        total_ref[index : index + 1, :] = jnp.sum(acc_ref[index], axis=0, keepdims=True)


def head_kernel(succ_ref, prev_ref, last_ref, head_ref, out_ref):
    blocks = last_ref.shape[0]

    def block(index, carry):
        succ = succ_ref[index]
        head = head_ref[jnp.maximum(succ, 0)]
        tail = last_ref[index] + jnp.where(succ >= 0, head, jnp.zeros_like(head))
        out_ref[index, :8, :] = prev_ref[index, :8, :]
        out_ref[index, 8:, :] = tail.astype(jnp.bfloat16)
        return carry

    lax.fori_loop(0, blocks, block, 0)


def shaped(shape, dtype=jnp.float32):
    return jax.ShapeDtypeStruct(shape, dtype)


def whole(kernel, scalars, arrays, outs, scratch, name):
    specs = [pl.BlockSpec(memory_space=pltpu.SMEM)] * len(scalars)
    specs += [pl.BlockSpec(memory_space=pltpu.VMEM)] * len(arrays)
    return pl.pallas_call(
        kernel,
        out_shape=outs,
        in_specs=specs,
        out_specs=[pl.BlockSpec(memory_space=pltpu.VMEM)] * len(outs),
        scratch_shapes=scratch,
        compiler_params=pltpu.CompilerParams(vmem_limit_bytes=VMEM_LIMIT),
        name=name,
    )(*scalars, *arrays)


def shards(
    tokens,
    cotangent,
    lengths,
    offsets,
    deal,
    norm_gain1,
    w_branch,
    w_input,
    conv_kernel,
    conv_bias,
    gate_rec,
    bias_rec,
    gate_in,
    bias_in,
    decay_param,
    w_out,
    norm_gain2,
    w_gate,
    w_up,
    w_down,
):
    seq_size, z_size = lax.axis_size("seq"), lax.axis_size("fsdp")
    seq_at, z_at = lax.axis_index("seq"), lax.axis_index("fsdp")
    rows_here, model = tokens.shape
    blocks_here = rows_here // BLOCK
    blocks = seq_size * blocks_here
    every = blocks * z_size
    count = rows_here * seq_size
    width = w_branch.shape[1] // seq_size
    ffw = w_gate.shape[1] // seq_size
    chunk = w_branch.shape[0]
    gate_width = gate_rec.shape[1]
    groups = width // gate_width
    tiles = len(lane_tiles(width))
    tiled = shaped((tiles, count, LANES))

    order = jnp.array([k for k in range(seq_size) if k % 2 == 0] + [k for k in range(seq_size) if k % 2], jnp.int32)
    source = jnp.bitwise_xor(order, seq_at)
    flips = jnp.bitwise_xor(jnp.arange(z_size, dtype=jnp.int32), z_at)
    stored = (source[None, :, None] * z_size + flips[:, None, None]) * blocks_here
    stored = (stored + jnp.arange(blocks_here, dtype=jnp.int32)[None, None, :]).reshape(every)
    logical = deal[stored]
    places = jnp.arange(every, dtype=jnp.int32)
    at_place = logical[None, :] == places[:, None]
    position = jnp.sum(jnp.where(at_place, places[None, :], 0), axis=1)
    mine = logical[:blocks]

    def place_of(wanted):
        hit = logical[None, :] == wanted[:, None]
        return jnp.sum(jnp.where(hit, places[None, :] + 1, 0), axis=1) - 1

    pred = place_of(mine - 1)
    succ = place_of(mine + 1)
    left_over = lengths[None, :] - (mine[:, None] - offsets[None, :]) * BLOCK
    inside = (mine[:, None] >= offsets[None, :]) & (left_over > 0)
    live_count = jnp.max(jnp.where(inside, jnp.minimum(left_over, BLOCK), 0), axis=1)
    first = jnp.any(inside & (mine[:, None] == offsets[None, :]), axis=1).astype(jnp.int32)
    own_live = live_count[:blocks_here]
    live_col = (
        jnp.arange(BLOCK, dtype=jnp.int32)[None, :] < own_live[:, None]
    ).astype(jnp.float32).reshape(rows_here, 1)

    def columns(weight):
        return jnp.swapaxes(as_low(weight).reshape(chunk, seq_size, -1), 0, 1)

    def exchange(value):
        return lax.all_to_all(value, "seq", 0, 0, tiled=True)

    def gather_columns(value):
        got = lax.all_gather(value, "fsdp", axis=0, tiled=False)
        return jnp.swapaxes(got, 0, 1).reshape(-1, value.shape[-1])

    def gather_rows(value):
        return lax.all_gather(value, "fsdp", axis=0, tiled=True)

    barrier = lax.optimization_barrier
    out_w = gather_rows(as_low(w_out))
    mix = exchange(jnp.stack([columns(w_input), columns(w_branch)], axis=1))
    x_pieces = gather_plane(tokens)
    wide_small = jnp.concatenate(
        [
            as_low(conv_kernel),
            as_low(conv_bias)[None],
            as_low(bias_rec)[None],
            as_low(bias_in)[None],
            as_low(decay_param)[None],
            as_low(jnp.pad(jnp.stack([norm_gain1, norm_gain2]), ((0, 0), (0, width // z_size - chunk)))),
        ],
        axis=0,
    ).T
    small = jnp.concatenate([as_low(gate_rec), as_low(gate_in), wide_small], axis=1)
    small, x_pieces = barrier((small, x_pieces))
    small = lax.all_gather(small, "fsdp", axis=0, tiled=False)
    gains = lax.all_gather(small[:, :chunk, 2 * gate_width + 8 :], "seq", axis=0, tiled=False)
    gains = as_wide(gains.reshape(model, 2)).T
    gain_one, gain_two = gains[:1], gains[1:]
    small = small.reshape(width, -1)
    input_w = gather_columns(mix[:, 0])
    branch_w = gather_columns(mix[:, 1])
    ff = exchange(jnp.stack([columns(w_gate), columns(w_up)], axis=1))
    down_w = gather_rows(as_low(w_down))

    same = jnp.arange(width)[:, None] // gate_width == jnp.arange(width)[None, :] // gate_width

    def diagonal(part):
        return jnp.where(same, jnp.tile(part, (1, groups)), jnp.zeros((), jnp.bfloat16))

    rec_w = diagonal(small[:, :gate_width])
    in_w = diagonal(small[:, gate_width : 2 * gate_width])
    vectors = as_wide(small[:, 2 * gate_width : 2 * gate_width + 8]).T
    decay = vectors[7]
    vectors = jnp.concatenate([vectors[:7], -GATE_SCALE * jax.nn.softplus(-decay)[None]], axis=0)

    x_pieces, top_own = barrier((x_pieces, as_low(live_col * as_wide(cotangent))))
    normed_one, u_value = stack(x_pieces, "norm_one", gain_one, (input_w,))
    normed_one, ff = barrier((normed_one, ff))
    gate_w = gather_columns(ff[:, 0])
    up_w = gather_columns(ff[:, 1])
    top_pieces = gather_plane(top_own)

    def edges(rows):
        rows = spread_z(as_low(rows).reshape(blocks * (TAPS - 1), width))
        rows = as_wide(rows).reshape(every, TAPS - 1, width)
        return jnp.pad(rows, ((0, 0), (9 - TAPS, 0), (0, 0)))

    tails = edges(u_value.reshape(blocks, BLOCK, width)[:, BLOCK - TAPS + 1 :])
    branch_pre = mm(normed_one, branch_w)
    conv_low, keep, drive, rate, entry, summary = whole(
        lru_forward_kernel,
        (live_count, first, pred),
        (u_value, tails, vectors, rec_w, in_w),
        (
            shaped((count, width), jnp.bfloat16),
            tiled,
            tiled,
            tiled,
            tiled,
            shaped((2, tiles, blocks, LANES)),
        ),
        [pltpu.VMEM((BLOCK + 8, LANES), jnp.float32)],
        "lru_forward",
    )
    summaries = spread_z(summary)
    summaries, top_pieces, out_w, branch_pre = barrier(
        (summaries, top_pieces, out_w, branch_pre)
    )
    state, gated, enter = whole(
        lru_state_kernel,
        (position,),
        (summaries, keep, drive, branch_pre),
        (
            tiled,
            shaped((count, width), jnp.bfloat16),
            shaped((tiles, blocks, LANES)),
        ),
        [pltpu.VMEM((tiles, every, LANES), jnp.float32)],
        "lru_state",
    )
    gated, gate_w = barrier((gated, gate_w))
    half = count // 2

    def side(rows, odd):
        return rows[half:] if odd else rows[:half]

    resid_in = as_wide(tokens)
    resid_mid = resid_in + scatter_plane(lambda odd: mm(side(gated, odd), out_w))
    scale_two = lax.rsqrt(jnp.mean(resid_mid * resid_mid, axis=-1, keepdims=True) + NORM_EPSILON)
    own_two = as_low(resid_mid * scale_two * gain_two)
    own_two, up_w = barrier((own_two, up_w))
    two_pieces = gather_plane(own_two)
    (top_low,) = stack(top_pieces, "stack_top")
    two_pieces, top_low = barrier((two_pieces, top_low))
    (normed_two,) = stack(two_pieces, "stack_two")
    gate_pre = mm(normed_two, gate_w)
    up_pre = mm(normed_two, up_w)
    act, bend = gelu_parts(gate_pre)
    hidden = as_low(act * up_pre)
    grad_down = mm_tn(hidden, top_low, jnp.bfloat16)
    gate_pre, up_pre, hidden, grad_down, down_w = barrier(
        (gate_pre, up_pre, hidden, grad_down, down_w)
    )
    act, bend = gelu_parts(gate_pre)
    grad_hidden = mm_nt(top_low, down_w)
    d_gate = as_low(grad_hidden * up_pre * gelu_slope(gate_pre, bend))
    d_up = as_low(grad_hidden * act)
    grad_normed_two = scatter_plane(
        lambda odd: mm_nt(side(d_gate, odd), gate_w) + mm_nt(side(d_up, odd), up_w)
    )
    grad_gate = mm_tn(normed_two, d_gate, jnp.bfloat16)
    grad_up = mm_tn(normed_two, d_up, jnp.bfloat16)

    def home_rows(value):
        return lax.psum_scatter(value, "fsdp", scatter_dimension=0, tiled=True)

    def by_owner(values):
        parts = [value.reshape(seq_size, z_size, chunk, value.shape[-1]) for value in values]
        return jnp.transpose(jnp.stack(parts, axis=0), (2, 1, 0, 3, 4))

    def own_columns(got):
        return as_wide(jnp.swapaxes(got, 0, 1).reshape(chunk, -1))

    down_home = home_rows(grad_down)
    ff_pair = by_owner((grad_gate, grad_up)).reshape(z_size * seq_size * 2 * chunk, ffw)
    grad_normed_two, ff_pair, down_home = barrier((grad_normed_two, ff_pair, down_home))
    ff_home = home_rows(ff_pair)

    def gain_home(gain, pairs):
        total = sum(jnp.sum(grad * as_wide(as_low(weight)), axis=1) for grad, weight in pairs)
        return total / as_wide(as_low(gain))

    scaled_two = gain_two * grad_normed_two
    grad_mid = (
        live_col * as_wide(cotangent)
        + scale_two * scaled_two
        - resid_mid
        * scale_two
        * scale_two
        * scale_two
        * jnp.mean(scaled_two * resid_mid, axis=-1, keepdims=True)
    )
    out_pieces = gather_plane(as_low(grad_mid))

    def after_out(value):
        return barrier((value, out_pieces))[0]

    mlp_out = scatter_plane(lambda odd: mm(side(hidden, odd), down_w), after_out)
    mixed = as_low(live_col * (resid_mid + mlp_out))
    grad_out_low, d_branch, direct, send = lru_back(out_pieces, out_w, state, branch_pre, keep)
    backs = spread_z(send)
    grad_out = mm_tn(gated, grad_out_low, jnp.bfloat16)
    backs, grad_out = barrier((backs, grad_out))
    out_home = home_rows(grad_out)
    d_rec, d_in, du_part, du_last, heads, totals = whole(
        lru_grad_kernel,
        (live_count, first, pred, position),
        (
            summaries,
            backs,
            direct,
            keep,
            drive,
            rate,
            entry,
            state,
            enter,
            conv_low,
            u_value,
            tails,
            vectors,
            rec_w,
            in_w,
        ),
        (
            shaped((count, width), jnp.bfloat16),
            shaped((count, width), jnp.bfloat16),
            shaped((count, width), jnp.bfloat16),
            shaped((blocks, 8, width)),
            shaped((blocks, 8, width)),
            shaped((8, width)),
        ),
        [
            pltpu.VMEM((tiles, every, LANES), jnp.float32),
            pltpu.VMEM((tiles, count, LANES), jnp.float32),
            pltpu.VMEM((BLOCK + 16, LANES), jnp.float32),
            pltpu.VMEM((8, 8, width), jnp.float32),
            pltpu.VMEM((BLOCK, width), jnp.float32),
        ],
        "lru_grad",
    )
    du_part, heads, totals, d_rec, d_in, d_branch, ff_home = barrier(
        (du_part, heads, totals, d_rec, d_in, d_branch, ff_home)
    )
    heads = edges(heads[:, 9 - TAPS :])
    grad_branch = mm_tn(normed_one, d_branch, jnp.bfloat16)
    full_rec, full_in = mm_tn(conv_low, d_rec), mm_tn(conv_low, d_in)
    du_part = du_part.reshape(blocks, BLOCK, width)
    (patch,) = whole(
        head_kernel,
        (succ,),
        (du_part[:, BLOCK - 16 :], du_last, heads),
        (shaped((blocks, 16, width), jnp.bfloat16),),
        [],
        "lru_heads",
    )
    d_input = lax.dynamic_update_slice(du_part, patch, (0, BLOCK - 16, 0)).reshape(count, width)
    d_input, mixed, grad_branch, full_rec, full_in, out_home = barrier(
        (d_input, mixed, grad_branch, full_rec, full_in, out_home)
    )
    grad_input = mm_tn(normed_one, d_input, jnp.bfloat16)
    got = exchange(ff_home.reshape(seq_size, 2, chunk, ffw))
    grad_gate_home, grad_up_home = own_columns(got[:, 0]), own_columns(got[:, 1])
    grad_gain_two = gain_home(norm_gain2, ((grad_gate_home, w_gate), (grad_up_home, w_up)))
    grad_normed_one = scatter_plane(
        lambda odd: mm_nt(side(d_branch, odd), branch_w) + mm_nt(side(d_input, odd), input_w)
    )
    scaled_one = gain_one * grad_normed_one
    scale_one = lax.rsqrt(jnp.mean(resid_in * resid_in, axis=-1, keepdims=True) + NORM_EPSILON)
    tokens_grad = as_low(
        grad_mid
        + scale_one * scaled_one
        - resid_in
        * scale_one
        * scale_one
        * scale_one
        * jnp.mean(scaled_one * resid_in, axis=-1, keepdims=True)
    )

    def blocks_of(full, start):
        place = start + jnp.arange(width)[:, None] % gate_width
        fold = (place == jnp.arange(2 * gate_width)[None, :]).astype(jnp.float32)
        full = jnp.where(same, full, 0.0)
        return jnp.dot(full, fold, precision=lax.Precision.HIGHEST)

    totals = jnp.concatenate(
        [totals[:7], totals[7:] * (GATE_SCALE * jax.nn.sigmoid(-decay))[None]], axis=0
    )
    owned = width // z_size
    gates = blocks_of(full_rec, 0) + blocks_of(full_in, gate_width)
    gates = as_low(gates).reshape(z_size, owned, 2 * gate_width)
    totals = jnp.swapaxes(jnp.pad(totals, ((0, 8), (0, 0))).reshape(16, z_size, owned), 0, 1)
    totals = as_low(totals)
    lanes = max(width, 2 * gate_width)
    edge = seq_size * chunk
    pack = jnp.concatenate(
        [
            jnp.pad(part, ((0, 0), (0, 0), (0, lanes - part.shape[-1])))
            for part in (by_owner((grad_branch,)).reshape(z_size, edge, width), gates, totals)
        ],
        axis=1,
    )
    pack = home_rows(pack.reshape(z_size * pack.shape[1], lanes))
    input_home = home_rows(by_owner((grad_input,)).reshape(z_size * edge, width))
    grad_branch_home = own_columns(exchange(pack[:edge, :width].reshape(seq_size, chunk, width)))
    grad_input_home = own_columns(exchange(input_home.reshape(seq_size, chunk, width)))
    grad_gain_one = gain_home(
        norm_gain1, ((grad_branch_home, w_branch), (grad_input_home, w_input))
    )
    gates = as_wide(pack[edge : edge + owned])
    totals = as_wide(pack[edge + owned :, :owned])
    return (
        mixed,
        tokens_grad,
        grad_gain_one,
        grad_branch_home,
        grad_input_home,
        totals[:TAPS],
        totals[4],
        gates[:, :gate_width],
        totals[5],
        gates[:, gate_width : 2 * gate_width],
        totals[6],
        totals[7],
        as_wide(out_home),
        grad_gain_two,
        grad_gate_home,
        grad_up_home,
        as_wide(down_home),
    )


def solution(mesh):
    row = P(("seq", "fsdp"))
    rows = P(("seq", "fsdp"), None)
    columns = P(None, ("seq", "fsdp"))
    return jax.shard_map(
        shards,
        mesh=mesh,
        in_specs=(
            rows,
            rows,
            P(),
            P(),
            P(),
            row,
            rows,
            rows,
            columns,
            row,
            rows,
            row,
            rows,
            row,
            row,
            rows,
            row,
            rows,
            rows,
            rows,
        ),
        out_specs=(
            rows,
            rows,
            row,
            rows,
            rows,
            columns,
            row,
            rows,
            row,
            rows,
            row,
            row,
            rows,
            row,
            rows,
            rows,
            rows,
        ),
        check_vma=False,
    )
```

time: 4260 us -> 869 us (0.20)
  waiting for transfers between devices: 2880 us -> 259 us
  blocking collectives: 467 us -> 42.8 us
  local copies, waits for them, and re-layouts: 433 us -> 84.4 us
  Pallas kernels: 0 us -> 113 us
  other arithmetic: 189 us -> 77.3 us
  starting transfers between devices: 0.62 us -> 90.2 us
  matrix products: 255 us -> 179 us
    reduce_scatter x8 -> x5, waiting for transfers between devices: 2860 us -> 36.9 us  [home_rows(): return lax.psum_scatter(value, 'fsdp', scatter_dimension=0, tiled=True)]
    all_gather x13 -> x2, blocking collectives: 378 us -> 25.2 us  [the longest x1 16.3 us: shards(): small = lax.all_gather(small, 'fsdp', axis=0, tiled=False)]
    slice x128 -> x28, local copies, waits for them, and re-layouts: 232 us -> 24.8 us  [the longest x4 6.39 us: part(): return pair[start:start + half]]
    ppermute x0 -> x76, waiting for transfers between devices: none -> 189 us  [swap(): return lax.ppermute(values, axis, [(i, i ^ flip) for i in range(count)])]
    pallas_call x0 -> x8, Pallas kernels: none -> 113 us  [the longest x4 62.2 us: whole(): pl.pallas_call(kernel, out_shape=outs, in_specs=specs, out_specs=[pl.Bloc...]
    unnamed x3 -> x0, blocking collectives: 89.3 us -> none
    pad x62 -> x0, local copies, waits for them, and re-layouts: 77.9 us -> none  [the longest x24 51.8 us: shards(): lax.associative_scan(chain_join, (keep_blocks, drive_blocks), axis=1)]
    dot_general x33 -> x26, matrix products: 255 us -> 179 us  [the longest x9 73.1 us: mm_nt(): lax.dot_general(left, right, (((1,), (1,)), ((), ())), preferred_element_...]
  transfers between devices with their start and end apart: 15 -> 91, of which waited for: 9 -> 31; matrix products, arithmetic and copies ran while one was open for 12% -> 30% of each run, Pallas kernels for 0% -> 13%
where the time goes in v1:
time: 869 us; the launch traced here: 862 us
  waiting for transfers between devices  259 us (30%)
  matrix products  179 us (21%)
  Pallas kernels  113 us (13%)
  starting transfers between devices  90.2 us (10%)
  local copies, waits for them, and re-layouts  84.4 us (10%)
  other arithmetic  77.3 us (9%)
  blocking collectives  42.8 us (5%)
  between operations  15.8 us (2%)
    ppermute x76, waiting for transfers between devices, swap(): return lax.ppermute(values, axis, [(i, i ^ flip) for i in range(count)])  189 us
    dot_general x9, matrix products, mm_nt(): lax.dot_general(left, right, (((1,), (1,)), ((), ())), preferred_element_...  73.1 us
    ppermute x76, starting transfers between devices, swap(): return lax.ppermute(values, axis, [(i, i ^ flip) for i in range(count)])  72.3 us
    pallas_call x4, Pallas kernels, whole(): pl.pallas_call(kernel, out_shape=outs, in_specs=specs, out_specs=[pl.Bloc...  62.2 us
    dot_general x8, matrix products, mm_tn(): lax.dot_general(left, right, (((0,), (0,)), ((), ())), preferred_element_...  53.7 us
    dot_general x7, matrix products, mm(): return jnp.dot(left, right, preferred_element_type=jnp.float32).astype(out)  50.3 us
    reduce_scatter x5, waiting for transfers between devices, home_rows(): return lax.psum_scatter(value, 'fsdp', scatter_dimension=0, tiled=True)  36.9 us
    pallas_call x3, Pallas kernels, stack(): pl.pallas_call(kernel, grid=(steps,), in_specs=slot_specs(pieces, steps)...  30.1 us
  transfers between devices with their start and end apart: 91, of which 31 were waited for; matrix products, arithmetic and copies ran while one was open for 30% of the time, Pallas kernels for 13%

profile of v1, /device:TPU:0, one launch (start us, length us, event | category | flops | bytes accessed | tf_op | source)
XLA Modules:
  0.0 861.6 jit_solution(15847782151531962613)
XLA Ops:
  10.4 17.7 %all_to_all.25 = bf16[8,2,64,320]{3,2,1,0:T(8,128)(2,1)S(1)} all-to-all(bf16[8,2,64,320]{3,2,1,0:T(8,128)(2,1)S(1)} %copy.206), channel_id=1, replica_groups=mesh['seq'=8,'fsdp'=4] {'seq'}, dimensions={0} | all-to-all | bytes 1310720 | tf_op jit(solution)/shard_map/all_to_all | solution.py:626
  36.0 4.4 all-to-all-start.1
  42.6 13.4 %collective-permute-done.1.refs_2_ = bf16[256,2048]{1,0:T(8,128)(2,1)S(1)} collective-permute-done((bf16[256,2048]{1,0:T(8,128)(2,1)S(1)}, bf16[256,2048]{1,0:T(8,128)(2,1)S(1)}, u32[]{:S(2)}, u32[]{:S(2)}) %collective-permute-start.1) | collective-permute-done | bytes 1048608 | tf_op jit(solution)/shard_map/ppermute | solution.py:45
  60.8 21.8 %collective-permute-done.2.refs_3_ = bf16[128,2048]{1,0:T(8,128)(2,1)} collective-permute-done((bf16[128,2048]{1,0:T(8,128)(2,1)S(1)}, bf16[128,2048]{1,0:T(8,128)(2,1)}, u32[]{:S(2)}, u32[]{:S(2)}) %collective-permute-start.2) | collective-permute-done | bytes 524320 | tf_op jit(solution)/shard_map/ppermute | solution.py:45
  86.3 16.3 %all-gather = bf16[320,330]{1,0:T(8,128)(2,1)S(1)} all-gather(bf16[80,330]{1,0:T(8,128)(2,1)S(1)} %pad_maximum_fusion.8), channel_id=2, replica_groups=mesh['seq'=8,'fsdp'=4] {'fsdp'}, dimensions={0}, use_global_device_ids=true | all-gather | bytes 264000 | tf_op jit(solution)/shard_map/all_gather | solution.py:652
  102.8 8.8 %all-gather.1 = bf16[32,64,2]{1,2,0:T(2,128)(2,1)S(1)} all-gather(bf16[4,64,2]{1,2,0:T(2,128)(2,1)S(1)} %copy.204), channel_id=3, replica_groups=mesh['seq'=8,'fsdp'=4] {'seq'}, dimensions={0}, use_global_device_ids=true | all-gather | bytes 9216 | tf_op jit(solution)/shard_map/all_gather | solution.py:653
  114.7 13.1 %norm_one.1 = (bf16[8,256,2048]{2,1,0:T(8,128)(2,1)}, f32[8,256,320]{2,1,0:T(8,128)}) custom-call(bf16[256,2048]{1,0:T(8,128)(2,1)S(1)} %copy-done.2, bf16[256,2048]{1,0:T(8,128)(2,1)} %collective-permute-done.refs_1_, bf16[256,2048]{1,0:T(8,128)(2,1)S(1)} %collective-permute-done.1.refs_2_, bf16[128,2048]{1,0:T(8,128)(2,1)} %collective-permute-done.2.refs_3_, ...), custom_call_target="tpu_custom_call" | custom-call | tf_op jit(solution)/shard_map/norm_one/pallas_call | solution.py:172
  143.8 12.8 %collective-permute-done.16.refs_2_ = bf16[256,2048]{1,0:T(8,128)(2,1)S(1)} collective-permute-done((bf16[256,2048]{1,0:T(8,128)(2,1)S(1)}, bf16[256,2048]{1,0:T(8,128)(2,1)S(1)}, u32[]{:S(2)}, u32[]{:S(2)}) %collective-permute-start.16) | collective-permute-done | bytes 1048608 | tf_op jit(solution)/shard_map/ppermute | solution.py:45
  180.8 17.0 %lru_forward.1 = (bf16[2048,320]{1,0:T(8,128)(2,1)S(1)}, f32[3,2048,128]{2,1,0:T(8,128)S(1)}, f32[3,2048,128]{2,1,0:T(8,128)}, f32[3,2048,128]{2,1,0:T(8,128)}, ...) custom-call(s32[16]{0:T(128)S(1)} %select_reduce_fusion.3.live_ref, s32[16]{0:T(128)S(1)} %convert_element_type.354.first_ref, ...), custom_call_target="tpu_custom_call" | custom-call | tf_op jit(solution)/shard_map/lru_forward/pallas_call | solution.py:548
  214.2 7.9 fusion.102
  226.3 13.9 %lru_state.1 = (f32[3,2048,128]{2,1,0:T(8,128)S(1)}, bf16[2048,320]{1,0:T(8,128)(2,1)S(1)}, f32[3,16,128]{2,1,0:T(8,128)S(1)}) custom-call(s32[64]{0:T(128)S(1)} %select_reduce_fusion.pos_ref, f32[4,2,3,16,128]{4,3,2,1,0:T(8,128)S(1)} %copy-done.13, f32[3,2048,128]{2,1,0:T(8,128)} %copy-done.3, f32[3,2048,128]{2,1,0:T(8,128)} %get-tuple-element.142.drive_ref, ...), custom_call_target="tpu_custom_call" | custom-call | tf_op jit(solution)/shard_map/lru_state/pallas_call | solution.py:548
  252.1 6.9 collective-permute-done.24
  259.0 5.5 fusion.99
  269.2 11.3 %collective-permute-done.26 = bf16[128,2048]{1,0:T(8,128)(2,1)S(1)} collective-permute-done((bf16[128,2048]{1,0:T(8,128)(2,1)S(1)}, bf16[128,2048]{1,0:T(8,128)(2,1)S(1)}, u32[]{:S(2)}, u32[]{:S(2)}) %collective-permute-start.26) | collective-permute-done | bytes 524320 | tf_op jit(solution)/shard_map/ppermute | solution.py:45
  282.7 8.4 collective-permute-done.25
  298.1 16.8 %all-gather.23.cloned.1.call-done = bf16[32,1,64,768]{3,2,1,0:T(8,128)(2,1)} async-done(((bf16[8,1,64,768]{3,2,1,0:T(8,128)(2,1)}), bf16[32,1,64,768]{3,2,1,0:T(8,128)(2,1)}) %all-gather.23.cloned.1.call-update) | async-done | bytes 3145744 | tf_op jit(solution)/shard_map/all_gather | solution.py:629
  325.7 22.0 %collective-permute-done.32.refs_2_ = bf16[256,2048]{1,0:T(8,128)(2,1)} collective-permute-done((bf16[256,2048]{1,0:T(8,128)(2,1)S(1)}, bf16[256,2048]{1,0:T(8,128)(2,1)}, u32[]{:S(2)}, u32[]{:S(2)}) %collective-permute-start.32) | collective-permute-done | bytes 1048608 | tf_op jit(solution)/shard_map/ppermute | solution.py:45
  353.4 8.2 collective-permute-done.33.refs_3_
  366.3 8.3 stack_top.1
  374.7 8.7 %stack_two.1 = bf16[8,256,2048]{2,1,0:T(8,128)(2,1)} custom-call(bf16[256,2048]{1,0:T(8,128)(2,1)S(1)} %multiply_convert_fusion.1.refs_0_, bf16[256,2048]{1,0:T(8,128)(2,1)} %collective-permute-done.31.refs_1_, bf16[256,2048]{1,0:T(8,128)(2,1)} %collective-permute-done.32.refs_2_, bf16[128,2048]{1,0:T(8,128)(2,1)} %collective-permute-done.33.refs_3_, ...), custom_call_target="tpu_custom_call" | custom-call | tf_op jit(solution)/shard_map/stack_two/pallas_call | solution.py:172
  383.4 10.9 %fusion.103 = f32[2048,768]{1,0:T(8,128)} fusion(bf16[2048,2048]{1,0:T(8,128)(2,1)} %bitcast.194, bf16[2048,768]{1,0:T(8,128)(2,1)S(1)} %bitcast.213), kind=kOutput, calls=%fused_computation.231 | convolution fusion | flops 6442450944 | bytes 17825792 | tf_op jit(solution)/shard_map/dot_general | solution.py:28
  394.3 12.2 %fusion.5 = (bf16[2048,768]{1,0:T(8,128)(2,1)S(1)}, f32[2048,768]{1,0:T(8,128)}) fusion(f32[2048,768]{1,0:T(8,128)} %fusion.103, bf16[2048,2048]{1,0:T(8,128)(2,1)S(1)} %bitcast.196, bf16[2048,768]{1,0:T(8,128)(2,1)S(1)} %bitcast.191), kind=kOutput, calls=%fused_computation.15 | convolution fusion | flops 6458179584 | bytes 27262976 | tf_op jit(solution)/shard_map/dot_general | solution.py:28
  408.2 8.4 convolution_convert_fusion.2
  416.5 10.5 %all-gather.15.cloned.1.call-done = bf16[768,2048]{1,0:T(8,128)(2,1)} async-done(((bf16[192,2048]{1,0:T(8,128)(2,1)}), bf16[768,2048]{1,0:T(8,128)(2,1)}) %all-gather.15.cloned.1.call-update) | async-done | bytes 3145744 | tf_op jit(solution)/shard_map/all_gather | solution.py:633
  427.1 16.5 %multiply_convert_fusion = (bf16[2048,768]{1,0:T(8,128)(2,1)S(1)}, bf16[2048,768]{1,0:T(8,128)(2,1)S(1)}) fusion(f32[2048,768]{1,0:T(8,128)} %fusion.103, f32[2048,768]{1,0:T(8,128)} %get-tuple-element.173, bf16[2048,2048]{1,0:T(8,128)(2,1)} %bitcast.200, bf16[768,2048]{1,0:T(8,128)(2,1)} %all-gather.15.cloned.1.call-done), kind=kOutput, calls=%fused_computation.24 | convolution fusion | flops 6478626816 | bytes 30408704 | tf_op jit(solution)/shard_map/dot_general | solution.py:38
  443.6 5.8 fusion.26
  449.4 7.4 add_convert_fusion.1
  464.3 7.8 fusion.100
  476.7 11.3 %collective-permute-done.42 = bf16[128,2048]{1,0:T(8,128)(2,1)S(1)} collective-permute-done((bf16[128,2048]{1,0:T(8,128)(2,1)}, bf16[128,2048]{1,0:T(8,128)(2,1)S(1)}, u32[]{:S(2)}, u32[]{:S(2)}) %collective-permute-start.42) | collective-permute-done | bytes 524320 | tf_op jit(solution)/shard_map/ppermute | solution.py:45
  491.1 10.6 %convolution_convert_fusion.4 = bf16[2048,768]{1,0:T(8,128)(2,1)S(1)} fusion(bf16[2048,2048]{1,0:T(8,128)(2,1)} %bitcast.195, bf16[2048,768]{1,0:T(8,128)(2,1)} %copy-done.100), kind=kOutput, calls=%fused_computation.35 | convolution fusion | flops 6444023808 | bytes 14680064 | tf_op jit(solution)/shard_map/dot_general | solution.py:32
  506.2 7.4 convolution_convert_fusion.3
  520.1 12.7 %reduce-scatter.6.cloned.1.call-done = bf16[192,2048]{1,0:T(8,128)(2,1)} async-done(((bf16[768,2048]{1,0:T(8,128)(2,1)}), bf16[192,2048]{1,0:T(8,128)(2,1)}) %reduce-scatter.6.cloned.1.call-update) | async-done | bytes 786448 | tf_op jit(solution)/shard_map/reduce_scatter | solution.py:752
  542.0 21.8 %collective-permute-done.48.refs_2_ = bf16[256,2048]{1,0:T(8,128)(2,1)S(1)} collective-permute-done((bf16[256,2048]{1,0:T(8,128)(2,1)S(1)}, bf16[256,2048]{1,0:T(8,128)(2,1)S(1)}, u32[]{:S(2)}, u32[]{:S(2)}) %collective-permute-start.48) | collective-permute-done | bytes 1048608 | tf_op jit(solution)/shard_map/ppermute | solution.py:45
  567.5 9.1 %collective-permute-done.49.refs_3_ = bf16[128,2048]{1,0:T(8,128)(2,1)S(1)} collective-permute-done((bf16[128,2048]{1,0:T(8,128)(2,1)S(1)}, bf16[128,2048]{1,0:T(8,128)(2,1)S(1)}, u32[]{:S(2)}, u32[]{:S(2)}) %collective-permute-start.49) | collective-permute-done | bytes 524320 | tf_op jit(solution)/shard_map/ppermute | solution.py:45
  582.4 5.7 fusion.32
  589.3 11.5 %fusion.88 = (bf16[1024,2048]{1,0:T(8,128)(2,1)}, f32[1024,2048]{1,0:T(8,128)}) fusion(f32[1024,2048]{1,0:T(8,128)} %fusion.32, bf16[1024,2048]{1,0:T(8,128)(2,1)} %collective-permute-done.62), kind=kLoop, calls=%fused_computation.216 | loop fusion | flops 6291456 | bytes 25165824 | tf_op jit(solution)/shard_map/convert.32
  605.5 21.2 %lru_back.1 = (bf16[8,256,2048]{2,1,0:T(8,128)(2,1)}, bf16[8,256,320]{2,1,0:T(8,128)(2,1)}, f32[3,2048,128]{2,1,0:T(8,128)}, f32[3,16,128]{2,1,0:T(8,128)S(1)}) custom-call(bf16[256,2048]{1,0:T(8,128)(2,1)S(1)} %get-tuple-element.217.refs_0_, bf16[256,2048]{1,0:T(8,128)(2,1)S(1)} %collective-permute-done.47.refs_1_, ...), custom_call_target="tpu_custom_call" | custom-call | tf_op jit(solution)/shard_map/lru_back/pallas_call | solution.py:356
  638.2 7.6 convolution_convert_fusion.7
  646.0 30.2 %lru_grad.1 = (bf16[2048,320]{1,0:T(8,128)(2,1)S(1)}, bf16[2048,320]{1,0:T(8,128)(2,1)S(1)}, bf16[2048,320]{1,0:T(8,128)(2,1)}, f32[16,8,320]{2,1,0:T(8,128)S(1)...) custom-call(s32[16]{0:T(128)S(1)} %select_reduce_fusion.3.live_ref, s32[16]{0:T(128)S(1)} %convert_element_type.354.first_ref, ...), custom_call_target="tpu_custom_call" | custom-call | tf_op jit(solution)/shard_map/lru_grad/pallas_call | solution.py:548
  689.8 5.6 fusion.52
  695.5 7.6 convolution_convert_fusion.6
  707.9 8.1 add_convert_fusion
  716.1 7.4 convolution_convert_fusion.5
  744.2 7.4 fusion.55
  752.5 4.6 all-to-all-done.4
  768.8 11.0 %fusion.101 = (bf16[1024,2048]{1,0:T(8,128)(2,1)S(1)}, f32[1024,2048]{1,0:T(8,128)}) fusion(bf16[1024,2048]{1,0:T(8,128)(2,1)} %collective-permute-done.69, f32[1024,2048]{1,0:T(8,128)} %fusion.55, bf16[2048,320]{1,0:T(8,128)(2,1)S(1)} %bitcast.187, bf16[2048,320]{1,0:T(8,128)(2,1)} %bitcast.231), kind=kOutput, calls=%fused_computation.229 | convolution fusion | flops 1350565888 | bytes 27262976 | tf_op jit(solution)/shard_map/dot_general | solution.py:38
  784.1 22.0 %reduce-scatter.12.cloned.1.call-done = bf16[608,320]{1,0:T(8,128)(2,1)} async-done(((bf16[2432,320]{1,0:T(8,128)(2,1)}), bf16[608,320]{1,0:T(8,128)(2,1)}) %reduce-scatter.12.cloned.1.call-update) | async-done | bytes 389136 | tf_op jit(solution)/shard_map/reduce_scatter | solution.py:752
  824.7 12.1 %collective-permute-done.72 = bf16[128,2048]{1,0:T(8,128)(2,1)} collective-permute-done((bf16[128,2048]{1,0:T(8,128)(2,1)}, bf16[128,2048]{1,0:T(8,128)(2,1)}, u32[]{:S(2)}, u32[]{:S(2)}) %collective-permute-start.72) | collective-permute-done | bytes 524320 | tf_op jit(solution)/shard_map/ppermute | solution.py:45
  (553 shorter events, 288.1 us)
Async XLA Ops:
  7.2 104.6 %all-gather.17.cloned.1.call-start = ((), (), s32[]{:S(2)}) async-start(), calls=%async_computation.17 | async-start | bytes 1966080 | tf_op jit(solution)/shard_map/all_gather | solution.py:629
  29.1 182.8 %all-gather.19.cloned.1.call-start = ((), (), s32[]{:S(2)}) async-start(), calls=%async_computation.18 | async-start | bytes 1966080 | tf_op jit(solution)/shard_map/all_gather | solution.py:629
  29.8 26.2 %collective-permute-start.1 = (bf16[256,2048]{1,0:T(8,128)(2,1)S(1)}, bf16[256,2048]{1,0:T(8,128)(2,1)S(1)}, u32[]{:S(2)}, u32[]{:S(2)}) collective-permute-start(bf16[256,2048]{1,0:T(8,128)(2,1)S(1)} %copy-done.2), channel_id=1, source_target_pairs={{0,16},{4,20},{8,24},{12,28},{16,0},{20,4},{24,8},{28,12},{1,17},{... | collective-permute-start | bytes 3145736 | tf_op jit(solution)/shard_map/ppermute | solution.py:45
  30.4 27.4 %collective-permute-start = (bf16[256,2048]{1,0:T(8,128)(2,1)S(1)}, bf16[256,2048]{1,0:T(8,128)(2,1)}, u32[]{:S(2)}, u32[]{:S(2)}) collective-permute-start(bf16[256,2048]{1,0:T(8,128)(2,1)S(1)} %copy-done.2), channel_id=1, source_target_pairs={{0,8},{4,12},{8,0},{12,4},{16,24},{20,28},{24,16},{28,20},{1,9},{5... | collective-permute-start | bytes 3145736 | tf_op jit(solution)/shard_map/ppermute | solution.py:45
  31.0 53.7 %collective-permute-start.4 = (bf16[256,2048]{1,0:T(8,128)(2,1)S(1)}, bf16[256,2048]{1,0:T(8,128)(2,1)}, u32[]{:S(2)}, u32[]{:S(2)}) collective-permute-start(bf16[256,2048]{1,0:T(8,128)(2,1)S(1)} %copy-done.2), channel_id=1, source_target_pairs={{0,4},{4,0},{8,12},{12,8},{16,20},{20,16},{24,28},{28,24},{1,5},{5... | collective-permute-start | bytes 3145736 | tf_op jit(solution)/shard_map/ppermute | solution.py:45
  36.0 91.7 %all-to-all-start.1 = ((bf16[8,2,64,768]{3,2,1,0:T(8,128)(2,1)}), bf16[8,2,64,768]{3,2,1,0:T(8,128)(2,1)}, u32[]{:S(2)}, u32[]{:S(2)}) async-start(bf16[8,2,64,768]{3,2,1,0:T(8,128)(2,1)} %copy.213), calls=%async_computation.1 | async-start | bytes 3145728 | tf_op jit(solution)/shard_map/all_to_all | solution.py:626
  40.5 182.3 %all-gather.13.cloned.1.call-start = ((), (), s32[]{:S(2)}) async-start(), calls=%async_computation.10 | async-start | bytes 1638400 | tf_op jit(solution)/shard_map/all_gather | solution.py:633
  41.3 201.7 %all-gather.21.cloned.1.call-start = ((), (), s32[]{:S(2)}) async-start(), calls=%async_computation.19 | async-start | bytes 3932160 | tf_op jit(solution)/shard_map/all_gather | solution.py:629
  56.0 26.6 %collective-permute-start.2 = (bf16[128,2048]{1,0:T(8,128)(2,1)S(1)}, bf16[128,2048]{1,0:T(8,128)(2,1)}, u32[]{:S(2)}, u32[]{:S(2)}) collective-permute-start(bf16[128,2048]{1,0:T(8,128)(2,1)S(1)} %slice.353), channel_id=1, source_target_pairs={{0,8},{4,12},{8,0},{12,4},{16,24},{20,28},{24,16},{28,20},{1,9},{5... | collective-permute-start | bytes 1572872 | tf_op jit(solution)/shard_map/ppermute | solution.py:45
  58.9 23.7 %collective-permute-start.3 = (bf16[128,2048]{1,0:T(8,128)(2,1)S(1)}, bf16[128,2048]{1,0:T(8,128)(2,1)}, u32[]{:S(2)}, u32[]{:S(2)}) collective-permute-start(bf16[128,2048]{1,0:T(8,128)(2,1)S(1)} %slice.354), channel_id=1, source_target_pairs={{0,16},{4,20},{8,24},{12,28},{16,0},{20,4},{24,8},{28,12},{1,17},{... | collective-permute-start | bytes 1572872 | tf_op jit(solution)/shard_map/ppermute | solution.py:45
  59.8 26.5 %collective-permute-start.5 = (bf16[256,2048]{1,0:T(8,128)(2,1)}, bf16[256,2048]{1,0:T(8,128)(2,1)}, u32[]{:S(2)}, u32[]{:S(2)}) collective-permute-start(bf16[256,2048]{1,0:T(8,128)(2,1)} %collective-permute-done.refs_1_), channel_id=1, source_target_pairs={{0,4},{4,0},{8,12},{12,8},{16,20},{20,16},{24,28},{28,24},{1,5},{5... | collective-permute-start | bytes 3145736 | tf_op jit(solution)/shard_map/ppermute | solution.py:45
  59.9 26.4 %collective-permute-start.6 = (bf16[256,2048]{1,0:T(8,128)(2,1)S(1)}, bf16[256,2048]{1,0:T(8,128)(2,1)}, u32[]{:S(2)}, u32[]{:S(2)}) collective-permute-start(bf16[256,2048]{1,0:T(8,128)(2,1)S(1)} %collective-permute-done.1.refs_2_), channel_id=1, source_target_pairs={{0,4},{4,0},{8,12},{12,8},{16,20},{20,16},{24,28},{28,24},{1,5},{5... | collective-permute-start | bytes 3145736 | tf_op jit(solution)/shard_map/ppermute | solution.py:45
  130.4 184.5 %all-gather.23.cloned.1.call-start = ((), (), s32[]{:S(2)}) async-start(), calls=%async_computation.20 | async-start | bytes 3932160 | tf_op jit(solution)/shard_map/all_gather | solution.py:629
  131.2 25.5 %collective-permute-start.16 = (bf16[256,2048]{1,0:T(8,128)(2,1)S(1)}, bf16[256,2048]{1,0:T(8,128)(2,1)S(1)}, u32[]{:S(2)}, u32[]{:S(2)}) collective-permute-start(bf16[256,2048]{1,0:T(8,128)(2,1)S(1)} %fusion.23.refs_0_), channel_id=1, source_target_pairs={{0,16},{4,20},{8,24},{12,28},{16,0},{20,4},{24,8},{28,12},{1,17},{... | collective-permute-start | bytes 3145736 | tf_op jit(solution)/shard_map/ppermute | solution.py:45
  132.7 26.3 %collective-permute-start.15 = (bf16[256,2048]{1,0:T(8,128)(2,1)S(1)}, bf16[256,2048]{1,0:T(8,128)(2,1)}, u32[]{:S(2)}, u32[]{:S(2)}) collective-permute-start(bf16[256,2048]{1,0:T(8,128)(2,1)S(1)} %fusion.23.refs_0_), channel_id=1, source_target_pairs={{0,8},{4,12},{8,0},{12,4},{16,24},{20,28},{24,16},{28,20},{1,9},{5... | collective-permute-start | bytes 3145736 | tf_op jit(solution)/shard_map/ppermute | solution.py:45
  157.6 55.9 %collective-permute-start.17 = (bf16[128,2048]{1,0:T(8,128)(2,1)}, bf16[128,2048]{1,0:T(8,128)(2,1)}, u32[]{:S(2)}, u32[]{:S(2)}) collective-permute-start(bf16[128,2048]{1,0:T(8,128)(2,1)} %slice.364), channel_id=1, source_target_pairs={{0,8},{4,12},{8,0},{12,4},{16,24},{20,28},{24,16},{28,20},{1,9},{5... | collective-permute-start | bytes 1572872 | tf_op jit(solution)/shard_map/ppermute | solution.py:45
  160.9 53.2 %collective-permute-start.18 = (bf16[128,2048]{1,0:T(8,128)(2,1)}, bf16[128,2048]{1,0:T(8,128)(2,1)}, u32[]{:S(2)}, u32[]{:S(2)}) collective-permute-start(bf16[128,2048]{1,0:T(8,128)(2,1)} %slice.365), channel_id=1, source_target_pairs={{0,16},{4,20},{8,24},{12,28},{16,0},{20,4},{24,8},{28,12},{1,17},{... | collective-permute-start | bytes 1572872 | tf_op jit(solution)/shard_map/ppermute | solution.py:45
  251.9 175.2 %all-gather.15.cloned.1.call-start = ((), (), s32[]{:S(2)}) async-start(), calls=%async_computation.11 | async-start | bytes 3932160 | tf_op jit(solution)/shard_map/all_gather | solution.py:633
  267.2 24.0 %collective-permute-start.25 = (bf16[128,2048]{1,0:T(8,128)(2,1)S(1)}, bf16[128,2048]{1,0:T(8,128)(2,1)S(1)}, u32[]{:S(2)}, u32[]{:S(2)}) collective-permute-start(bf16[128,2048]{1,0:T(8,128)(2,1)S(1)} %get-tuple-element.243), channel_id=1, source_target_pairs={{0,8},{4,12},{8,0},{12,4},{16,24},{20,28},{24,16},{28,20},{1,9},{5... | collective-permute-start | bytes 1572872 | tf_op jit(solution)/shard_map/ppermute | solution.py:45
  267.7 23.4 %collective-permute-start.28 = (bf16[128,2048]{1,0:T(8,128)(2,1)S(1)}, bf16[128,2048]{1,0:T(8,128)(2,1)S(1)}, u32[]{:S(2)}, u32[]{:S(2)}) collective-permute-start(bf16[128,2048]{1,0:T(8,128)(2,1)S(1)} %get-tuple-element.245), channel_id=1, source_target_pairs={{0,16},{4,20},{8,24},{12,28},{16,0},{20,4},{24,8},{28,12},{1,17},{... | collective-permute-start | bytes 1572872 | tf_op jit(solution)/shard_map/ppermute | solution.py:45
  282.1 36.7 %collective-permute-start.30 = (bf16[128,2048]{1,0:T(8,128)(2,1)}, bf16[128,2048]{1,0:T(8,128)(2,1)}, u32[]{:S(2)}, u32[]{:S(2)}) collective-permute-start(bf16[128,2048]{1,0:T(8,128)(2,1)} %get-tuple-element.244), channel_id=1, source_target_pairs={{0,16},{4,20},{8,24},{12,28},{16,0},{20,4},{24,8},{28,12},{1,17},{... | collective-permute-start | bytes 1572872 | tf_op jit(solution)/shard_map/ppermute | solution.py:45
  296.7 22.1 %collective-permute-start.29 = (bf16[128,2048]{1,0:T(8,128)(2,1)}, bf16[128,2048]{1,0:T(8,128)(2,1)}, u32[]{:S(2)}, u32[]{:S(2)}) collective-permute-start(bf16[128,2048]{1,0:T(8,128)(2,1)} %get-tuple-element.230), channel_id=1, source_target_pairs={{0,8},{4,12},{8,0},{12,4},{16,24},{20,28},{24,16},{28,20},{1,9},{5... | collective-permute-start | bytes 1572872 | tf_op jit(solution)/shard_map/ppermute | solution.py:45
  322.7 25.0 %collective-permute-start.32 = (bf16[256,2048]{1,0:T(8,128)(2,1)S(1)}, bf16[256,2048]{1,0:T(8,128)(2,1)}, u32[]{:S(2)}, u32[]{:S(2)}) collective-permute-start(bf16[256,2048]{1,0:T(8,128)(2,1)S(1)} %multiply_convert_fusion.1.refs_0_), channel_id=1, source_target_pairs={{0,16},{4,20},{8,24},{12,28},{16,0},{20,4},{24,8},{28,12},{1,17},{... | collective-permute-start | bytes 3145736 | tf_op jit(solution)/shard_map/ppermute | solution.py:45
  324.2 26.1 %collective-permute-start.31 = (bf16[256,2048]{1,0:T(8,128)(2,1)S(1)}, bf16[256,2048]{1,0:T(8,128)(2,1)}, u32[]{:S(2)}, u32[]{:S(2)}) collective-permute-start(bf16[256,2048]{1,0:T(8,128)(2,1)S(1)} %multiply_convert_fusion.1.refs_0_), channel_id=1, source_target_pairs={{0,8},{4,12},{8,0},{12,4},{16,24},{20,28},{24,16},{28,20},{1,9},{5... | collective-permute-start | bytes 3145736 | tf_op jit(solution)/shard_map/ppermute | solution.py:45
  325.7 49.0 %collective-permute-start.35 = (bf16[256,2048]{1,0:T(8,128)(2,1)S(1)}, bf16[256,2048]{1,0:T(8,128)(2,1)}, u32[]{:S(2)}, u32[]{:S(2)}) collective-permute-start(bf16[256,2048]{1,0:T(8,128)(2,1)S(1)} %multiply_convert_fusion.1.refs_0_), channel_id=1, source_target_pairs={{0,4},{4,0},{8,12},{12,8},{16,20},{20,16},{24,28},{28,24},{1,5},{5... | collective-permute-start | bytes 3145736 | tf_op jit(solution)/shard_map/ppermute | solution.py:45
  365.1 167.7 %reduce-scatter.6.cloned.1.call-start = ((), (), s32[]{:S(2)}) async-start(), calls=%async_computation.12 | async-start | bytes 3932160 | tf_op jit(solution)/shard_map/reduce_scatter | solution.py:752
  474.6 207.2 %reduce-scatter.8.cloned.1.call-start = ((), (), s32[]{:S(2)}) async-start(), calls=%async_computation.13 | async-start | bytes 7864320 | tf_op jit(solution)/shard_map/reduce_scatter | solution.py:752
  474.7 28.0 %collective-permute-start.41 = (bf16[128,2048]{1,0:T(8,128)(2,1)S(1)}, bf16[128,2048]{1,0:T(8,128)(2,1)S(1)}, u32[]{:S(2)}, u32[]{:S(2)}) collective-permute-start(bf16[128,2048]{1,0:T(8,128)(2,1)S(1)} %get-tuple-element.239), channel_id=1, source_target_pairs={{0,8},{4,12},{8,0},{12,4},{16,24},{20,28},{24,16},{28,20},{1,9},{5... | collective-permute-start | bytes 1572872 | tf_op jit(solution)/shard_map/ppermute | solution.py:45
  475.3 27.4 %collective-permute-start.44 = (bf16[128,2048]{1,0:T(8,128)(2,1)S(1)}, bf16[128,2048]{1,0:T(8,128)(2,1)S(1)}, u32[]{:S(2)}, u32[]{:S(2)}) collective-permute-start(bf16[128,2048]{1,0:T(8,128)(2,1)S(1)} %get-tuple-element.241), channel_id=1, source_target_pairs={{0,16},{4,20},{8,24},{12,28},{16,0},{20,4},{24,8},{28,12},{1,17},{... | collective-permute-start | bytes 1572872 | tf_op jit(solution)/shard_map/ppermute | solution.py:45
  532.8 175.1 %reduce-scatter.10.cloned.1.call-start = ((), (), s32[]{:S(2)}) async-start(), calls=%async_computation.14 | async-start | bytes 1638400 | tf_op jit(solution)/shard_map/reduce_scatter | solution.py:752
  539.1 24.7 %collective-permute-start.48 = (bf16[256,2048]{1,0:T(8,128)(2,1)S(1)}, bf16[256,2048]{1,0:T(8,128)(2,1)S(1)}, u32[]{:S(2)}, u32[]{:S(2)}) collective-permute-start(bf16[256,2048]{1,0:T(8,128)(2,1)S(1)} %get-tuple-element.217.refs_0_), channel_id=1, source_target_pairs={{0,16},{4,20},{8,24},{12,28},{16,0},{20,4},{24,8},{28,12},{1,17},{... | collective-permute-start | bytes 3145736 | tf_op jit(solution)/shard_map/ppermute | solution.py:45
  540.6 24.8 %collective-permute-start.47 = (bf16[256,2048]{1,0:T(8,128)(2,1)S(1)}, bf16[256,2048]{1,0:T(8,128)(2,1)S(1)}, u32[]{:S(2)}, u32[]{:S(2)}) collective-permute-start(bf16[256,2048]{1,0:T(8,128)(2,1)S(1)} %get-tuple-element.217.refs_0_), channel_id=1, source_target_pairs={{0,8},{4,12},{8,0},{12,4},{16,24},{20,28},{24,16},{28,20},{1,9},{5... | collective-permute-start | bytes 3145736 | tf_op jit(solution)/shard_map/ppermute | solution.py:45
  603.6 27.6 %collective-permute-start.64 = (bf16[128,2048]{1,0:T(8,128)(2,1)S(1)}, bf16[128,2048]{1,0:T(8,128)(2,1)S(1)}, u32[]{:S(2)}, u32[]{:S(2)}) collective-permute-start(bf16[128,2048]{1,0:T(8,128)(2,1)S(1)} %get-tuple-element.238), channel_id=1, source_target_pairs={{0,8},{4,12},{8,0},{12,4},{16,24},{20,28},{24,16},{28,20},{1,9},{5... | collective-permute-start | bytes 1572872 | tf_op jit(solution)/shard_map/ppermute | solution.py:45
  604.6 28.2 %collective-permute-start.66 = (bf16[128,2048]{1,0:T(8,128)(2,1)S(1)}, bf16[128,2048]{1,0:T(8,128)(2,1)S(1)}, u32[]{:S(2)}, u32[]{:S(2)}) collective-permute-start(bf16[128,2048]{1,0:T(8,128)(2,1)S(1)} %get-tuple-element.237), channel_id=1, source_target_pairs={{0,16},{4,20},{8,24},{12,28},{16,0},{20,4},{24,8},{28,12},{1,17},{... | collective-permute-start | bytes 1572872 | tf_op jit(solution)/shard_map/ppermute | solution.py:45
  631.3 45.0 %collective-permute-start.63 = (bf16[128,2048]{1,0:T(8,128)(2,1)}, bf16[128,2048]{1,0:T(8,128)(2,1)}, u32[]{:S(2)}, u32[]{:S(2)}) collective-permute-start(bf16[128,2048]{1,0:T(8,128)(2,1)} %get-tuple-element.235), channel_id=1, source_target_pairs={{0,8},{4,12},{8,0},{12,4},{16,24},{20,28},{24,16},{28,20},{1,9},{5... | collective-permute-start | bytes 1572872 | tf_op jit(solution)/shard_map/ppermute | solution.py:45
  632.9 43.4 %collective-permute-start.68 = (bf16[128,2048]{1,0:T(8,128)(2,1)}, bf16[128,2048]{1,0:T(8,128)(2,1)}, u32[]{:S(2)}, u32[]{:S(2)}) collective-permute-start(bf16[128,2048]{1,0:T(8,128)(2,1)} %get-tuple-element.236), channel_id=1, source_target_pairs={{0,16},{4,20},{8,24},{12,28},{16,0},{20,4},{24,8},{28,12},{1,17},{... | collective-permute-start | bytes 1572872 | tf_op jit(solution)/shard_map/ppermute | solution.py:45
  636.2 40.0 %collective-permute-start.65 = (bf16[128,2048]{1,0:T(8,128)(2,1)}, bf16[128,2048]{1,0:T(8,128)(2,1)}, u32[]{:S(2)}, u32[]{:S(2)}) collective-permute-start(bf16[128,2048]{1,0:T(8,128)(2,1)} %get-tuple-element.225), channel_id=1, source_target_pairs={{0,16},{4,20},{8,24},{12,28},{16,0},{20,4},{24,8},{28,12},{1,17},{... | collective-permute-start | bytes 1572872 | tf_op jit(solution)/shard_map/ppermute | solution.py:45
  637.7 38.5 %collective-permute-start.67 = (bf16[128,2048]{1,0:T(8,128)(2,1)}, bf16[128,2048]{1,0:T(8,128)(2,1)}, u32[]{:S(2)}, u32[]{:S(2)}) collective-permute-start(bf16[128,2048]{1,0:T(8,128)(2,1)} %get-tuple-element.226), channel_id=1, source_target_pairs={{0,8},{4,12},{8,0},{12,4},{16,24},{20,28},{24,16},{28,20},{1,9},{5... | collective-permute-start | bytes 1572872 | tf_op jit(solution)/shard_map/ppermute | solution.py:45
  645.9 119.0 %reduce-scatter.14.cloned.1.call-start = ((), (), s32[]{:S(2)}) async-start(), calls=%async_computation.16 | async-start | bytes 1966080 | tf_op jit(solution)/shard_map/reduce_scatter | solution.py:752
  681.9 23.9 %collective-permute-start.59 = (bf16[48,320]{1,0:T(8,128)(2,1)S(1)}, bf16[48,320]{1,0:T(8,128)(2,1)S(1)}, u32[]{:S(2)}, u32[]{:S(2)}) collective-permute-start(bf16[48,320]{1,0:T(8,128)(2,1)S(1)} %reshape.362), channel_id=1, source_target_pairs={{0,1},{1,0},{2,3},{3,2},{4,5},{5,4},{6,7},{7,6},{8,9},{9,8},{10,11... | collective-permute-start | bytes 92168 | tf_op jit(solution)/shard_map/ppermute | solution.py:45
  683.3 22.5 %collective-permute-start.60 = (bf16[48,320]{1,0:T(8,128)(2,1)S(1)}, bf16[48,320]{1,0:T(8,128)(2,1)S(1)}, u32[]{:S(2)}, u32[]{:S(2)}) collective-permute-start(bf16[48,320]{1,0:T(8,128)(2,1)S(1)} %reshape.362), channel_id=1, source_target_pairs={{0,2},{1,3},{2,0},{3,1},{4,6},{5,7},{6,4},{7,5},{8,10},{9,11},{10,... | collective-permute-start | bytes 92168 | tf_op jit(solution)/shard_map/ppermute | solution.py:45
  716.1 52.7 %collective-permute-start.69 = (bf16[1024,2048]{1,0:T(8,128)(2,1)}, bf16[1024,2048]{1,0:T(8,128)(2,1)}, u32[]{:S(2)}, u32[]{:S(2)}) collective-permute-start(bf16[1024,2048]{1,0:T(8,128)(2,1)} %add_convert_fusion), channel_id=1, source_target_pairs={{0,4},{4,0},{8,12},{12,8},{16,20},{20,16},{24,28},{28,24},{1,5},{5... | collective-permute-start | bytes 12582920 | tf_op jit(solution)/shard_map/ppermute | solution.py:45
  731.8 25.4 %all-to-all-start.4 = ((bf16[8,2,64,768]{3,2,1,0:T(8,128)(2,1)}), bf16[8,2,64,768]{3,2,1,0:T(8,128)(2,1)}, u32[]{:S(2)}, u32[]{:S(2)}) async-start(bf16[8,2,64,768]{3,2,1,0:T(8,128)(2,1)} %bitcast.234), calls=%async_computation.9 | async-start | bytes 3145728 | tf_op jit(solution)/shard_map/all_to_all | solution.py:626
  736.1 70.0 %reduce-scatter.12.cloned.1.call-start = ((), (), s32[]{:S(2)}) async-start(), calls=%async_computation.15 | async-start | bytes 2334720 | tf_op jit(solution)/shard_map/reduce_scatter | solution.py:752
  781.2 28.6 %collective-permute-start.71 = (bf16[128,2048]{1,0:T(8,128)(2,1)}, bf16[128,2048]{1,0:T(8,128)(2,1)}, u32[]{:S(2)}, u32[]{:S(2)}) collective-permute-start(bf16[128,2048]{1,0:T(8,128)(2,1)} %get-tuple-element.234), channel_id=1, source_target_pairs={{0,8},{4,12},{8,0},{12,4},{16,24},{20,28},{24,16},{28,20},{1,9},{5... | collective-permute-start | bytes 1572872 | tf_op jit(solution)/shard_map/ppermute | solution.py:45
  812.1 24.7 %collective-permute-start.72 = (bf16[128,2048]{1,0:T(8,128)(2,1)}, bf16[128,2048]{1,0:T(8,128)(2,1)}, u32[]{:S(2)}, u32[]{:S(2)}) collective-permute-start(bf16[128,2048]{1,0:T(8,128)(2,1)} %fusion.37), channel_id=1, source_target_pairs={{0,16},{4,20},{8,24},{12,28},{16,0},{20,4},{24,8},{28,12},{1,17},{... | collective-permute-start | bytes 1572872 | tf_op jit(solution)/shard_map/ppermute | solution.py:45
  815.5 25.0 %all-to-all-start.2 = ((bf16[8,64,320]{2,1,0:T(8,128)(2,1)}), bf16[8,64,320]{2,1,0:T(8,128)(2,1)}, u32[]{:S(2)}, u32[]{:S(2)}) async-start(bf16[8,64,320]{2,1,0:T(8,128)(2,1)} %bitcast.72), calls=%async_computation.6 | async-start | bytes 786432 | tf_op jit(solution)/shard_map/all_to_all | solution.py:626
  821.2 27.3 %collective-permute-start.75 = (bf16[128,2048]{1,0:T(8,128)(2,1)}, bf16[128,2048]{1,0:T(8,128)(2,1)}, u32[]{:S(2)}, u32[]{:S(2)}) collective-permute-start(bf16[128,2048]{1,0:T(8,128)(2,1)} %get-tuple-element.232), channel_id=1, source_target_pairs={{0,16},{4,20},{8,24},{12,28},{16,0},{20,4},{24,8},{28,12},{1,17},{... | collective-permute-start | bytes 1572872 | tf_op jit(solution)/shard_map/ppermute | solution.py:45
  (149 other events, 1664.4 us)
Sparse Core Ops, SparseCore 0:
  29.2 36.4 all-gather.16
  67.8 39.8 all-gather.18
  109.3 31.5 all-gather.12
  142.9 69.5 all-gather.20
  252.0 62.8 all-gather.22
  365.2 61.8 all-gather.14
  474.7 58.0 reduce-scatter.5
  535.1 112.3 reduce-scatter.7
  649.8 31.7 reduce-scatter.9
  728.9 35.9 reduce-scatter.13
  767.2 38.8 reduce-scatter.11

commit v2 on v1

--- a/solution.py
+++ b/solution.py
@@ -14,6 +14,7 @@
 VMEM_LIMIT = 48 * 1024 * 1024
 GELU_C = 0.7978845608028654
 GELU_A = 0.044715
+LIGHT = pl.CostEstimate(flops=1, transcendentals=0, bytes_accessed=1)
 
 
 def as_low(values):
@@ -45,44 +46,110 @@
     return lax.ppermute(values, axis, [(i, i ^ flip) for i in range(count)])
 
 
-def gather_plane(own):
+barrier = lax.optimization_barrier
+
+
+def plane_even(own):
+    return [own] + [swap(own, "seq", k) for k in range(2, lax.axis_size("seq"), 2)]
+
+
+def plane_first(own):
     count = lax.axis_size("seq")
-    if count == 8:
+    flips = (2, 4) if count == 8 else range(2, count, 2)
+    return [swap(own, "seq", k) for k in flips]
+
+
+def plane_second(own, first):
+    even = [own, *first]
+    if lax.axis_size("seq") == 8:
         half = own.shape[0] // 2
-        near, side = swap(own, "seq", 2), swap(own, "seq", 4)
-        far = (swap(side[:half], "seq", 2), swap(near[half:], "seq", 4))
-        even = [(own,), (near,), (side,), far]
-    else:
-        even = [(own,)] + [(swap(own, "seq", k),) for k in range(2, count, 2)]
-    odd = [tuple(swap(part, "seq", 1) for part in slot) for slot in even]
-    return even + odd
-
-
-def scatter_plane(product, hold=lambda value: value):
-    count = lax.axis_size("seq")
-    other = swap(hold(as_low(product(True))), "seq", 1)
-    pair = product(False) + as_wide(other)
-    rows = pair.shape[0] // (count // 2)
-    if count != 8:
-        total = pair[:rows]
-        for index, k in enumerate(range(2, count, 2), start=1):
-            total = total + as_wide(swap(as_low(pair[index * rows : (index + 1) * rows]), "seq", k))
-        return total
-    half = rows // 2
-
-    def part(slot, lower):
-        start = slot * rows + (half if lower else 0)
-        return pair[start : start + half]
-
-    far_top = swap(as_low(part(3, False)), "seq", 2)
-    far_low = swap(as_low(part(3, True)), "seq", 4)
-    near_top = swap(as_low(part(1, False)), "seq", 2)
-    side_low = swap(as_low(part(2, True)), "seq", 4)
-    near_low = swap(as_low(part(1, True) + as_wide(far_low)), "seq", 2)
-    side_top = swap(as_low(part(2, False) + as_wide(far_top)), "seq", 4)
-    top = part(0, False) + as_wide(near_top) + as_wide(side_top)
-    low = part(0, True) + as_wide(near_low) + as_wide(side_low)
-    return jnp.concatenate([top, low], axis=0)
+        near, side = first
+        even.append((swap(side[:half], "seq", 2), swap(near[half:], "seq", 4)))
+    return even
+
+
+def plane_all(even):
+    return list(even) + [jax.tree.map(lambda part: swap(part, "seq", 1), piece) for piece in even]
+
+
+def slot_order():
+    evens = lax.axis_size("seq") // 2
+    return sorted(range(1, evens), key=lambda slot: -bin(slot).count("1")) + [0]
+
+
+def scatter_plane(product):
+    evens = lax.axis_size("seq") // 2
+    order = slot_order()
+    ready, pairs, after = {}, {}, None
+
+    def odd(slot):
+        value = as_low(product(evens + slot, after))
+        ready[slot] = swap(value, "seq", 1)
+        return value
+
+    after = odd(order[0])
+    for index, slot in enumerate(order):
+        if index + 1 < evens:
+            after = odd(order[index + 1])
+        after = product(slot, after) + as_wide(ready[slot])
+        pairs[slot] = after
+    if evens != 4:
+        return [swap(as_low(pairs[slot]), "seq", 2 * slot) if slot else after for slot in order], after
+    own, near, side, far = (pairs[slot] for slot in range(4))
+    half = far.shape[0] // 2
+    far_top = swap(as_low(far[:half]), "seq", 2)
+    far_low = swap(as_low(far[half:]), "seq", 4)
+    near_top = swap(as_low(near[:half]), "seq", 2)
+    side_low = swap(as_low(side[half:]), "seq", 4)
+    near_low = swap(as_low(near[half:] + as_wide(far_low)), "seq", 2)
+    side_top = swap(as_low(side[:half] + as_wide(far_top)), "seq", 4)
+    return [own, (near_top, near_low), (side_top, side_low)], own
+
+
+def split_pairs(pair):
+    rows = pair.shape[0] // (lax.axis_size("seq") // 2)
+    parts = [pair[slot * rows : (slot + 1) * rows] for slot in slot_order()]
+    return [as_low(part) for part in parts[:-1]] + parts[-1:]
+
+
+def scatter_pairs(parts):
+    return [
+        swap(part, "seq", 2 * slot) if slot else part for slot, part in zip(slot_order(), parts)
+    ]
+
+
+def slot_product(operands, multiply):
+    rows = operands[0].shape[0] // lax.axis_size("seq")
+
+    def product(slot, after):
+        parts = tuple(operand[slot * rows : (slot + 1) * rows] for operand in operands)
+        if after is not None:
+            parts = barrier((*parts, after))[:-1]
+        return multiply(*parts)
+
+    return product
+
+
+def summed(parts):
+    total = None
+    for part in parts:
+        if isinstance(part, (tuple, list)):
+            part = jnp.concatenate(part, axis=0)
+        total = as_wide(part) if total is None else total + as_wide(part)
+    return total
+
+
+def gather_small(value, axis):
+    value = value[None]
+    bit = 1
+    while bit < lax.axis_size(axis):
+        other = swap(value, axis, bit)
+        upper = (lax.axis_index(axis) // bit) % 2 == 1
+        value = jnp.where(
+            upper, jnp.concatenate([other, value]), jnp.concatenate([value, other])
+        )
+        bit *= 2
+    return value
 
 
 def spread_z(value):
@@ -117,45 +184,44 @@
     return [(low, min(LANES, width - low)) for low in range(0, width, LANES)]
 
 
-def stack_step(refs, slots):
-    step = pl.program_id(0)
-    steps = pl.num_programs(0)
+def piece_specs(pieces, steps):
+    specs = []
+    chunk = pieces[0].shape[0] // steps
+    block = (chunk, pieces[0].shape[1])
+    last = steps // 2 - 1
+    for piece in pieces:
+        if isinstance(piece, (tuple, list)):
+            specs.append(pl.BlockSpec(block, lambda i: (jnp.minimum(i, last), 0)))
+            specs.append(pl.BlockSpec(block, lambda i: (jnp.maximum(i - last - 1, 0), 0)))
+        else:
+            specs.append(pl.BlockSpec(block, lambda i: (i, 0)))
+    return specs
+
+
+def piece_halves(pieces):
+    return [len(piece) if isinstance(piece, (tuple, list)) else 1 for piece in pieces]
+
+
+def joined_rows(refs, halves):
+    upper = pl.program_id(0) < pl.num_programs(0) // 2
     rows, at = [], 0
-    for parts in slots:
-        if parts == 1:
-            rows.append(refs[at][...])
-        else:
-            rows.append(jnp.where(step < steps // 2, refs[at][...], refs[at + 1][...]))
+    for parts in halves:
+        value = refs[at][...]
+        rows.append(value if parts == 1 else jnp.where(upper, value, refs[at + 1][...]))
         at += parts
     return jnp.concatenate(rows, axis=0)
 
 
-def slot_specs(pieces, steps):
-    specs = []
-    for slot in pieces:
-        chunk = sum(part.shape[0] for part in slot) // steps
-        model = slot[0].shape[1]
-        if len(slot) == 1:
-            specs.append(pl.BlockSpec((chunk, model), lambda i: (i, 0)))
-        else:
-            last = steps // 2 - 1
-            specs.append(pl.BlockSpec((chunk, model), lambda i, last=last: (jnp.minimum(i, last), 0)))
-            specs.append(pl.BlockSpec((chunk, model), lambda i, last=last: (jnp.maximum(i - last - 1, 0), 0)))
-    return specs
-
-
-def stack(pieces, name, gain=None, weights=(), steps=8):
-    slots = tuple(len(slot) for slot in pieces)
+def stack(pieces, name, gain=None, weights=(), gated=False, steps=8):
     count = len(pieces)
-    flat = [part for slot in pieces for part in slot]
-    rows = sum(part.shape[0] for part in pieces[0])
-    model = flat[0].shape[1]
+    halves, flat = piece_halves(pieces), jax.tree.leaves(pieces)
+    rows, model = pieces[0].shape
     chunk = rows // steps
     extra = ([gain] if gain is not None else []) + list(weights)
 
     def kernel(*refs):
-        pieces_in, refs = refs[: len(flat)], refs[len(flat) :]
-        values = stack_step(pieces_in, slots)
+        values = joined_rows(refs[: len(flat)], halves)
+        refs = refs[len(flat) :]
         if gain is not None:
             gain_ref, refs = refs[0], refs[1:]
             wide = values.astype(jnp.float32)
@@ -163,22 +229,87 @@
             values = (wide * scale * gain_ref[...]).astype(jnp.bfloat16)
         weight_refs, refs = refs[: len(weights)], refs[len(weights) :]
         refs[0][...] = values.reshape(count, chunk, model)
+        products = []
         for weight_ref, out_ref in zip(weight_refs, refs[1:]):
             out = jnp.dot(values, weight_ref[...], preferred_element_type=jnp.float32)
             out_ref[...] = out.reshape(count, chunk, out.shape[1])
+            products.append(out)
+        if gated:
+            out = (gelu_parts(products[0])[0] * products[1]).astype(jnp.bfloat16)
+            refs[-1][...] = out.reshape(count, chunk, out.shape[1])
 
     widths = [weight.shape[1] for weight in weights]
     outs = [shaped((count, rows, model), jnp.bfloat16)] + [shaped((count, rows, w)) for w in widths]
+    if gated:
+        outs.append(shaped((count, rows, widths[0]), jnp.bfloat16))
     done = pl.pallas_call(
         kernel,
         grid=(steps,),
-        in_specs=slot_specs(pieces, steps) + [pl.BlockSpec(e.shape, lambda i: (0, 0)) for e in extra],
-        out_specs=[pl.BlockSpec((count, chunk, w), lambda i: (0, i, 0)) for w in [model] + widths],
+        in_specs=piece_specs(pieces, steps) + [pl.BlockSpec(e.shape, lambda i: (0, 0)) for e in extra],
+        out_specs=[pl.BlockSpec((count, chunk, o.shape[2]), lambda i: (0, i, 0)) for o in outs],
         out_shape=outs,
         compiler_params=pltpu.CompilerParams(vmem_limit_bytes=VMEM_LIMIT),
+        cost_estimate=LIGHT,
         name=name,
     )(*flat, *extra)
     return [out.reshape(count * rows, out.shape[2]) for out in done]
+
+
+def ff_backward(top, down_w, gate_pre, up_pre, steps=8):
+    chunk = top.shape[0] // steps
+    ffw, model = down_w.shape
+
+    def kernel(top_ref, down_ref, gate_ref, up_ref, d_gate_ref, d_up_ref):
+        grad = lax.dot_general(
+            top_ref[...], down_ref[...], (((1,), (1,)), ((), ())), preferred_element_type=jnp.float32
+        )
+        gate = gate_ref[...]
+        act, bend = gelu_parts(gate)
+        d_gate_ref[...] = (grad * up_ref[...] * gelu_slope(gate, bend)).astype(jnp.bfloat16)
+        d_up_ref[...] = (grad * act).astype(jnp.bfloat16)
+
+    block = pl.BlockSpec((chunk, ffw), lambda i: (i, 0))
+    return pl.pallas_call(
+        kernel,
+        grid=(steps,),
+        in_specs=[
+            pl.BlockSpec((chunk, model), lambda i: (i, 0)),
+            pl.BlockSpec((ffw, model), lambda i: (0, 0)),
+            block,
+            block,
+        ],
+        out_specs=[block, block],
+        out_shape=[shaped((top.shape[0], ffw), jnp.bfloat16)] * 2,
+        compiler_params=pltpu.CompilerParams(vmem_limit_bytes=VMEM_LIMIT),
+        cost_estimate=LIGHT,
+        name="ff_backward",
+    )(top, down_w, gate_pre, up_pre)
+
+
+def project(rows, weight, name, steps=8):
+    chunk = rows.shape[0] // steps
+    width = weight.shape[1]
+
+    def kernel(rows_ref, weight_ref, out_ref):
+        out_ref[...] = jnp.dot(rows_ref[...], weight_ref[...], preferred_element_type=jnp.float32)
+
+    return pl.pallas_call(
+        kernel,
+        grid=(steps,),
+        in_specs=[
+            pl.BlockSpec((chunk, rows.shape[1]), lambda i: (i, 0)),
+            pl.BlockSpec(weight.shape, lambda i: (0, 0)),
+        ],
+        out_specs=pl.BlockSpec((chunk, width), lambda i: (i, 0)),
+        out_shape=shaped((rows.shape[0], width)),
+        compiler_params=pltpu.CompilerParams(vmem_limit_bytes=VMEM_LIMIT),
+        cost_estimate=pl.CostEstimate(
+            flops=2 * rows.size * width,
+            transcendentals=0,
+            bytes_accessed=2 * rows.size + 4 * rows.shape[0] * width,
+        ),
+        name=name,
+    )(rows, weight)
 
 
 def dead_mask(rows, live_count):
@@ -308,18 +439,16 @@
 
 
 def lru_back(pieces, out_w, state, branch_pre, keep, steps=8):
-    slots = tuple(len(slot) for slot in pieces)
     count = len(pieces)
-    flat = [part for slot in pieces for part in slot]
-    rows = sum(part.shape[0] for part in pieces[0])
-    model = flat[0].shape[1]
+    halves, flat = piece_halves(pieces), jax.tree.leaves(pieces)
+    rows, model = pieces[0].shape
     width = out_w.shape[0]
     tiles = lane_tiles(width)
     chunk = rows // steps
     blocks = count * rows // BLOCK
 
     def kernel(*refs):
-        values = stack_step(refs[: len(flat)], slots)
+        values = joined_rows(refs[: len(flat)], halves)
         w_ref, h_ref, ypre_ref, keep_ref, out_ref, dy_ref, dh_ref, send_ref = refs[len(flat) :]
         here = pl.program_id(0)
         out_ref[...] = values.reshape(count, chunk, model)
@@ -356,7 +485,7 @@
     out, dy, dh, send = pl.pallas_call(
         kernel,
         grid=(steps,),
-        in_specs=slot_specs(pieces, steps)
+        in_specs=piece_specs(pieces, steps)
         + [
             pl.BlockSpec((width, model), lambda i: (0, 0)),
             pl.BlockSpec((depth, count, chunk, LANES), lambda i: (0, 0, i, 0)),
@@ -376,6 +505,7 @@
             shaped((depth, blocks, LANES)),
         ],
         compiler_params=pltpu.CompilerParams(vmem_limit_bytes=VMEM_LIMIT),
+        cost_estimate=LIGHT,
         name="lru_back",
     )(
         *flat,
@@ -552,6 +682,7 @@
         out_specs=[pl.BlockSpec(memory_space=pltpu.VMEM)] * len(outs),
         scratch_shapes=scratch,
         compiler_params=pltpu.CompilerParams(vmem_limit_bytes=VMEM_LIMIT),
+        cost_estimate=LIGHT,
         name=name,
     )(*scalars, *arrays)
 
@@ -625,65 +756,63 @@
     def exchange(value):
         return lax.all_to_all(value, "seq", 0, 0, tiled=True)
 
+    def gather_rows(value):
+        return lax.all_gather(value, "fsdp", axis=0, tiled=True)
+
     def gather_columns(value):
         got = lax.all_gather(value, "fsdp", axis=0, tiled=False)
         return jnp.swapaxes(got, 0, 1).reshape(-1, value.shape[-1])
 
-    def gather_rows(value):
-        return lax.all_gather(value, "fsdp", axis=0, tiled=True)
-
-    barrier = lax.optimization_barrier
+    gains = gather_small(as_low(jnp.stack([norm_gain1, norm_gain2])), "seq")
+    x_first = plane_first(tokens)
     out_w = gather_rows(as_low(w_out))
     mix = exchange(jnp.stack([columns(w_input), columns(w_branch)], axis=1))
-    x_pieces = gather_plane(tokens)
-    wide_small = jnp.concatenate(
-        [
-            as_low(conv_kernel),
-            as_low(conv_bias)[None],
-            as_low(bias_rec)[None],
-            as_low(bias_in)[None],
-            as_low(decay_param)[None],
-            as_low(jnp.pad(jnp.stack([norm_gain1, norm_gain2]), ((0, 0), (0, width // z_size - chunk)))),
-        ],
-        axis=0,
-    ).T
-    small = jnp.concatenate([as_low(gate_rec), as_low(gate_in), wide_small], axis=1)
-    small, x_pieces = barrier((small, x_pieces))
-    small = lax.all_gather(small, "fsdp", axis=0, tiled=False)
-    gains = lax.all_gather(small[:, :chunk, 2 * gate_width + 8 :], "seq", axis=0, tiled=False)
-    gains = as_wide(gains.reshape(model, 2)).T
+    x_even = plane_second(tokens, x_first)
+    mix, out_w, x_even = barrier((mix, out_w, x_even))
+    input_w = gather_columns(mix[:, 0])
+    branch_w = gather_columns(mix[:, 1])
+    x_pieces = plane_all(x_even)
+    params = [conv_kernel, conv_bias[None], bias_rec[None], bias_in[None], decay_param[None]]
+    gains = jnp.pad(gains.reshape(2 * seq_size, chunk), ((0, 0), (0, width // z_size - chunk)))
+    params = jnp.concatenate([as_low(part) for part in params] + [gains], axis=0).T
+    small = jnp.concatenate([as_low(gate_rec), as_low(gate_in), params], axis=1)
+    small = gather_small(small, "fsdp")
+    gains = small[:, :chunk, 2 * gate_width + 8 :].reshape(z_size, chunk, seq_size, 2)
+    gains = as_wide(jnp.transpose(gains, (3, 2, 0, 1)).reshape(2, model))
     gain_one, gain_two = gains[:1], gains[1:]
     small = small.reshape(width, -1)
-    input_w = gather_columns(mix[:, 0])
-    branch_w = gather_columns(mix[:, 1])
-    ff = exchange(jnp.stack([columns(w_gate), columns(w_up)], axis=1))
-    down_w = gather_rows(as_low(w_down))
 
     same = jnp.arange(width)[:, None] // gate_width == jnp.arange(width)[None, :] // gate_width
 
     def diagonal(part):
         return jnp.where(same, jnp.tile(part, (1, groups)), jnp.zeros((), jnp.bfloat16))
 
-    rec_w = diagonal(small[:, :gate_width])
-    in_w = diagonal(small[:, gate_width : 2 * gate_width])
     vectors = as_wide(small[:, 2 * gate_width : 2 * gate_width + 8]).T
     decay = vectors[7]
     vectors = jnp.concatenate([vectors[:7], -GATE_SCALE * jax.nn.softplus(-decay)[None]], axis=0)
-
-    x_pieces, top_own = barrier((x_pieces, as_low(live_col * as_wide(cotangent))))
+    ff = jnp.stack([columns(w_gate), columns(w_up)], axis=1)
+    top_own = as_low(live_col * as_wide(cotangent))
+    x_pieces, ff, top_own = barrier((x_pieces, ff, top_own))
+    ff = exchange(ff)
+    top_even = plane_even(top_own)
+
     normed_one, u_value = stack(x_pieces, "norm_one", gain_one, (input_w,))
-    normed_one, ff = barrier((normed_one, ff))
-    gate_w = gather_columns(ff[:, 0])
-    up_w = gather_columns(ff[:, 1])
-    top_pieces = gather_plane(top_own)
+    u_value, gates_in = barrier((u_value, small))
+    rec_w = diagonal(gates_in[:, :gate_width])
+    in_w = diagonal(gates_in[:, gate_width : 2 * gate_width])
+    down_w = gather_rows(as_low(w_down))
 
     def edges(rows):
-        rows = spread_z(as_low(rows).reshape(blocks * (TAPS - 1), width))
+        rows = spread_z(as_low(barrier(rows)).reshape(blocks * (TAPS - 1), width))
         rows = as_wide(rows).reshape(every, TAPS - 1, width)
         return jnp.pad(rows, ((0, 0), (9 - TAPS, 0), (0, 0)))
 
     tails = edges(u_value.reshape(blocks, BLOCK, width)[:, BLOCK - TAPS + 1 :])
-    branch_pre = mm(normed_one, branch_w)
+    tails, rec_w, in_w, vectors, ff_gate, ff_up = barrier(
+        (tails, rec_w, in_w, vectors, ff[:, 0], ff[:, 1])
+    )
+    gate_w = gather_columns(ff_gate)
+    up_w = gather_columns(ff_up)
     conv_low, keep, drive, rate, entry, summary = whole(
         lru_forward_kernel,
         (live_count, first, pred),
@@ -699,10 +828,9 @@
         [pltpu.VMEM((BLOCK + 8, LANES), jnp.float32)],
         "lru_forward",
     )
+    branch_pre = project(normed_one, branch_w, "branch_pre")
     summaries = spread_z(summary)
-    summaries, top_pieces, out_w, branch_pre = barrier(
-        (summaries, top_pieces, out_w, branch_pre)
-    )
+    summaries, branch_pre, top_even = barrier((summaries, branch_pre, top_even))
     state, gated, enter = whole(
         lru_state_kernel,
         (position,),
@@ -715,38 +843,28 @@
         [pltpu.VMEM((tiles, every, LANES), jnp.float32)],
         "lru_state",
     )
-    gated, gate_w = barrier((gated, gate_w))
-    half = count // 2
-
-    def side(rows, odd):
-        return rows[half:] if odd else rows[:half]
-
     resid_in = as_wide(tokens)
-    resid_mid = resid_in + scatter_plane(lambda odd: mm(side(gated, odd), out_w))
+    mid_parts, mid_last = scatter_plane(slot_product((gated,), lambda rows: mm(rows, out_w)))
+    top_even, mid_last = barrier((top_even, mid_last))
+    (top_low,) = stack(plane_all(top_even), "stack_top")
+    mid_parts, top_low, gate_w = barrier((mid_parts, top_low, gate_w))
+    resid_mid = resid_in + summed(mid_parts)
     scale_two = lax.rsqrt(jnp.mean(resid_mid * resid_mid, axis=-1, keepdims=True) + NORM_EPSILON)
     own_two = as_low(resid_mid * scale_two * gain_two)
-    own_two, up_w = barrier((own_two, up_w))
-    two_pieces = gather_plane(own_two)
-    (top_low,) = stack(top_pieces, "stack_top")
-    two_pieces, top_low = barrier((two_pieces, top_low))
-    (normed_two,) = stack(two_pieces, "stack_two")
-    gate_pre = mm(normed_two, gate_w)
-    up_pre = mm(normed_two, up_w)
-    act, bend = gelu_parts(gate_pre)
-    hidden = as_low(act * up_pre)
-    grad_down = mm_tn(hidden, top_low, jnp.bfloat16)
-    gate_pre, up_pre, hidden, grad_down, down_w = barrier(
-        (gate_pre, up_pre, hidden, grad_down, down_w)
-    )
-    act, bend = gelu_parts(gate_pre)
-    grad_hidden = mm_nt(top_low, down_w)
-    d_gate = as_low(grad_hidden * up_pre * gelu_slope(gate_pre, bend))
-    d_up = as_low(grad_hidden * act)
-    grad_normed_two = scatter_plane(
-        lambda odd: mm_nt(side(d_gate, odd), gate_w) + mm_nt(side(d_up, odd), up_w)
-    )
-    grad_gate = mm_tn(normed_two, d_gate, jnp.bfloat16)
-    grad_up = mm_tn(normed_two, d_up, jnp.bfloat16)
+    two_first = plane_first(own_two)
+    two_first, up_w = barrier((two_first, up_w))
+    normed_two, gate_pre, up_pre, hidden = stack(
+        plane_all(plane_second(own_two, two_first)), "ff_forward", None, (gate_w, up_w), True
+    )
+    d_gate, d_up = ff_backward(top_low, down_w, gate_pre, up_pre)
+    two_parts, two_last = scatter_plane(
+        slot_product((d_gate, d_up), lambda one, two: mm_nt(one, gate_w) + mm_nt(two, up_w))
+    )
+    late_gate, late_up, late_hidden, two_last = barrier((d_gate, d_up, hidden, two_last))
+    grad_down = mm_tn(late_hidden, top_low, jnp.bfloat16)
+    grad_down, late_gate, late_up = barrier((grad_down, late_gate, late_up))
+    grad_gate = mm_tn(normed_two, late_gate, jnp.bfloat16)
+    grad_up = mm_tn(normed_two, late_up, jnp.bfloat16)
 
     def home_rows(value):
         return lax.psum_scatter(value, "fsdp", scatter_dimension=0, tiled=True)
@@ -760,7 +878,8 @@
 
     down_home = home_rows(grad_down)
     ff_pair = by_owner((grad_gate, grad_up)).reshape(z_size * seq_size * 2 * chunk, ffw)
-    grad_normed_two, ff_pair, down_home = barrier((grad_normed_two, ff_pair, down_home))
+    two_parts, ff_pair = barrier((two_parts, ff_pair))
+    grad_normed_two = summed(two_parts)
     ff_home = home_rows(ff_pair)
 
     def gain_home(gain, pairs):
@@ -777,18 +896,20 @@
         * scale_two
         * jnp.mean(scaled_two * resid_mid, axis=-1, keepdims=True)
     )
-    out_pieces = gather_plane(as_low(grad_mid))
-
-    def after_out(value):
-        return barrier((value, out_pieces))[0]
-
-    mlp_out = scatter_plane(lambda odd: mm(side(hidden, odd), down_w), after_out)
-    mixed = as_low(live_col * (resid_mid + mlp_out))
+    grad_low = as_low(grad_mid)
+    grad_low, late_hidden = barrier((grad_low, hidden))
+    out_first = plane_first(grad_low)
+    half = count // 2
+    mlp_odd = swap(mm(late_hidden[half:], down_w, jnp.bfloat16), "seq", 1)
+    mlp_pair = split_pairs(mm(late_hidden[:half], down_w) + as_wide(mlp_odd))
+    out_first, mlp_pair, down_home = barrier((out_first, mlp_pair, down_home))
+    out_pieces = plane_all(plane_second(grad_low, out_first))
+    out_pieces, mlp_pair = barrier((out_pieces, mlp_pair))
+    mlp_parts = scatter_pairs(mlp_pair)
     grad_out_low, d_branch, direct, send = lru_back(out_pieces, out_w, state, branch_pre, keep)
     backs = spread_z(send)
     grad_out = mm_tn(gated, grad_out_low, jnp.bfloat16)
     backs, grad_out = barrier((backs, grad_out))
-    out_home = home_rows(grad_out)
     d_rec, d_in, du_part, du_last, heads, totals = whole(
         lru_grad_kernel,
         (live_count, first, pred, position),
@@ -826,11 +947,14 @@
         ],
         "lru_grad",
     )
-    du_part, heads, totals, d_rec, d_in, d_branch, ff_home = barrier(
-        (du_part, heads, totals, d_rec, d_in, d_branch, ff_home)
-    )
+    du_part, heads, totals, d_rec, d_in, ff_home, mlp_parts, d_branch = barrier(
+        (du_part, heads, totals, d_rec, d_in, ff_home, mlp_parts, d_branch)
+    )
+    grad_out, ff_home = barrier((grad_out, ff_home))
+    out_home = home_rows(grad_out)
+    grad_branch = mm_tn(normed_one, d_branch, jnp.bfloat16)
+    ff_got = exchange(ff_home.reshape(seq_size, 2, chunk, ffw))
     heads = edges(heads[:, 9 - TAPS :])
-    grad_branch = mm_tn(normed_one, d_branch, jnp.bfloat16)
     full_rec, full_in = mm_tn(conv_low, d_rec), mm_tn(conv_low, d_in)
     du_part = du_part.reshape(blocks, BLOCK, width)
     (patch,) = whole(
@@ -842,16 +966,23 @@
         "lru_heads",
     )
     d_input = lax.dynamic_update_slice(du_part, patch, (0, BLOCK - 16, 0)).reshape(count, width)
-    d_input, mixed, grad_branch, full_rec, full_in, out_home = barrier(
-        (d_input, mixed, grad_branch, full_rec, full_in, out_home)
-    )
+    branch_pack = by_owner((grad_branch,)).reshape(z_size * seq_size * chunk, width)
+    d_input, full_rec, full_in, ff_got, branch_pack, out_home = barrier(
+        (d_input, full_rec, full_in, ff_got, branch_pack, out_home)
+    )
+    branch_home = home_rows(branch_pack)
     grad_input = mm_tn(normed_one, d_input, jnp.bfloat16)
-    got = exchange(ff_home.reshape(seq_size, 2, chunk, ffw))
-    grad_gate_home, grad_up_home = own_columns(got[:, 0]), own_columns(got[:, 1])
+    grad_gate_home, grad_up_home = own_columns(ff_got[:, 0]), own_columns(ff_got[:, 1])
+    late_input, grad_input = barrier((d_input, grad_input))
     grad_gain_two = gain_home(norm_gain2, ((grad_gate_home, w_gate), (grad_up_home, w_up)))
-    grad_normed_one = scatter_plane(
-        lambda odd: mm_nt(side(d_branch, odd), branch_w) + mm_nt(side(d_input, odd), input_w)
-    )
+    one_parts, one_last = scatter_plane(
+        slot_product(
+            (d_branch, late_input), lambda one, two: mm_nt(one, branch_w) + mm_nt(two, input_w)
+        )
+    )
+    one_last, mlp_parts = barrier((one_last, mlp_parts))
+    mixed = as_low(live_col * (resid_mid + summed(mlp_parts)))
+    grad_normed_one = summed(one_parts)
     scaled_one = gain_one * grad_normed_one
     scale_one = lax.rsqrt(jnp.mean(resid_in * resid_in, axis=-1, keepdims=True) + NORM_EPSILON)
     tokens_grad = as_low(
@@ -873,8 +1004,8 @@
     totals = jnp.concatenate(
         [totals[:7], totals[7:] * (GATE_SCALE * jax.nn.sigmoid(-decay))[None]], axis=0
     )
+    gates = blocks_of(full_rec, 0) + blocks_of(full_in, gate_width)
     owned = width // z_size
-    gates = blocks_of(full_rec, 0) + blocks_of(full_in, gate_width)
     gates = as_low(gates).reshape(z_size, owned, 2 * gate_width)
     totals = jnp.swapaxes(jnp.pad(totals, ((0, 8), (0, 0))).reshape(16, z_size, owned), 0, 1)
     totals = as_low(totals)
@@ -883,14 +1014,18 @@
     pack = jnp.concatenate(
         [
             jnp.pad(part, ((0, 0), (0, 0), (0, lanes - part.shape[-1])))
-            for part in (by_owner((grad_branch,)).reshape(z_size, edge, width), gates, totals)
+            for part in (
+                by_owner((grad_input,)).reshape(z_size, edge, width),
+                gates,
+                totals,
+            )
         ],
         axis=1,
     )
-    pack = home_rows(pack.reshape(z_size * pack.shape[1], lanes))
-    input_home = home_rows(by_owner((grad_input,)).reshape(z_size * edge, width))
-    grad_branch_home = own_columns(exchange(pack[:edge, :width].reshape(seq_size, chunk, width)))
-    grad_input_home = own_columns(exchange(input_home.reshape(seq_size, chunk, width)))
+    pack, branch_home = barrier((pack.reshape(z_size * pack.shape[1], lanes), branch_home))
+    pack = home_rows(pack)
+    grad_branch_home = own_columns(exchange(branch_home.reshape(seq_size, chunk, width)))
+    grad_input_home = own_columns(exchange(pack[:edge, :width].reshape(seq_size, chunk, width)))
     grad_gain_one = gain_home(
         norm_gain1, ((grad_branch_home, w_branch), (grad_input_home, w_input))
     )

time: 869 us -> 727 us (0.84)
  matrix products: 179 us -> 113 us
  waiting for transfers between devices: 259 us -> 209 us
  blocking collectives: 42.8 us -> 0 us
  Pallas kernels: 113 us -> 149 us
  other arithmetic: 77.3 us -> 51.4 us
    pallas_call x4 -> x6, Pallas kernels: 51.2 us -> 89.3 us  [the longest x3 41.9 us: stack(): pl.pallas_call(kernel, grid=(steps,), in_specs=piece_specs(pieces, steps)...]
    dot_general x7 -> x10, matrix products: 50.3 us -> 18.2 us  [mm(): return jnp.dot(left, right, preferred_element_type=jnp.float32).astype(out)]
    reduce_scatter x5, waiting for transfers between devices: 36.9 us -> 6.14 us  [home_rows(): return lax.psum_scatter(value, 'fsdp', scatter_dimension=0, tiled=True)]
    dot_general x9 -> x32, matrix products: 73.1 us -> 43.3 us  [mm_nt(): lax.dot_general(left, right, (((1,), (1,)), ((), ())), preferred_element_...]
    all_gather x2 -> x0, blocking collectives: 25.2 us -> none  [the longest x1 16.3 us: shards(): small = lax.all_gather(small, 'fsdp', axis=0, tiled=False)]
    ppermute x76 -> x85, waiting for transfers between devices: 189 us -> 170 us  [swap(): return lax.ppermute(values, axis, [(i, i ^ flip) for i in range(count)])]
    all_to_all x1 -> x0, blocking collectives: 17.7 us -> none  [exchange(): return lax.all_to_all(value, 'seq', 0, 0, tiled=True)]
    add x7 -> x1, other arithmetic: 14.8 us -> 0.32 us  [scatter_plane(): after = product(slot, after) + as_wide(ready[slot])]
  transfers between devices with their start and end apart: 91 -> 101, of which waited for: 31 -> 46; matrix products, arithmetic and copies ran while one was open for 30% -> 27% of each run, Pallas kernels for 13% -> 18%
where the time goes in v2:
time: 727 us; the launch traced here: 718 us
  waiting for transfers between devices  209 us (29%)
  Pallas kernels  149 us (20%)
  matrix products  113 us (16%)
  starting transfers between devices  93.7 us (13%)
  local copies, waits for them, and re-layouts  84.9 us (12%)
  other arithmetic  51.4 us (7%)
  between operations  16.5 us (2%)
    ppermute x85, waiting for transfers between devices, swap(): return lax.ppermute(values, axis, [(i, i ^ flip) for i in range(count)])  170 us
    ppermute x85, starting transfers between devices, swap(): return lax.ppermute(values, axis, [(i, i ^ flip) for i in range(count)])  73 us
    pallas_call x4, Pallas kernels, whole(): pl.pallas_call(kernel, out_shape=outs, in_specs=specs, out_specs=[pl.Bloc...  59.8 us
    dot_general x8, matrix products, mm_tn(): lax.dot_general(left, right, (((0,), (0,)), ((), ())), preferred_element_...  50.2 us
    dot_general x32, matrix products, mm_nt(): lax.dot_general(left, right, (((1,), (1,)), ((), ())), preferred_element_...  43.3 us
    pallas_call x3, Pallas kernels, stack(): pl.pallas_call(kernel, grid=(steps,), in_specs=piece_specs(pieces, steps)...  41.9 us
    convert_element_type x20, other arithmetic, as_low(): return values.astype(jnp.bfloat16)  25 us
    pallas_call x1, Pallas kernels, lru_back(): pl.pallas_call(kernel, grid=(steps,), in_specs=piece_specs(pieces, steps)...  21.7 us
  transfers between devices with their start and end apart: 101, of which 46 were waited for; matrix products, arithmetic and copies ran while one was open for 27% of the time, Pallas kernels for 18%

profile of v2, /device:TPU:0, one launch (start us, length us, event | category | flops | bytes accessed | tf_op | source)
XLA Modules:
  0.0 717.9 jit_solution(16971792900743664931)
XLA Ops:
  17.8 3.7 all-to-all-start
  22.0 12.6 %collective-permute-done.1.refs_2_ = bf16[256,2048]{1,0:T(8,128)(2,1)} collective-permute-done((bf16[256,2048]{1,0:T(8,128)(2,1)}, bf16[256,2048]{1,0:T(8,128)(2,1)}, u32[]{:S(2)}, u32[]{:S(2)}) %collective-permute-start.1) | collective-permute-done | bytes 1048608 | tf_op jit(solution)/shard_map/ppermute | solution.py:46
  44.5 10.3 %collective-permute-done.2.refs_3_ = bf16[128,2048]{1,0:T(8,128)(2,1)S(1)} collective-permute-done((bf16[128,2048]{1,0:T(8,128)(2,1)S(1)}, bf16[128,2048]{1,0:T(8,128)(2,1)S(1)}, u32[]{:S(2)}, u32[]{:S(2)}) %collective-permute-start.2) | collective-permute-done | bytes 524320 | tf_op jit(solution)/shard_map/ppermute | solution.py:46
  65.1 7.5 %collective-permute-done.12 = bf16[1,80,344]{1,2,0:T(8,128)(2,1)S(1)} collective-permute-done((bf16[1,80,344]{1,2,0:T(8,128)(2,1)S(1)}, bf16[1,80,344]{1,2,0:T(8,128)(2,1)S(1)}, u32[]{:S(2)}, u32[]{:S(2)}) %collective-permute-start.12) | collective-permute-done | bytes 55072 | tf_op jit(solution)/shard_map/ppermute | solution.py:46
  76.0 15.2 %collective-permute-done.13 = bf16[2,80,344]{1,2,0:T(8,128)(2,1)S(1)} collective-permute-done((bf16[2,80,344]{1,2,0:T(8,128)(2,1)S(1)}, bf16[2,80,344]{1,2,0:T(8,128)(2,1)S(1)}, u32[]{:S(2)}, u32[]{:S(2)}) %collective-permute-start.13) | collective-permute-done | bytes 110112 | tf_op jit(solution)/shard_map/ppermute | solution.py:46
  100.5 4.3 all-to-all-start.1
  109.6 13.3 %norm_one.1 = (bf16[8,256,2048]{2,1,0:T(8,128)(2,1)}, f32[8,256,320]{2,1,0:T(8,128)}) custom-call(bf16[256,2048]{1,0:T(8,128)(2,1)S(1)} %copy-done.9, bf16[256,2048]{1,0:T(8,128)(2,1)} %collective-permute-done.refs_1_, bf16[256,2048]{1,0:T(8,128)(2,1)} %collective-permute-done.1.refs_2_, bf16[128,2048]{1,0:T(8,128)(2,1)S(1)} %collective-permute-done.2.refs_3_, ...), custom_call_target="tpu_custom_call" | custom-call | flops 1 | bytes 1 | tf_op jit(solution)/shard_map/norm_one/pallas_call | solution.py:245
  124.6 3.5 collective-permute-start.15
  144.5 16.9 %lru_forward.1 = (bf16[2048,320]{1,0:T(8,128)(2,1)S(1)}, f32[3,2048,128]{2,1,0:T(8,128)S(1)}, f32[3,2048,128]{2,1,0:T(8,128)}, f32[3,2048,128]{2,1,0:T(8,128)}, ...) custom-call(s32[16]{0:T(128)S(1)} %select_reduce_fusion.3.live_ref, s32[16]{0:T(128)S(1)} %convert_element_type.397.first_ref, ...), custom_call_target="tpu_custom_call" | custom-call | flops 1 | bytes 1 | tf_op jit(solution)/shard_map/lru_forward/pallas_call | solution.py:678
  171.5 4.1 collective-permute-start.19
  175.6 8.7 %branch_pre.1.ypre_ref = f32[2048,320]{1,0:T(8,128)S(1)} custom-call(bf16[2048,2048]{1,0:T(8,128)(2,1)} %bitcast.287, bf16[2048,320]{1,0:T(8,128)(2,1)S(1)} %bitcast.238), custom_call_target="tpu_custom_call" | custom-call | flops 2684354560 | bytes 11010048 | tf_op jit(solution)/shard_map/branch_pre/pallas_call | solution.py:296
  188.0 12.0 %lru_state.1 = (f32[3,2048,128]{2,1,0:T(8,128)S(1)}, bf16[2048,320]{1,0:T(8,128)(2,1)S(1)}, f32[3,16,128]{2,1,0:T(8,128)S(1)}) custom-call(s32[64]{0:T(128)S(1)} %select_reduce_fusion.pos_ref, f32[4,2,3,16,128]{4,3,2,1,0:T(8,128)S(1)} %pad_maximum_fusion.3.all_ref, f32[3,2048,128]{2,1,0:T(8,128)} %copy-done.5, f32[3,2048,128]{2,1,0:T(8,128)} %get-tuple-element.219.drive_ref, ...), custom_call_target="tpu_custom_call" | custom-call | flops 1 | bytes 1 | tf_op jit(solution)/shard_map/lru_state/pallas_call | solution.py:678
  219.9 4.3 collective-permute-done.28
  236.6 8.7 %stack_top.1 = bf16[8,256,2048]{2,1,0:T(8,128)(2,1)} custom-call(bf16[256,2048]{1,0:T(8,128)(2,1)S(1)} %fusion.20.refs_0_, bf16[256,2048]{1,0:T(8,128)(2,1)} %collective-permute-done.20.refs_1_, bf16[256,2048]{1,0:T(8,128)(2,1)} %collective-permute-done.21.refs_2_, bf16[256,2048]{1,0:T(8,128)(2,1)} %collective-permute-done.22.refs_3_, ...), custom_call_target="tpu_custom_call" | custom-call | flops 1 | bytes 1 | tf_op jit(solution)/shard_map/stack_top/pallas_call | solution.py:245
  245.3 4.1 copy.174
  249.4 6.1 collective-permute-done.29
  263.3 11.4 %all-gather.21.cloned.1.call-done = bf16[32,64,768]{2,1,0:T(8,128)(2,1)} async-done(((bf16[8,64,768]{2,1,0:T(8,128)(2,1)}), bf16[32,64,768]{2,1,0:T(8,128)(2,1)}) %all-gather.21.cloned.1.call-update) | async-done | bytes 3145744 | tf_op jit(solution)/shard_map/all_gather | solution.py:763
  274.6 3.9 copy.176
  278.5 6.3 collective-permute-done.37.refs_1_
  289.1 12.4 %collective-permute-done.39.refs_3_ = bf16[128,2048]{1,0:T(8,128)(2,1)S(1)} collective-permute-done((bf16[128,2048]{1,0:T(8,128)(2,1)S(1)}, bf16[128,2048]{1,0:T(8,128)(2,1)S(1)}, u32[]{:S(2)}, u32[]{:S(2)}) %collective-permute-start.39) | collective-permute-done | bytes 524320 | tf_op jit(solution)/shard_map/ppermute | solution.py:46
  304.2 19.9 %ff_forward.1 = (bf16[8,256,2048]{2,1,0:T(8,128)(2,1)}, f32[8,256,768]{2,1,0:T(8,128)}, f32[8,256,768]{2,1,0:T(8,128)}, bf16[8,256,768]{2,1,0:T(8,128)(2,1)}) custom-call(bf16[256,2048]{1,0:T(8,128)(2,1)S(1)} %multiply_convert_fusion.1.refs_0_, bf16[256,2048]{1,0:T(8,128)(2,1)S(1)} %collective-permute-done.37.refs_1_, ...), custom_call_target="tpu_custom_call" | custom-call | flops 1 | bytes 1 | tf_op jit(solution)/shard_map/ff_forward/pallas_call | solution.py:245
  324.0 14.7 %all-gather.13.cloned.1.call-done.down_ref = bf16[768,2048]{1,0:T(8,128)(2,1)} async-done(((bf16[192,2048]{1,0:T(8,128)(2,1)}), bf16[768,2048]{1,0:T(8,128)(2,1)}) %all-gather.13.cloned.1.call-update) | async-done | bytes 3145744 | tf_op jit(solution)/shard_map/all_gather | solution.py:760
  338.8 17.0 %ff_backward.1 = (bf16[2048,768]{1,0:T(8,128)(2,1)S(1)}, bf16[2048,768]{1,0:T(8,128)(2,1)}) custom-call(bf16[2048,2048]{1,0:T(8,128)(2,1)} %bitcast.279, bf16[768,2048]{1,0:T(8,128)(2,1)} %all-gather.13.cloned.1.call-done.down_ref, f32[2048,768]{1,0:T(8,128)} %bitcast.299, f32[2048,768]{1,0:T(8,128)} %bitcast.300), custom_call_target="tpu_custom_call" | custom-call | flops 1 | bytes 1 | tf_op jit(solution)/shard_map/ff_backward/pallas_call | solution.py:272
  382.1 8.3 %convolution_convert_fusion.1 = bf16[768,2048]{1,0:T(8,128)(2,1)} fusion(bf16[2048,768]{1,0:T(8,128)(2,1)S(1)} %bitcast.348, bf16[2048,2048]{1,0:T(8,128)(2,1)S(1)} %bitcast.282), kind=kOutput, calls=%fused_computation.10 | convolution fusion | flops 6444023808 | bytes 14680064 | tf_op jit(solution)/shard_map/dot_general | solution.py:33
  395.4 9.0 %collective-permute-done.51 = bf16[128,2048]{1,0:T(8,128)(2,1)S(1)} collective-permute-done((bf16[128,2048]{1,0:T(8,128)(2,1)S(1)}, bf16[128,2048]{1,0:T(8,128)(2,1)S(1)}, u32[]{:S(2)}, u32[]{:S(2)}) %collective-permute-start.51) | collective-permute-done | bytes 524320 | tf_op jit(solution)/shard_map/ppermute | solution.py:46
  409.1 9.5 %convolution_convert_fusion.3 = bf16[2048,768]{1,0:T(8,128)(2,1)S(1)} fusion(bf16[2048,2048]{1,0:T(8,128)(2,1)} %bitcast.342, bf16[2048,768]{1,0:T(8,128)(2,1)S(1)} %copy-done.12), kind=kOutput, calls=%fused_computation.12 | convolution fusion | flops 6444023808 | bytes 14680064 | tf_op jit(solution)/shard_map/dot_general | solution.py:33
  418.7 7.4 %convolution_convert_fusion.2 = bf16[2048,768]{1,0:T(8,128)(2,1)S(1)} fusion(bf16[2048,2048]{1,0:T(8,128)(2,1)S(1)} %bitcast.345, bf16[2048,768]{1,0:T(8,128)(2,1)S(1)} %copy-done.51), kind=kOutput, calls=%fused_computation.11 | convolution fusion | flops 6444023808 | bytes 14680064 | tf_op jit(solution)/shard_map/dot_general | solution.py:33
  435.7 3.9 fusion.67
  439.6 3.6 convolution_convert_fusion
  445.3 5.1 collective-permute-done.58
  450.4 4.9 fusion.81
  459.0 9.9 %collective-permute-done.56.refs_1_ = bf16[256,2048]{1,0:T(8,128)(2,1)S(1)} collective-permute-done((bf16[256,2048]{1,0:T(8,128)(2,1)S(1)}, bf16[256,2048]{1,0:T(8,128)(2,1)S(1)}, u32[]{:S(2)}, u32[]{:S(2)}) %collective-permute-start.56) | collective-permute-done | bytes 1048608 | tf_op jit(solution)/shard_map/ppermute | solution.py:46
  474.0 10.0 %collective-permute-done.59.refs_3_ = bf16[128,2048]{1,0:T(8,128)(2,1)S(1)} collective-permute-done((bf16[128,2048]{1,0:T(8,128)(2,1)S(1)}, bf16[128,2048]{1,0:T(8,128)(2,1)S(1)}, u32[]{:S(2)}, u32[]{:S(2)}) %collective-permute-start.59) | collective-permute-done | bytes 524320 | tf_op jit(solution)/shard_map/ppermute | solution.py:46
  490.3 21.7 %lru_back.1 = (bf16[8,256,2048]{2,1,0:T(8,128)(2,1)}, bf16[8,256,320]{2,1,0:T(8,128)(2,1)}, f32[3,2048,128]{2,1,0:T(8,128)}, f32[3,16,128]{2,1,0:T(8,128)S(1)}) custom-call(bf16[256,2048]{1,0:T(8,128)(2,1)S(1)} %get-tuple-element.289.refs_0_, bf16[256,2048]{1,0:T(8,128)(2,1)S(1)} %collective-permute-done.56.refs_1_, ...), custom_call_target="tpu_custom_call" | custom-call | flops 1 | bytes 1 | tf_op jit(solution)/shard_map/lru_back/pallas_call | solution.py:485
  513.6 4.9 collective-permute-done.66
  518.6 7.5 %convolution_convert_fusion.6 = bf16[320,2048]{1,0:T(8,128)(2,1)} fusion(bf16[2048,320]{1,0:T(8,128)(2,1)S(1)} %copy-done.20, bf16[2048,2048]{1,0:T(8,128)(2,1)} %bitcast.346), kind=kOutput, calls=%fused_computation.35 | convolution fusion | flops 2685009920 | bytes 11010048 | tf_op jit(solution)/shard_map/dot_general | solution.py:33
  526.2 30.2 %lru_grad.1 = (bf16[2048,320]{1,0:T(8,128)(2,1)S(1)}, bf16[2048,320]{1,0:T(8,128)(2,1)S(1)}, bf16[2048,320]{1,0:T(8,128)(2,1)}, f32[16,8,320]{2,1,0:T(8,128)S(1)...) custom-call(s32[16]{0:T(128)S(1)} %copy-done.24, s32[16]{0:T(128)S(1)} %copy-done.28, s32[16]{0:T(128)S(1)} %copy-done.26, ...), custom_call_target="tpu_custom_call" | custom-call | flops 1 | bytes 1 | tf_op jit(solution)/shard_map/lru_grad/pallas_call | solution.py:678
  559.4 4.7 reduce-scatter.8.cloned.1.call-done
  571.3 4.4 all-to-all-start.2
  582.8 7.4 %convolution_convert_fusion.5 = bf16[2048,320]{0,1:T(8,128)(2,1)} fusion(bf16[2048,2048]{1,0:T(8,128)(2,1)} %bitcast.288, bf16[2048,320]{1,0:T(8,128)(2,1)S(1)} %bitcast.318), kind=kOutput, calls=%fused_computation.34 | convolution fusion | flops 2685009920 | bytes 11010048 | tf_op jit(solution)/shard_map/dot_general | solution.py:33
  598.2 6.9 convolution_convert_fusion.4
  642.5 7.4 %collective-permute-done.80 = bf16[128,2048]{1,0:T(8,128)(2,1)S(1)} collective-permute-done((bf16[128,2048]{1,0:T(8,128)(2,1)S(1)}, bf16[128,2048]{1,0:T(8,128)(2,1)S(1)}, u32[]{:S(2)}, u32[]{:S(2)}) %collective-permute-start.80) | collective-permute-done | bytes 524320 | tf_op jit(solution)/shard_map/ppermute | solution.py:46
  665.8 11.2 %collective-permute-done.81 = bf16[128,2048]{1,0:T(8,128)(2,1)} collective-permute-done((bf16[128,2048]{1,0:T(8,128)(2,1)}, bf16[128,2048]{1,0:T(8,128)(2,1)}, u32[]{:S(2)}, u32[]{:S(2)}) %collective-permute-start.81) | collective-permute-done | bytes 524320 | tf_op jit(solution)/shard_map/ppermute | solution.py:46
  677.0 5.8 collective-permute-done.84
  682.9 4.3 fusion.13
  687.2 3.8 multiply_convert_fusion
  691.1 3.6 fusion.18
  704.6 4.9 all-to-all-done.4
  (643 shorter events, 280.4 us)
Async XLA Ops:
  7.2 47.6 %all-gather.11.cloned.1.call-start = ((), (), s32[]{:S(2)}) async-start(), calls=%async_computation.10 | async-start | bytes 1638400 | tf_op jit(solution)/shard_map/all_gather | solution.py:760
  7.3 27.3 %collective-permute-start.1 = (bf16[256,2048]{1,0:T(8,128)(2,1)}, bf16[256,2048]{1,0:T(8,128)(2,1)}, u32[]{:S(2)}, u32[]{:S(2)}) collective-permute-start(bf16[256,2048]{1,0:T(8,128)(2,1)} %refs_0_), channel_id=1, source_target_pairs={{0,16},{4,20},{8,24},{12,28},{16,0},{20,4},{24,8},{28,12},{1,17},{... | collective-permute-start | bytes 3145736 | tf_op jit(solution)/shard_map/ppermute | solution.py:46
  10.3 28.5 %collective-permute-start = (bf16[256,2048]{1,0:T(8,128)(2,1)}, bf16[256,2048]{1,0:T(8,128)(2,1)}, u32[]{:S(2)}, u32[]{:S(2)}) collective-permute-start(bf16[256,2048]{1,0:T(8,128)(2,1)} %refs_0_), channel_id=1, source_target_pairs={{0,8},{4,12},{8,0},{12,4},{16,24},{20,28},{24,16},{28,20},{1,9},{5... | collective-permute-start | bytes 3145736 | tf_op jit(solution)/shard_map/ppermute | solution.py:46
  14.9 41.1 %collective-permute-start.9 = (bf16[1,2,64]{2,1,0:T(2,128)(2,1)}, bf16[1,2,64]{2,1,0:T(2,128)(2,1)S(1)}, u32[]{:S(2)}, u32[]{:S(2)}) collective-permute-start(bf16[1,2,64]{2,1,0:T(2,128)(2,1)} %pad_maximum_fusion.8), channel_id=1, source_target_pairs={{0,4},{4,0},{8,12},{12,8},{16,20},{20,16},{24,28},{28,24},{1,5},{5... | collective-permute-start | bytes 776 | tf_op jit(solution)/shard_map/ppermute | solution.py:46
  17.8 26.7 %all-to-all-start = ((bf16[8,2,64,320]{3,2,1,0:T(8,128)(2,1)}), bf16[8,2,64,320]{3,2,1,0:T(8,128)(2,1)S(1)}, u32[]{:S(2)}, u32[]{:S(2)}) async-start(bf16[8,2,64,320]{3,2,1,0:T(8,128)(2,1)} %copy.161), calls=%async_computation | async-start | bytes 1572864 | tf_op jit(solution)/shard_map/all_to_all | solution.py:757
  21.5 85.3 %all-gather.15.cloned.1.call-start = ((), (), s32[]{:S(2)}) async-start(), calls=%async_computation.17 | async-start | bytes 1966080 | tf_op jit(solution)/shard_map/all_gather | solution.py:763
  55.8 111.2 %all-gather.17.cloned.1.call-start = ((), (), s32[]{:S(2)}) async-start(), calls=%async_computation.18 | async-start | bytes 1966080 | tf_op jit(solution)/shard_map/all_gather | solution.py:763
  73.5 24.1 %collective-permute-start.4 = (bf16[256,2048]{1,0:T(8,128)(2,1)S(1)}, bf16[256,2048]{1,0:T(8,128)(2,1)}, u32[]{:S(2)}, u32[]{:S(2)}) collective-permute-start(bf16[256,2048]{1,0:T(8,128)(2,1)S(1)} %copy-done.9), channel_id=1, source_target_pairs={{0,4},{4,0},{8,12},{12,8},{16,20},{20,16},{24,28},{28,24},{1,5},{5... | collective-permute-start | bytes 3145736 | tf_op jit(solution)/shard_map/ppermute | solution.py:46
  73.5 24.1 %collective-permute-start.5 = (bf16[256,2048]{1,0:T(8,128)(2,1)}, bf16[256,2048]{1,0:T(8,128)(2,1)}, u32[]{:S(2)}, u32[]{:S(2)}) collective-permute-start(bf16[256,2048]{1,0:T(8,128)(2,1)} %collective-permute-done.refs_1_), channel_id=1, source_target_pairs={{0,4},{4,0},{8,12},{12,8},{16,20},{20,16},{24,28},{28,24},{1,5},{5... | collective-permute-start | bytes 3145736 | tf_op jit(solution)/shard_map/ppermute | solution.py:46
  74.0 23.6 %collective-permute-start.6 = (bf16[256,2048]{1,0:T(8,128)(2,1)}, bf16[256,2048]{1,0:T(8,128)(2,1)}, u32[]{:S(2)}, u32[]{:S(2)}) collective-permute-start(bf16[256,2048]{1,0:T(8,128)(2,1)} %collective-permute-done.1.refs_2_), channel_id=1, source_target_pairs={{0,4},{4,0},{8,12},{12,8},{16,20},{20,16},{24,28},{28,24},{1,5},{5... | collective-permute-start | bytes 3145736 | tf_op jit(solution)/shard_map/ppermute | solution.py:46
  75.4 22.1 %collective-permute-start.7 = (bf16[128,2048]{1,0:T(8,128)(2,1)S(1)}, bf16[128,2048]{1,0:T(8,128)(2,1)}, u32[]{:S(2)}, u32[]{:S(2)}) collective-permute-start(bf16[128,2048]{1,0:T(8,128)(2,1)S(1)} %collective-permute-done.2.refs_3_), channel_id=1, source_target_pairs={{0,4},{4,0},{8,12},{12,8},{16,20},{20,16},{24,28},{28,24},{1,5},{5... | collective-permute-start | bytes 1572872 | tf_op jit(solution)/shard_map/ppermute | solution.py:46
  100.5 37.1 %all-to-all-start.1 = ((bf16[8,2,64,768]{3,2,1,0:T(8,128)(2,1)}), bf16[8,2,64,768]{3,2,1,0:T(8,128)(2,1)}, u32[]{:S(2)}, u32[]{:S(2)}) async-start(bf16[8,2,64,768]{3,2,1,0:T(8,128)(2,1)} %copy.172), calls=%async_computation.1 | async-start | bytes 3145728 | tf_op jit(solution)/shard_map/all_to_all | solution.py:757
  104.8 140.5 %all-gather.19.cloned.1.call-start = ((), (), s32[]{:S(2)}) async-start(), calls=%async_computation.19 | async-start | bytes 3932160 | tf_op jit(solution)/shard_map/all_gather | solution.py:763
  140.3 134.3 %all-gather.21.cloned.1.call-start = ((), (), s32[]{:S(2)}) async-start(), calls=%async_computation.20 | async-start | bytes 3932160 | tf_op jit(solution)/shard_map/all_gather | solution.py:763
  140.3 46.5 %collective-permute-start.20 = (bf16[256,2048]{1,0:T(8,128)(2,1)S(1)}, bf16[256,2048]{1,0:T(8,128)(2,1)}, u32[]{:S(2)}, u32[]{:S(2)}) collective-permute-start(bf16[256,2048]{1,0:T(8,128)(2,1)S(1)} %fusion.20.refs_0_), channel_id=1, source_target_pairs={{0,8},{4,12},{8,0},{12,4},{16,24},{20,28},{24,16},{28,20},{1,9},{5... | collective-permute-start | bytes 3145736 | tf_op jit(solution)/shard_map/ppermute | solution.py:46
  142.2 45.8 %collective-permute-start.21 = (bf16[256,2048]{1,0:T(8,128)(2,1)S(1)}, bf16[256,2048]{1,0:T(8,128)(2,1)}, u32[]{:S(2)}, u32[]{:S(2)}) collective-permute-start(bf16[256,2048]{1,0:T(8,128)(2,1)S(1)} %fusion.20.refs_0_), channel_id=1, source_target_pairs={{0,16},{4,20},{8,24},{12,28},{16,0},{20,4},{24,8},{28,12},{1,17},{... | collective-permute-start | bytes 3145736 | tf_op jit(solution)/shard_map/ppermute | solution.py:46
  143.7 44.4 %collective-permute-start.22 = (bf16[256,2048]{1,0:T(8,128)(2,1)S(1)}, bf16[256,2048]{1,0:T(8,128)(2,1)}, u32[]{:S(2)}, u32[]{:S(2)}) collective-permute-start(bf16[256,2048]{1,0:T(8,128)(2,1)S(1)} %fusion.20.refs_0_), channel_id=1, source_target_pairs={{0,24},{4,28},{8,16},{12,20},{16,8},{20,12},{24,0},{28,4},{1,25},{... | collective-permute-start | bytes 3145736 | tf_op jit(solution)/shard_map/ppermute | solution.py:46
  144.1 194.7 %all-gather.13.cloned.1.call-start = ((), (), s32[]{:S(2)}) async-start(), calls=%async_computation.11 | async-start | bytes 3932160 | tf_op jit(solution)/shard_map/all_gather | solution.py:760
  217.5 252.1 %reduce-scatter.6.cloned.1.call-start = ((), (), s32[]{:S(2)}) async-start(), calls=%async_computation.12 | async-start | bytes 3932160 | tf_op jit(solution)/shard_map/reduce_scatter | solution.py:870
  233.0 22.5 %collective-permute-start.29 = (bf16[128,2048]{1,0:T(8,128)(2,1)}, bf16[128,2048]{1,0:T(8,128)(2,1)}, u32[]{:S(2)}, u32[]{:S(2)}) collective-permute-start(bf16[128,2048]{1,0:T(8,128)(2,1)} %fusion.33), channel_id=1, source_target_pairs={{0,8},{4,12},{8,0},{12,4},{16,24},{20,28},{24,16},{28,20},{1,9},{5... | collective-permute-start | bytes 1572872 | tf_op jit(solution)/shard_map/ppermute | solution.py:46
  235.0 23.9 %collective-permute-start.32 = (bf16[128,2048]{1,0:T(8,128)(2,1)}, bf16[128,2048]{1,0:T(8,128)(2,1)}, u32[]{:S(2)}, u32[]{:S(2)}) collective-permute-start(bf16[128,2048]{1,0:T(8,128)(2,1)} %slice.533), channel_id=1, source_target_pairs={{0,16},{4,20},{8,24},{12,28},{16,0},{20,4},{24,8},{28,12},{1,17},{... | collective-permute-start | bytes 1572872 | tf_op jit(solution)/shard_map/ppermute | solution.py:46
  261.4 23.3 %collective-permute-start.37 = (bf16[256,2048]{1,0:T(8,128)(2,1)S(1)}, bf16[256,2048]{1,0:T(8,128)(2,1)S(1)}, u32[]{:S(2)}, u32[]{:S(2)}) collective-permute-start(bf16[256,2048]{1,0:T(8,128)(2,1)S(1)} %multiply_convert_fusion.1.refs_0_), channel_id=1, source_target_pairs={{0,8},{4,12},{8,0},{12,4},{16,24},{20,28},{24,16},{28,20},{1,9},{5... | collective-permute-start | bytes 3145736 | tf_op jit(solution)/shard_map/ppermute | solution.py:46
  262.6 23.3 %collective-permute-start.38 = (bf16[256,2048]{1,0:T(8,128)(2,1)S(1)}, bf16[256,2048]{1,0:T(8,128)(2,1)}, u32[]{:S(2)}, u32[]{:S(2)}) collective-permute-start(bf16[256,2048]{1,0:T(8,128)(2,1)S(1)} %multiply_convert_fusion.1.refs_0_), channel_id=1, source_target_pairs={{0,16},{4,20},{8,24},{12,28},{16,0},{20,4},{24,8},{28,12},{1,17},{... | collective-permute-start | bytes 3145736 | tf_op jit(solution)/shard_map/ppermute | solution.py:46
  263.3 39.0 %collective-permute-start.41 = (bf16[256,2048]{1,0:T(8,128)(2,1)S(1)}, bf16[256,2048]{1,0:T(8,128)(2,1)}, u32[]{:S(2)}, u32[]{:S(2)}) collective-permute-start(bf16[256,2048]{1,0:T(8,128)(2,1)S(1)} %multiply_convert_fusion.1.refs_0_), channel_id=1, source_target_pairs={{0,4},{4,0},{8,12},{12,8},{16,20},{20,16},{24,28},{28,24},{1,5},{5... | collective-permute-start | bytes 3145736 | tf_op jit(solution)/shard_map/ppermute | solution.py:46
  390.3 173.7 %reduce-scatter.8.cloned.1.call-start = ((), (), s32[]{:S(2)}) async-start(), calls=%async_computation.13 | async-start | bytes 7864320 | tf_op jit(solution)/shard_map/reduce_scatter | solution.py:870
  394.8 34.9 %collective-permute-start.50 = (bf16[128,2048]{1,0:T(8,128)(2,1)S(1)}, bf16[128,2048]{1,0:T(8,128)(2,1)S(1)}, u32[]{:S(2)}, u32[]{:S(2)}) collective-permute-start(bf16[128,2048]{1,0:T(8,128)(2,1)S(1)} %slice.532), channel_id=1, source_target_pairs={{0,8},{4,12},{8,0},{12,4},{16,24},{20,28},{24,16},{28,20},{1,9},{5... | collective-permute-start | bytes 1572872 | tf_op jit(solution)/shard_map/ppermute | solution.py:46
  404.6 25.1 %collective-permute-start.52 = (bf16[128,2048]{1,0:T(8,128)(2,1)S(1)}, bf16[128,2048]{1,0:T(8,128)(2,1)S(1)}, u32[]{:S(2)}, u32[]{:S(2)}) collective-permute-start(bf16[128,2048]{1,0:T(8,128)(2,1)S(1)} %fusion.31), channel_id=1, source_target_pairs={{0,8},{4,12},{8,0},{12,4},{16,24},{20,28},{24,16},{28,20},{1,9},{5... | collective-permute-start | bytes 1572872 | tf_op jit(solution)/shard_map/ppermute | solution.py:46
  407.0 22.7 %collective-permute-start.54 = (bf16[128,2048]{1,0:T(8,128)(2,1)S(1)}, bf16[128,2048]{1,0:T(8,128)(2,1)S(1)}, u32[]{:S(2)}, u32[]{:S(2)}) collective-permute-start(bf16[128,2048]{1,0:T(8,128)(2,1)S(1)} %fusion.30), channel_id=1, source_target_pairs={{0,16},{4,20},{8,24},{12,28},{16,0},{20,4},{24,8},{28,12},{1,17},{... | collective-permute-start | bytes 1572872 | tf_op jit(solution)/shard_map/ppermute | solution.py:46
  407.9 22.6 %collective-permute-start.55 = (bf16[128,2048]{1,0:T(8,128)(2,1)S(1)}, bf16[128,2048]{1,0:T(8,128)(2,1)S(1)}, u32[]{:S(2)}, u32[]{:S(2)}) collective-permute-start(bf16[128,2048]{1,0:T(8,128)(2,1)S(1)} %slice.531), channel_id=1, source_target_pairs={{0,16},{4,20},{8,24},{12,28},{16,0},{20,4},{24,8},{28,12},{1,17},{... | collective-permute-start | bytes 1572872 | tf_op jit(solution)/shard_map/ppermute | solution.py:46
  431.3 166.9 %reduce-scatter.10.cloned.1.call-start = ((), (), s32[]{:S(2)}) async-start(), calls=%async_computation.14 | async-start | bytes 1638400 | tf_op jit(solution)/shard_map/reduce_scatter | solution.py:870
  443.3 25.6 %collective-permute-start.56 = (bf16[256,2048]{1,0:T(8,128)(2,1)S(1)}, bf16[256,2048]{1,0:T(8,128)(2,1)S(1)}, u32[]{:S(2)}, u32[]{:S(2)}) collective-permute-start(bf16[256,2048]{1,0:T(8,128)(2,1)S(1)} %get-tuple-element.289.refs_0_), channel_id=1, source_target_pairs={{0,8},{4,12},{8,0},{12,4},{16,24},{20,28},{24,16},{28,20},{1,9},{5... | collective-permute-start | bytes 3145736 | tf_op jit(solution)/shard_map/ppermute | solution.py:46
  444.3 25.3 %collective-permute-start.57 = (bf16[256,2048]{1,0:T(8,128)(2,1)S(1)}, bf16[256,2048]{1,0:T(8,128)(2,1)}, u32[]{:S(2)}, u32[]{:S(2)}) collective-permute-start(bf16[256,2048]{1,0:T(8,128)(2,1)S(1)} %get-tuple-element.289.refs_0_), channel_id=1, source_target_pairs={{0,16},{4,20},{8,24},{12,28},{16,0},{20,4},{24,8},{28,12},{1,17},{... | collective-permute-start | bytes 3145736 | tf_op jit(solution)/shard_map/ppermute | solution.py:46
  445.3 39.5 %collective-permute-start.61 = (bf16[256,2048]{1,0:T(8,128)(2,1)S(1)}, bf16[256,2048]{1,0:T(8,128)(2,1)}, u32[]{:S(2)}, u32[]{:S(2)}) collective-permute-start(bf16[256,2048]{1,0:T(8,128)(2,1)S(1)} %get-tuple-element.289.refs_0_), channel_id=1, source_target_pairs={{0,4},{4,0},{8,12},{12,8},{16,20},{20,16},{24,28},{28,24},{1,5},{5... | collective-permute-start | bytes 3145736 | tf_op jit(solution)/shard_map/ppermute | solution.py:46
  486.8 72.6 %collective-permute-start.69 = (bf16[256,2048]{1,0:T(8,128)(2,1)}, bf16[256,2048]{1,0:T(8,128)(2,1)}, u32[]{:S(2)}, u32[]{:S(2)}) collective-permute-start(bf16[256,2048]{1,0:T(8,128)(2,1)} %get-tuple-element.314), channel_id=1, source_target_pairs={{0,24},{4,28},{8,16},{12,20},{16,8},{20,12},{24,0},{28,4},{1,25},{... | collective-permute-start | bytes 3145736 | tf_op jit(solution)/shard_map/ppermute | solution.py:46
  488.7 70.7 %collective-permute-start.70 = (bf16[256,2048]{1,0:T(8,128)(2,1)}, bf16[256,2048]{1,0:T(8,128)(2,1)}, u32[]{:S(2)}, u32[]{:S(2)}) collective-permute-start(bf16[256,2048]{1,0:T(8,128)(2,1)} %get-tuple-element.315), channel_id=1, source_target_pairs={{0,8},{4,12},{8,0},{12,4},{16,24},{20,28},{24,16},{28,20},{1,9},{5... | collective-permute-start | bytes 3145736 | tf_op jit(solution)/shard_map/ppermute | solution.py:46
  489.8 69.6 %collective-permute-start.71 = (bf16[256,2048]{1,0:T(8,128)(2,1)}, bf16[256,2048]{1,0:T(8,128)(2,1)}, u32[]{:S(2)}, u32[]{:S(2)}) collective-permute-start(bf16[256,2048]{1,0:T(8,128)(2,1)} %get-tuple-element.316), channel_id=1, source_target_pairs={{0,16},{4,20},{8,24},{12,28},{16,0},{20,4},{24,8},{28,12},{1,17},{... | collective-permute-start | bytes 3145736 | tf_op jit(solution)/shard_map/ppermute | solution.py:46
  566.8 27.7 %collective-permute-start.72 = (bf16[48,320]{1,0:T(8,128)(2,1)S(1)}, bf16[48,320]{1,0:T(8,128)(2,1)S(1)}, u32[]{:S(2)}, u32[]{:S(2)}) collective-permute-start(bf16[48,320]{1,0:T(8,128)(2,1)S(1)} %reshape.427), channel_id=1, source_target_pairs={{0,1},{1,0},{2,3},{3,2},{4,5},{5,4},{6,7},{7,6},{8,9},{9,8},{10,11... | collective-permute-start | bytes 92168 | tf_op jit(solution)/shard_map/ppermute | solution.py:46
  568.8 25.6 %collective-permute-start.73 = (bf16[48,320]{1,0:T(8,128)(2,1)S(1)}, bf16[48,320]{1,0:T(8,128)(2,1)S(1)}, u32[]{:S(2)}, u32[]{:S(2)}) collective-permute-start(bf16[48,320]{1,0:T(8,128)(2,1)S(1)} %reshape.427), channel_id=1, source_target_pairs={{0,2},{1,3},{2,0},{3,1},{4,6},{5,7},{6,4},{7,5},{8,10},{9,11},{10,... | collective-permute-start | bytes 92168 | tf_op jit(solution)/shard_map/ppermute | solution.py:46
  570.0 24.5 %collective-permute-start.74 = (bf16[48,320]{1,0:T(8,128)(2,1)S(1)}, bf16[48,320]{1,0:T(8,128)(2,1)S(1)}, u32[]{:S(2)}, u32[]{:S(2)}) collective-permute-start(bf16[48,320]{1,0:T(8,128)(2,1)S(1)} %reshape.427), channel_id=1, source_target_pairs={{0,3},{1,2},{2,1},{3,0},{4,7},{5,6},{6,5},{7,4},{8,11},{9,10},{10,... | collective-permute-start | bytes 92168 | tf_op jit(solution)/shard_map/ppermute | solution.py:46
  571.3 25.5 %all-to-all-start.2 = ((bf16[8,2,64,768]{3,2,1,0:T(8,128)(2,1)}), bf16[8,2,64,768]{3,2,1,0:T(8,128)(2,1)}, u32[]{:S(2)}, u32[]{:S(2)}) async-start(bf16[8,2,64,768]{3,2,1,0:T(8,128)(2,1)} %bitcast.72), calls=%async_computation.4 | async-start | bytes 3145728 | tf_op jit(solution)/shard_map/all_to_all | solution.py:757
  575.7 81.6 %reduce-scatter.12.cloned.1.call-start = ((), (), s32[]{:S(2)}) async-start(), calls=%async_computation.15 | async-start | bytes 1966080 | tf_op jit(solution)/shard_map/reduce_scatter | solution.py:870
  618.4 77.6 %reduce-scatter.14.cloned.1.call-start = ((), (), s32[]{:S(2)}) async-start(), calls=%async_computation.16 | async-start | bytes 2334720 | tf_op jit(solution)/shard_map/reduce_scatter | solution.py:870
  639.5 37.5 %collective-permute-start.78 = (bf16[256,2048]{1,0:T(8,128)(2,1)}, bf16[256,2048]{1,0:T(8,128)(2,1)}, u32[]{:S(2)}, u32[]{:S(2)}) collective-permute-start(bf16[256,2048]{1,0:T(8,128)(2,1)} %fusion.12), channel_id=1, source_target_pairs={{0,4},{4,0},{8,12},{12,8},{16,20},{20,16},{24,28},{28,24},{1,5},{5... | collective-permute-start | bytes 3145736 | tf_op jit(solution)/shard_map/ppermute | solution.py:46
  641.2 24.6 %collective-permute-start.79 = (bf16[128,2048]{1,0:T(8,128)(2,1)}, bf16[128,2048]{1,0:T(8,128)(2,1)}, u32[]{:S(2)}, u32[]{:S(2)}) collective-permute-start(bf16[128,2048]{1,0:T(8,128)(2,1)} %slice.530), channel_id=1, source_target_pairs={{0,8},{4,12},{8,0},{12,4},{16,24},{20,28},{24,16},{28,20},{1,9},{5... | collective-permute-start | bytes 1572872 | tf_op jit(solution)/shard_map/ppermute | solution.py:46
  650.7 26.3 %collective-permute-start.81 = (bf16[128,2048]{1,0:T(8,128)(2,1)}, bf16[128,2048]{1,0:T(8,128)(2,1)}, u32[]{:S(2)}, u32[]{:S(2)}) collective-permute-start(bf16[128,2048]{1,0:T(8,128)(2,1)} %fusion.29), channel_id=1, source_target_pairs={{0,8},{4,12},{8,0},{12,4},{16,24},{20,28},{24,16},{28,20},{1,9},{5... | collective-permute-start | bytes 1572872 | tf_op jit(solution)/shard_map/ppermute | solution.py:46
  655.3 21.7 %collective-permute-start.83 = (bf16[128,2048]{1,0:T(8,128)(2,1)}, bf16[128,2048]{1,0:T(8,128)(2,1)}, u32[]{:S(2)}, u32[]{:S(2)}) collective-permute-start(bf16[128,2048]{1,0:T(8,128)(2,1)} %fusion.28), channel_id=1, source_target_pairs={{0,16},{4,20},{8,24},{12,28},{16,0},{20,4},{24,8},{28,12},{1,17},{... | collective-permute-start | bytes 1572872 | tf_op jit(solution)/shard_map/ppermute | solution.py:46
  655.9 27.0 %collective-permute-start.84 = (bf16[128,2048]{1,0:T(8,128)(2,1)S(1)}, bf16[128,2048]{1,0:T(8,128)(2,1)}, u32[]{:S(2)}, u32[]{:S(2)}) collective-permute-start(bf16[128,2048]{1,0:T(8,128)(2,1)S(1)} %slice.529), channel_id=1, source_target_pairs={{0,16},{4,20},{8,24},{12,28},{16,0},{20,4},{24,8},{28,12},{1,17},{... | collective-permute-start | bytes 1572872 | tf_op jit(solution)/shard_map/ppermute | solution.py:46
  660.3 34.4 %all-to-all-start.3 = ((bf16[8,64,320]{2,1,0:T(8,128)(2,1)}), bf16[8,64,320]{2,1,0:T(8,128)(2,1)S(1)}, u32[]{:S(2)}, u32[]{:S(2)}) async-start(bf16[8,64,320]{2,1,0:T(8,128)(2,1)} %bitcast.326), calls=%async_computation.7 | async-start | bytes 786432 | tf_op jit(solution)/shard_map/all_to_all | solution.py:757
  (177 other events, 2173.7 us)
Sparse Core Ops, SparseCore 0:
  13.8 32.0 all-gather.10
  55.9 44.5 all-gather.14
  102.6 39.3 all-gather.16
  144.1 66.3 all-gather.18
  212.5 62.1 all-gather.20
  276.6 62.1 all-gather.12
  390.5 58.8 reduce-scatter.5
  451.7 112.3 reduce-scatter.7
  566.4 31.7 reduce-scatter.9
  618.5 34.0 reduce-scatter.11
  657.5 37.8 reduce-scatter.13

commit v3 on v2

--- a/solution.py
+++ b/solution.py
@@ -88,22 +88,22 @@
         return value
 
     after = odd(order[0])
-    for index, slot in enumerate(order):
-        if index + 1 < evens:
-            after = odd(order[index + 1])
+    for index, slot in enumerate(order[:-1]):
+        after = odd(order[index + 1])
         after = product(slot, after) + as_wide(ready[slot])
         pairs[slot] = after
     if evens != 4:
-        return [swap(as_low(pairs[slot]), "seq", 2 * slot) if slot else after for slot in order], after
-    own, near, side, far = (pairs[slot] for slot in range(4))
+        moved = [swap(as_low(pairs[slot]), "seq", 2 * slot) for slot in order[:-1]]
+        return moved + [product(0, after) + as_wide(ready[0])], moved[0]
+    near, side, far = (pairs[slot] for slot in (1, 2, 3))
     half = far.shape[0] // 2
-    far_top = swap(as_low(far[:half]), "seq", 2)
-    far_low = swap(as_low(far[half:]), "seq", 4)
-    near_top = swap(as_low(near[:half]), "seq", 2)
-    side_low = swap(as_low(side[half:]), "seq", 4)
-    near_low = swap(as_low(near[half:] + as_wide(far_low)), "seq", 2)
-    side_top = swap(as_low(side[:half] + as_wide(far_top)), "seq", 4)
-    return [own, (near_top, near_low), (side_top, side_low)], own
+    by_near = swap(as_low(jnp.concatenate([far[:half], near[:half]])), "seq", 2)
+    by_side = swap(as_low(jnp.concatenate([far[half:], side[half:]])), "seq", 4)
+    own = product(0, after) + as_wide(ready[0])
+    by_near, by_side, last = barrier((by_near, by_side, own))
+    near_low = swap(as_low(near[half:] + as_wide(by_side[:half])), "seq", 2)
+    side_top = swap(as_low(side[:half] + as_wide(by_near[:half])), "seq", 4)
+    return [last, (by_near[half:], near_low), (side_top, by_side[half:])], own
 
 
 def split_pairs(pair):
@@ -232,11 +232,15 @@
         products = []
         for weight_ref, out_ref in zip(weight_refs, refs[1:]):
             out = jnp.dot(values, weight_ref[...], preferred_element_type=jnp.float32)
-            out_ref[...] = out.reshape(count, chunk, out.shape[1])
             products.append(out)
+            if not gated:
+                out_ref[...] = out.reshape(count, chunk, out.shape[1])
         if gated:
-            out = (gelu_parts(products[0])[0] * products[1]).astype(jnp.bfloat16)
-            refs[-1][...] = out.reshape(count, chunk, out.shape[1])
+            act, bend = gelu_parts(products[0])
+            for out_ref, out in zip(
+                refs[1:], (act, products[1] * gelu_slope(products[0], bend), act * products[1])
+            ):
+                out_ref[...] = out.reshape(count, chunk, out.shape[1]).astype(out_ref.dtype)
 
     widths = [weight.shape[1] for weight in weights]
     outs = [shaped((count, rows, model), jnp.bfloat16)] + [shaped((count, rows, w)) for w in widths]
@@ -255,18 +259,16 @@
     return [out.reshape(count * rows, out.shape[2]) for out in done]
 
 
-def ff_backward(top, down_w, gate_pre, up_pre, steps=8):
+def ff_backward(top, down_w, act, bend, steps=8):
     chunk = top.shape[0] // steps
     ffw, model = down_w.shape
 
-    def kernel(top_ref, down_ref, gate_ref, up_ref, d_gate_ref, d_up_ref):
+    def kernel(top_ref, down_ref, act_ref, bend_ref, d_gate_ref, d_up_ref):
         grad = lax.dot_general(
             top_ref[...], down_ref[...], (((1,), (1,)), ((), ())), preferred_element_type=jnp.float32
         )
-        gate = gate_ref[...]
-        act, bend = gelu_parts(gate)
-        d_gate_ref[...] = (grad * up_ref[...] * gelu_slope(gate, bend)).astype(jnp.bfloat16)
-        d_up_ref[...] = (grad * act).astype(jnp.bfloat16)
+        d_gate_ref[...] = (grad * bend_ref[...]).astype(jnp.bfloat16)
+        d_up_ref[...] = (grad * act_ref[...]).astype(jnp.bfloat16)
 
     block = pl.BlockSpec((chunk, ffw), lambda i: (i, 0))
     return pl.pallas_call(
@@ -283,7 +285,7 @@
         compiler_params=pltpu.CompilerParams(vmem_limit_bytes=VMEM_LIMIT),
         cost_estimate=LIGHT,
         name="ff_backward",
-    )(top, down_w, gate_pre, up_pre)
+    )(top, down_w, act, bend)
 
 
 def project(rows, weight, name, steps=8):
@@ -329,7 +331,9 @@
     keep_ref,
     drive_ref,
     rate_ref,
-    entry_ref,
+    slope_ref,
+    into_ref,
+    bent_ref,
     sum_ref,
     ext_ref,
 ):
@@ -362,12 +366,15 @@
             rate = jax.nn.sigmoid(pre_rec[:, lanes] + vec_ref[5:6, lanes])
             entry = jax.nn.sigmoid(pre_in[:, lanes] + vec_ref[6:7, lanes])
             minus = expm1_small(rate * vec_ref[7:8, lanes])
+            twice = minus * (2.0 + minus)
+            into = jnp.sqrt(-twice) * entry
+            drive = into * low_rows[:, lanes].astype(jnp.float32)
             rate_ref[tile, at, :size] = rate
-            entry_ref[tile, at, :size] = entry
             keep_ref[tile, at, :size] = (1.0 + minus) * live[:, :size]
-            drive_ref[tile, at, :size] = (
-                jnp.sqrt(-minus * (2.0 + minus)) * entry * low_rows[:, lanes].astype(jnp.float32)
-            )
+            drive_ref[tile, at, :size] = drive
+            slope_ref[tile, at, :size] = drive + drive / twice
+            into_ref[tile, at, :size] = into
+            bent_ref[tile, at, :size] = drive * (1.0 - entry)
 
         @pl.when(first > 0)
         def _():
@@ -396,7 +403,24 @@
         sum_ref[1, tile] = state
 
 
-def lru_state_kernel(pos_ref, all_ref, keep_ref, drive_ref, ypre_ref, h_ref, hy_ref, enter_ref, line_ref):
+def lru_state_kernel(
+    pos_ref,
+    all_ref,
+    keep_ref,
+    drive_ref,
+    rate_ref,
+    slope_ref,
+    ypre_ref,
+    vec_ref,
+    hy_ref,
+    act_ref,
+    bend_ref,
+    slow_ref,
+    rec_ref,
+    line_ref,
+    h_ref,
+    ext_ref,
+):
     tiles = lane_tiles(ypre_ref.shape[1])
     turns, _, _, blocks, _ = all_ref.shape
 
@@ -412,9 +436,6 @@
 
     zero = jnp.zeros((1, LANES), jnp.float32)
     lax.fori_loop(0, turns * blocks, chain, tuple(zero for _ in tiles))
-    for tile in range(len(tiles)):
-        enter_ref[tile] = line_ref[tile, 0:blocks, :]
-
     def step(place, states):
         at = pl.ds(place, blocks, stride=BLOCK)
         after = []
@@ -431,14 +452,27 @@
         at = block_rows(index)
         for tile, (low, size) in enumerate(tiles):
             lanes = slice(low, low + size)
-            act = gelu_parts(ypre_ref[at, lanes])[0]
-            hy_ref[at, lanes] = (h_ref[tile, at, :size] * act).astype(jnp.bfloat16)
+            h_value = h_ref[tile, at, :size]
+            value = ypre_ref[at, lanes]
+            act, bend = gelu_parts(value)
+            hy_ref[at, lanes] = (h_value * act).astype(jnp.bfloat16)
+            act_ref[tile, at, :size] = act
+            bend_ref[tile, at, :size] = h_value * gelu_slope(value, bend)
+            ext_ref[7:8, :size] = line_ref[tile, pl.ds(index, 1), :size]
+            ext_ref[8 : 8 + BLOCK, :size] = h_value
+            rate = rate_ref[tile, at, :size]
+            slow = rate * (
+                keep_ref[tile, at, :size] * ext_ref[7 : 7 + BLOCK, :size]
+                + slope_ref[tile, at, :size]
+            )
+            slow_ref[tile, at, :size] = slow
+            rec_ref[tile, at, :size] = slow * (1.0 - rate) * vec_ref[7:8, lanes]
         return carry
 
     lax.fori_loop(0, blocks, block, 0)
 
 
-def lru_back(pieces, out_w, state, branch_pre, keep, steps=8):
+def lru_back(pieces, out_w, act, bend, keep, steps=8):
     count = len(pieces)
     halves, flat = piece_halves(pieces), jax.tree.leaves(pieces)
     rows, model = pieces[0].shape
@@ -449,7 +483,7 @@
 
     def kernel(*refs):
         values = joined_rows(refs[: len(flat)], halves)
-        w_ref, h_ref, ypre_ref, keep_ref, out_ref, dy_ref, dh_ref, send_ref = refs[len(flat) :]
+        w_ref, act_ref, bend_ref, keep_ref, out_ref, dy_ref, dh_ref, send_ref = refs[len(flat) :]
         here = pl.program_id(0)
         out_ref[...] = values.reshape(count, chunk, model)
         grads = lax.dot_general(
@@ -459,12 +493,9 @@
             span = pl.ds(pl.multiple_of(slot * rows + here * chunk, chunk), chunk)
             for tile, (low, size) in enumerate(tiles):
                 lanes = slice(low, low + size)
-                value = ypre_ref[slot, :, lanes]
-                act, bend = gelu_parts(value)
                 grad = grads[slot * chunk : (slot + 1) * chunk, lanes]
-                slope = gelu_slope(value, bend)
-                dy_ref[slot, :, lanes] = (grad * h_ref[tile, slot, :, :size] * slope).astype(jnp.bfloat16)
-                dh_ref[tile, span, :size] = grad * act
+                dy_ref[slot, :, lanes] = (grad * bend_ref[tile, slot, :, :size]).astype(jnp.bfloat16)
+                dh_ref[tile, span, :size] = grad * act_ref[tile, slot, :, :size]
 
         @pl.when(here == steps - 1)
         def _():
@@ -489,7 +520,7 @@
         + [
             pl.BlockSpec((width, model), lambda i: (0, 0)),
             pl.BlockSpec((depth, count, chunk, LANES), lambda i: (0, 0, i, 0)),
-            pl.BlockSpec((count, chunk, width), lambda i: (0, i, 0)),
+            pl.BlockSpec((depth, count, chunk, LANES), lambda i: (0, 0, i, 0)),
             pl.BlockSpec((depth, total, LANES), lambda i: (0, 0, 0)),
         ],
         out_specs=[
@@ -510,8 +541,8 @@
     )(
         *flat,
         out_w,
-        state.reshape(depth, count, rows, LANES),
-        branch_pre.reshape(count, rows, width),
+        act.reshape(depth, count, rows, LANES),
+        bend.reshape(depth, count, rows, LANES),
         keep,
     )
     return out.reshape(total, model), dy.reshape(total, width), dh, send
@@ -530,12 +561,10 @@
     back_ref,
     dh_ref,
     keep_ref,
-    drive_ref,
-    rate_ref,
-    entry_ref,
-    h_ref,
-    enter_ref,
-    xc_ref,
+    slow_ref,
+    bent_rec_ref,
+    into_ref,
+    bent_in_ref,
     u_ref,
     tail_ref,
     vec_ref,
@@ -596,28 +625,14 @@
         for tile, (low, size) in enumerate(tiles):
             lanes = slice(low, low + size)
             grad = g_ref[tile, at, :size]
-            rate = rate_ref[tile, at, :size]
-            entry = entry_ref[tile, at, :size]
-            decay = vec_ref[7:8, lanes]
-            minus = expm1_small(rate * decay)
-            twice = minus * (2.0 + minus)
-            ext_ref[7:8, :size] = enter_ref[tile, pl.ds(index, 1), :size]
-            ext_ref[8 : 8 + BLOCK, :size] = h_ref[tile, at, :size]
-            d_log = grad * (
-                keep_ref[tile, at, :size] * ext_ref[7 : 7 + BLOCK, :size]
-                + drive_ref[tile, at, :size] * ((1.0 + twice) / twice)
-            )
-            slow = rate * d_log
-            acc_ref[7, :, lanes] += fold_rows(slow)
-            d_rec = (decay * slow * (1.0 - rate)).astype(jnp.bfloat16)
-            scaled = grad * jnp.sqrt(-twice) * entry
-            d_in = scaled * xc_ref[at, lanes].astype(jnp.float32) * (1.0 - entry)
-            d_in = d_in.astype(jnp.bfloat16)
+            acc_ref[7, :, lanes] += fold_rows(grad * slow_ref[tile, at, :size])
+            d_rec = (grad * bent_rec_ref[tile, at, :size]).astype(jnp.bfloat16)
+            d_in = (grad * bent_in_ref[tile, at, :size]).astype(jnp.bfloat16)
             drec_ref[at, lanes] = d_rec
             din_ref[at, lanes] = d_in
             acc_ref[5, :, lanes] += fold_rows(d_rec.astype(jnp.float32))
             acc_ref[6, :, lanes] += fold_rows(d_in.astype(jnp.float32))
-            direct_ref[:, lanes] = scaled
+            direct_ref[:, lanes] = grad * into_ref[tile, at, :size]
         direct_ref[...] += lax.dot_general(
             drec_ref[at, :], rec_ref[...], contract, preferred_element_type=jnp.float32
         ) + lax.dot_general(
@@ -764,19 +779,21 @@
         return jnp.swapaxes(got, 0, 1).reshape(-1, value.shape[-1])
 
     gains = gather_small(as_low(jnp.stack([norm_gain1, norm_gain2])), "seq")
-    x_first = plane_first(tokens)
+    mix = jnp.stack([columns(w_input), columns(w_branch)], axis=1)
+    mix, own_tokens, gains = barrier((mix, tokens, gains))
+    x_first = plane_first(own_tokens)
     out_w = gather_rows(as_low(w_out))
-    mix = exchange(jnp.stack([columns(w_input), columns(w_branch)], axis=1))
-    x_even = plane_second(tokens, x_first)
-    mix, out_w, x_even = barrier((mix, out_w, x_even))
-    input_w = gather_columns(mix[:, 0])
-    branch_w = gather_columns(mix[:, 1])
-    x_pieces = plane_all(x_even)
+    mix = exchange(mix)
     params = [conv_kernel, conv_bias[None], bias_rec[None], bias_in[None], decay_param[None]]
     gains = jnp.pad(gains.reshape(2 * seq_size, chunk), ((0, 0), (0, width // z_size - chunk)))
     params = jnp.concatenate([as_low(part) for part in params] + [gains], axis=0).T
     small = jnp.concatenate([as_low(gate_rec), as_low(gate_in), params], axis=1)
     small = gather_small(small, "fsdp")
+    mix, out_w, small, x_first = barrier((mix, out_w, small, x_first))
+    x_even = plane_second(own_tokens, x_first)
+    input_w = gather_columns(mix[:, 0])
+    branch_w = gather_columns(mix[:, 1])
+    x_pieces = plane_all(x_even)
     gains = small[:, :chunk, 2 * gate_width + 8 :].reshape(z_size, chunk, seq_size, 2)
     gains = as_wide(jnp.transpose(gains, (3, 2, 0, 1)).reshape(2, model))
     gain_one, gain_two = gains[:1], gains[1:]
@@ -794,6 +811,7 @@
     top_own = as_low(live_col * as_wide(cotangent))
     x_pieces, ff, top_own = barrier((x_pieces, ff, top_own))
     ff = exchange(ff)
+    x_pieces, top_own = barrier((x_pieces, top_own))
     top_even = plane_even(top_own)
 
     normed_one, u_value = stack(x_pieces, "norm_one", gain_one, (input_w,))
@@ -813,16 +831,13 @@
     )
     gate_w = gather_columns(ff_gate)
     up_w = gather_columns(ff_up)
-    conv_low, keep, drive, rate, entry, summary = whole(
+    conv_low, keep, drive, rate, slope, into, bent_in, summary = whole(
         lru_forward_kernel,
         (live_count, first, pred),
         (u_value, tails, vectors, rec_w, in_w),
         (
             shaped((count, width), jnp.bfloat16),
-            tiled,
-            tiled,
-            tiled,
-            tiled,
+            *[tiled] * 6,
             shaped((2, tiles, blocks, LANES)),
         ),
         [pltpu.VMEM((BLOCK + 8, LANES), jnp.float32)],
@@ -831,16 +846,16 @@
     branch_pre = project(normed_one, branch_w, "branch_pre")
     summaries = spread_z(summary)
     summaries, branch_pre, top_even = barrier((summaries, branch_pre, top_even))
-    state, gated, enter = whole(
+    gated, act, bend, slow, bent_rec = whole(
         lru_state_kernel,
         (position,),
-        (summaries, keep, drive, branch_pre),
-        (
-            tiled,
-            shaped((count, width), jnp.bfloat16),
-            shaped((tiles, blocks, LANES)),
-        ),
-        [pltpu.VMEM((tiles, every, LANES), jnp.float32)],
+        (summaries, keep, drive, rate, slope, branch_pre, vectors),
+        (shaped((count, width), jnp.bfloat16), *[tiled] * 4),
+        [
+            pltpu.VMEM((tiles, every, LANES), jnp.float32),
+            pltpu.VMEM((tiles, count, LANES), jnp.float32),
+            pltpu.VMEM((BLOCK + 8, LANES), jnp.float32),
+        ],
         "lru_state",
     )
     resid_in = as_wide(tokens)
@@ -853,16 +868,17 @@
     own_two = as_low(resid_mid * scale_two * gain_two)
     two_first = plane_first(own_two)
     two_first, up_w = barrier((two_first, up_w))
-    normed_two, gate_pre, up_pre, hidden = stack(
+    normed_two, ff_act, ff_bend, hidden = stack(
         plane_all(plane_second(own_two, two_first)), "ff_forward", None, (gate_w, up_w), True
     )
-    d_gate, d_up = ff_backward(top_low, down_w, gate_pre, up_pre)
+    grad_down = mm_tn(hidden, top_low, jnp.bfloat16)
+    ff_act, ff_bend, grad_down, down_w = barrier((ff_act, ff_bend, grad_down, down_w))
+    d_gate, d_up = ff_backward(top_low, down_w, ff_act, ff_bend)
     two_parts, two_last = scatter_plane(
         slot_product((d_gate, d_up), lambda one, two: mm_nt(one, gate_w) + mm_nt(two, up_w))
     )
+    down_home = lax.psum_scatter(grad_down, "fsdp", scatter_dimension=0, tiled=True)
     late_gate, late_up, late_hidden, two_last = barrier((d_gate, d_up, hidden, two_last))
-    grad_down = mm_tn(late_hidden, top_low, jnp.bfloat16)
-    grad_down, late_gate, late_up = barrier((grad_down, late_gate, late_up))
     grad_gate = mm_tn(normed_two, late_gate, jnp.bfloat16)
     grad_up = mm_tn(normed_two, late_up, jnp.bfloat16)
 
@@ -876,9 +892,11 @@
     def own_columns(got):
         return as_wide(jnp.swapaxes(got, 0, 1).reshape(chunk, -1))
 
-    down_home = home_rows(grad_down)
     ff_pair = by_owner((grad_gate, grad_up)).reshape(z_size * seq_size * 2 * chunk, ffw)
-    two_parts, ff_pair = barrier((two_parts, ff_pair))
+    half = count // 2
+    mlp_odd = swap(mm(late_hidden[half:], down_w, jnp.bfloat16), "seq", 1)
+    mlp_pair = split_pairs(mm(late_hidden[:half], down_w) + as_wide(mlp_odd))
+    two_parts, ff_pair, mlp_pair = barrier((two_parts, ff_pair, mlp_pair))
     grad_normed_two = summed(two_parts)
     ff_home = home_rows(ff_pair)
 
@@ -897,16 +915,12 @@
         * jnp.mean(scaled_two * resid_mid, axis=-1, keepdims=True)
     )
     grad_low = as_low(grad_mid)
-    grad_low, late_hidden = barrier((grad_low, hidden))
     out_first = plane_first(grad_low)
-    half = count // 2
-    mlp_odd = swap(mm(late_hidden[half:], down_w, jnp.bfloat16), "seq", 1)
-    mlp_pair = split_pairs(mm(late_hidden[:half], down_w) + as_wide(mlp_odd))
-    out_first, mlp_pair, down_home = barrier((out_first, mlp_pair, down_home))
+    out_first, down_home = barrier((out_first, down_home))
     out_pieces = plane_all(plane_second(grad_low, out_first))
     out_pieces, mlp_pair = barrier((out_pieces, mlp_pair))
     mlp_parts = scatter_pairs(mlp_pair)
-    grad_out_low, d_branch, direct, send = lru_back(out_pieces, out_w, state, branch_pre, keep)
+    grad_out_low, d_branch, direct, send = lru_back(out_pieces, out_w, act, bend, keep)
     backs = spread_z(send)
     grad_out = mm_tn(gated, grad_out_low, jnp.bfloat16)
     backs, grad_out = barrier((backs, grad_out))
@@ -918,12 +932,10 @@
             backs,
             direct,
             keep,
-            drive,
-            rate,
-            entry,
-            state,
-            enter,
-            conv_low,
+            slow,
+            bent_rec,
+            into,
+            bent_in,
             u_value,
             tails,
             vectors,
@@ -947,13 +959,12 @@
         ],
         "lru_grad",
     )
-    du_part, heads, totals, d_rec, d_in, ff_home, mlp_parts, d_branch = barrier(
-        (du_part, heads, totals, d_rec, d_in, ff_home, mlp_parts, d_branch)
+    du_part, heads, totals, d_rec, d_in, mlp_parts, d_branch, ff_home = barrier(
+        (du_part, heads, totals, d_rec, d_in, mlp_parts, d_branch, ff_home)
     )
     grad_out, ff_home = barrier((grad_out, ff_home))
     out_home = home_rows(grad_out)
     grad_branch = mm_tn(normed_one, d_branch, jnp.bfloat16)
-    ff_got = exchange(ff_home.reshape(seq_size, 2, chunk, ffw))
     heads = edges(heads[:, 9 - TAPS :])
     full_rec, full_in = mm_tn(conv_low, d_rec), mm_tn(conv_low, d_in)
     du_part = du_part.reshape(blocks, BLOCK, width)
@@ -967,14 +978,13 @@
     )
     d_input = lax.dynamic_update_slice(du_part, patch, (0, BLOCK - 16, 0)).reshape(count, width)
     branch_pack = by_owner((grad_branch,)).reshape(z_size * seq_size * chunk, width)
-    d_input, full_rec, full_in, ff_got, branch_pack, out_home = barrier(
-        (d_input, full_rec, full_in, ff_got, branch_pack, out_home)
-    )
+    d_input, full_rec, full_in, branch_pack, ff_home, out_home = barrier(
+        (d_input, full_rec, full_in, branch_pack, ff_home, out_home)
+    )
+    ff_got = exchange(ff_home.reshape(seq_size, 2, chunk, ffw))
     branch_home = home_rows(branch_pack)
     grad_input = mm_tn(normed_one, d_input, jnp.bfloat16)
-    grad_gate_home, grad_up_home = own_columns(ff_got[:, 0]), own_columns(ff_got[:, 1])
     late_input, grad_input = barrier((d_input, grad_input))
-    grad_gain_two = gain_home(norm_gain2, ((grad_gate_home, w_gate), (grad_up_home, w_up)))
     one_parts, one_last = scatter_plane(
         slot_product(
             (d_branch, late_input), lambda one, two: mm_nt(one, branch_w) + mm_nt(two, input_w)
@@ -1023,7 +1033,10 @@
         axis=1,
     )
     pack, branch_home = barrier((pack.reshape(z_size * pack.shape[1], lanes), branch_home))
+    pack, ff_got = barrier((pack, ff_got))
     pack = home_rows(pack)
+    grad_gate_home, grad_up_home = own_columns(ff_got[:, 0]), own_columns(ff_got[:, 1])
+    grad_gain_two = gain_home(norm_gain2, ((grad_gate_home, w_gate), (grad_up_home, w_up)))
     grad_branch_home = own_columns(exchange(branch_home.reshape(seq_size, chunk, width)))
     grad_input_home = own_columns(exchange(pack[:edge, :width].reshape(seq_size, chunk, width)))
     grad_gain_one = gain_home(

time: 727 us -> 709 us (0.975)
  waiting for transfers between devices: 209 us -> 179 us
  starting transfers between devices: 93.7 us -> 80.2 us
  local copies, waits for them, and re-layouts: 84.9 us -> 92.2 us
    ppermute x85 -> x79, waiting for transfers between devices: 170 us -> 153 us  [swap(): return lax.ppermute(values, axis, [(i, i ^ flip) for i in range(count)])]
    ppermute x85 -> x79, starting transfers between devices: 73 us -> 59.3 us  [swap(): return lax.ppermute(values, axis, [(i, i ^ flip) for i in range(count)])]
    all_gather x2, waiting for transfers between devices: 14.7 us -> 1.71 us  [gather_rows(): return lax.all_gather(value, 'fsdp', axis=0, tiled=True)]
    unnamed x253 -> x271, local copies, waits for them, and re-layouts: 19.6 us -> 23.7 us
  transfers between devices with their start and end apart: 101 -> 95, of which waited for: 46 -> 36; matrix products, arithmetic and copies ran while one was open for 27% -> 32% of each run, Pallas kernels for 18% -> 20%
where the time goes in v3:
time: 709 us; the launch traced here: 699 us
  waiting for transfers between devices  179 us (25%)
  Pallas kernels  155 us (22%)
  matrix products  118 us (17%)
  local copies, waits for them, and re-layouts  92.2 us (13%)
  starting transfers between devices  80.2 us (11%)
  other arithmetic  58.3 us (8%)
  between operations  16.8 us (2%)
    ppermute x79, waiting for transfers between devices, swap(): return lax.ppermute(values, axis, [(i, i ^ flip) for i in range(count)])  153 us
    pallas_call x4, Pallas kernels, whole(): pl.pallas_call(kernel, out_shape=outs, in_specs=specs, out_specs=[pl.Bloc...  66.7 us
    ppermute x79, starting transfers between devices, swap(): return lax.ppermute(values, axis, [(i, i ^ flip) for i in range(count)])  59.3 us
    dot_general x8, matrix products, mm_tn(): lax.dot_general(left, right, (((0,), (0,)), ((), ())), preferred_element_...  53.6 us
    pallas_call x3, Pallas kernels, stack(): pl.pallas_call(kernel, grid=(steps,), in_specs=piece_specs(pieces, steps)...  41.7 us
    dot_general x32, matrix products, mm_nt(): lax.dot_general(left, right, (((1,), (1,)), ((), ())), preferred_element_...  39.4 us
    convert_element_type x20, other arithmetic, as_low(): return values.astype(jnp.bfloat16)  25.5 us
    unnamed x271, local copies, waits for them, and re-layouts  23.7 us
  transfers between devices with their start and end apart: 95, of which 36 were waited for; matrix products, arithmetic and copies ran while one was open for 32% of the time, Pallas kernels for 20%

profile of v3, /device:TPU:0, one launch (start us, length us, event | category | flops | bytes accessed | tf_op | source)
XLA Modules:
  0.0 699.0 jit_solution(4721346555808373367)
XLA Ops:
  27.0 4.2 all-to-all-start
  33.0 10.0 %collective-permute-done.3 = bf16[1,80,344]{1,2,0:T(8,128)(2,1)S(1)} collective-permute-done((bf16[1,80,344]{1,2,0:T(8,128)(2,1)S(1)}, bf16[1,80,344]{1,2,0:T(8,128)(2,1)S(1)}, u32[]{:S(2)}, u32[]{:S(2)}) %collective-permute-start.3) | collective-permute-done | bytes 55072 | tf_op jit(solution)/shard_map/ppermute | solution.py:46
  43.9 10.7 %collective-permute-done.4 = bf16[2,80,344]{1,2,0:T(8,128)(2,1)S(1)} collective-permute-done((bf16[2,80,344]{1,2,0:T(8,128)(2,1)S(1)}, bf16[2,80,344]{1,2,0:T(8,128)(2,1)S(1)}, u32[]{:S(2)}, u32[]{:S(2)}) %collective-permute-start.4) | collective-permute-done | bytes 110112 | tf_op jit(solution)/shard_map/ppermute | solution.py:46
  62.6 9.6 %collective-permute-done.7.refs_3_ = bf16[128,2048]{1,0:T(8,128)(2,1)} collective-permute-done((bf16[128,2048]{1,0:T(8,128)(2,1)S(1)}, bf16[128,2048]{1,0:T(8,128)(2,1)}, u32[]{:S(2)}, u32[]{:S(2)}) %collective-permute-start.7) | collective-permute-done | bytes 524320 | tf_op jit(solution)/shard_map/ppermute | solution.py:46
  82.2 4.3 all-to-all-start.1
  88.6 5.9 all-gather.15.cloned.1.call-done
  97.2 12.9 %norm_one.1 = (bf16[8,256,2048]{2,1,0:T(8,128)(2,1)}, f32[8,256,320]{2,1,0:T(8,128)}) custom-call(bf16[256,2048]{1,0:T(8,128)(2,1)S(1)} %copy-done.5, bf16[256,2048]{1,0:T(8,128)(2,1)S(1)} %collective-permute-done.5.refs_1_, bf16[256,2048]{1,0:T(8,128)(2,1)S(1)} %collective-permute-done.6.refs_2_, bf16[128,2048]{1,0:T(8,128)(2,1)} %collective-permute-done.7.refs_3_, ...), custom_call_target="tpu_custom_call" | custom-call | flops 1 | bytes 1 | tf_op jit(solution)/shard_map/norm_one/pallas_call | solution.py:249
  118.1 3.4 collective-permute-done.15
  130.6 19.4 %lru_forward.1 = (bf16[2048,320]{1,0:T(8,128)(2,1)S(1)}, f32[3,2048,128]{2,1,0:T(8,128)S(1)}, f32[3,2048,128]{2,1,0:T(8,128)}, f32[3,2048,128]{2,1,0:T(8,128)}, ...) custom-call(s32[16]{0:T(128)S(1)} %select_reduce_fusion.3.live_ref, ...), custom_call_target="tpu_custom_call" | custom-call | flops 1 | bytes 1 | tf_op jit(solution)/shard_map/lru_forward/pallas_call | solution.py:693
  155.2 3.6 collective-permute-done.19
  158.8 8.8 %branch_pre.1.ypre_ref = f32[2048,320]{1,0:T(8,128)S(1)} custom-call(bf16[2048,2048]{1,0:T(8,128)(2,1)} %bitcast.286, bf16[2048,320]{1,0:T(8,128)(2,1)S(1)} %bitcast.238), custom_call_target="tpu_custom_call" | custom-call | flops 2684354560 | bytes 11010048 | tf_op jit(solution)/shard_map/branch_pre/pallas_call | solution.py:298
  172.3 19.9 %lru_state.1 = (bf16[2048,320]{1,0:T(8,128)(2,1)S(1)}, f32[3,2048,128]{2,1,0:T(8,128)S(1)}, f32[3,2048,128]{2,1,0:T(8,128)}, f32[3,2048,128]{2,1,0:T(8,128)}, f32[3,2048,128]{2,1,0:T(8,128)}) custom-call(s32[64]{0:T(128)S(1)} %select_reduce_fusion.pos_ref, f32[4,2,3,16,128]{4,3,2,1,0:T(8,128)S(1)} %pad_maximum_fusion.9.all_ref, f32[3,2048,128]{2,1,0:T(8,128)} %copy-done.4, ...), custom_call_target="tpu_custom_call" | custom-call | flops 1 | bytes 1 | tf_op jit(solution)/shard_map/lru_state/pallas_call | solution.py:693
  210.5 19.3 %collective-permute-done.25 = bf16[256,2048]{1,0:T(8,128)(2,1)S(1)} collective-permute-done((bf16[256,2048]{1,0:T(8,128)(2,1)S(1)}, bf16[256,2048]{1,0:T(8,128)(2,1)S(1)}, u32[]{:S(2)}, u32[]{:S(2)}) %collective-permute-start.25) | collective-permute-done | bytes 1048608 | tf_op jit(solution)/shard_map/ppermute | solution.py:46
  239.7 8.6 %stack_top.1 = bf16[8,256,2048]{2,1,0:T(8,128)(2,1)} custom-call(bf16[256,2048]{1,0:T(8,128)(2,1)} %fusion.20.refs_0_, bf16[256,2048]{1,0:T(8,128)(2,1)} %collective-permute-done.20.refs_1_, bf16[256,2048]{1,0:T(8,128)(2,1)} %collective-permute-done.21.refs_2_, bf16[256,2048]{1,0:T(8,128)(2,1)} %collective-permute-done.22.refs_3_, ...), custom_call_target="tpu_custom_call" | custom-call | flops 1 | bytes 1 | tf_op jit(solution)/shard_map/stack_top/pallas_call | solution.py:249
  248.3 4.0 copy.174
  256.6 10.5 %all-gather.21.cloned.1.call-done = bf16[32,64,768]{2,1,0:T(8,128)(2,1)} async-done(((bf16[8,64,768]{2,1,0:T(8,128)(2,1)}), bf16[32,64,768]{2,1,0:T(8,128)(2,1)}) %all-gather.21.cloned.1.call-update) | async-done | bytes 3145744 | tf_op jit(solution)/shard_map/all_gather | solution.py:778
  267.1 4.0 copy.176
  271.1 7.1 %collective-permute-done.36.refs_2_ = bf16[256,2048]{1,0:T(8,128)(2,1)} collective-permute-done((bf16[256,2048]{1,0:T(8,128)(2,1)S(1)}, bf16[256,2048]{1,0:T(8,128)(2,1)}, u32[]{:S(2)}, u32[]{:S(2)}) %collective-permute-start.36) | collective-permute-done | bytes 1048608 | tf_op jit(solution)/shard_map/ppermute | solution.py:46
  284.0 12.1 %collective-permute-done.37.refs_3_ = bf16[128,2048]{1,0:T(8,128)(2,1)S(1)} collective-permute-done((bf16[128,2048]{1,0:T(8,128)(2,1)S(1)}, bf16[128,2048]{1,0:T(8,128)(2,1)S(1)}, u32[]{:S(2)}, u32[]{:S(2)}) %collective-permute-start.37) | collective-permute-done | bytes 524320 | tf_op jit(solution)/shard_map/ppermute | solution.py:46
  299.0 20.1 %ff_forward.1 = (bf16[8,256,2048]{2,1,0:T(8,128)(2,1)}, f32[8,256,768]{2,1,0:T(8,128)}, f32[8,256,768]{2,1,0:T(8,128)}, bf16[8,256,768]{2,1,0:T(8,128)(2,1)}) custom-call(bf16[256,2048]{1,0:T(8,128)(2,1)S(1)} %multiply_convert_fusion.1.refs_0_, bf16[256,2048]{1,0:T(8,128)(2,1)} %collective-permute-done.35.refs_1_, ...), custom_call_target="tpu_custom_call" | custom-call | flops 1 | bytes 1 | tf_op jit(solution)/shard_map/ff_forward/pallas_call | solution.py:249
  319.2 9.9 %convolution_convert_fusion.1 = bf16[768,2048]{1,0:T(8,128)(2,1)} fusion(bf16[2048,768]{1,0:T(8,128)(2,1)} %bitcast.349, bf16[2048,2048]{1,0:T(8,128)(2,1)S(1)} %bitcast.281), kind=kOutput, calls=%fused_computation.10 | convolution fusion | flops 6444023808 | bytes 14680064 | tf_op jit(solution)/shard_map/dot_general | solution.py:33
  330.8 14.9 %ff_backward.1 = (bf16[2048,768]{1,0:T(8,128)(2,1)S(1)}, bf16[2048,768]{1,0:T(8,128)(2,1)}) custom-call(bf16[2048,2048]{1,0:T(8,128)(2,1)} %bitcast.278, bf16[768,2048]{1,0:T(8,128)(2,1)} %all-gather.13.cloned.1.call-done.down_ref, f32[2048,768]{1,0:T(8,128)} %bitcast.298, f32[2048,768]{1,0:T(8,128)} %bitcast.299), custom_call_target="tpu_custom_call" | custom-call | flops 1 | bytes 1 | tf_op jit(solution)/shard_map/ff_backward/pallas_call | solution.py:274
  345.7 3.8 fusion.35
  354.5 3.6 fusion.5
  380.5 5.2 convolution_convert_fusion
  385.7 8.2 %convolution_convert_fusion.3 = bf16[2048,768]{1,0:T(8,128)(2,1)} fusion(bf16[2048,2048]{1,0:T(8,128)(2,1)S(1)} %bitcast.346, bf16[2048,768]{1,0:T(8,128)(2,1)S(1)} %copy-done.10), kind=kOutput, calls=%fused_computation.12 | convolution fusion | flops 6444023808 | bytes 14680064 | tf_op jit(solution)/shard_map/dot_general | solution.py:33
  393.9 8.3 %convolution_convert_fusion.2 = bf16[2048,768]{1,0:T(8,128)(2,1)} fusion(bf16[2048,2048]{1,0:T(8,128)(2,1)S(1)} %bitcast.347, bf16[2048,768]{1,0:T(8,128)(2,1)S(1)} %copy-done.59), kind=kOutput, calls=%fused_computation.11 | convolution fusion | flops 6444023808 | bytes 14680064 | tf_op jit(solution)/shard_map/dot_general | solution.py:33
  402.3 3.4 pad_maximum_fusion
  413.5 5.7 fusion.81
  422.4 3.6 collective-permute-done.51
  432.5 4.0 fusion.67
  437.7 22.6 %collective-permute-done.54.refs_2_ = bf16[256,2048]{1,0:T(8,128)(2,1)} collective-permute-done((bf16[256,2048]{1,0:T(8,128)(2,1)S(1)}, bf16[256,2048]{1,0:T(8,128)(2,1)}, u32[]{:S(2)}, u32[]{:S(2)}) %collective-permute-start.54) | collective-permute-done | bytes 1048608 | tf_op jit(solution)/shard_map/ppermute | solution.py:46
  465.4 9.1 %collective-permute-done.55.refs_3_ = bf16[128,2048]{1,0:T(8,128)(2,1)S(1)} collective-permute-done((bf16[128,2048]{1,0:T(8,128)(2,1)S(1)}, bf16[128,2048]{1,0:T(8,128)(2,1)S(1)}, u32[]{:S(2)}, u32[]{:S(2)}) %collective-permute-start.55) | collective-permute-done | bytes 524320 | tf_op jit(solution)/shard_map/ppermute | solution.py:46
  481.2 22.4 %lru_back.1 = (bf16[8,256,2048]{2,1,0:T(8,128)(2,1)}, bf16[8,256,320]{2,1,0:T(8,128)(2,1)}, f32[3,2048,128]{2,1,0:T(8,128)}, f32[3,16,128]{2,1,0:T(8,128)S(1)}) custom-call(bf16[256,2048]{1,0:T(8,128)(2,1)S(1)} %get-tuple-element.334.refs_0_, bf16[256,2048]{1,0:T(8,128)(2,1)} %collective-permute-done.53.refs_1_, ...), custom_call_target="tpu_custom_call" | custom-call | flops 1 | bytes 1 | tf_op jit(solution)/shard_map/lru_back/pallas_call | solution.py:516
  504.1 5.8 collective-permute-done.64
  510.0 7.5 %convolution_convert_fusion.6 = bf16[320,2048]{1,0:T(8,128)(2,1)} fusion(bf16[2048,320]{1,0:T(8,128)(2,1)S(1)} %copy-done.21, bf16[2048,2048]{1,0:T(8,128)(2,1)} %bitcast.348), kind=kOutput, calls=%fused_computation.35 | convolution fusion | flops 2685009920 | bytes 11010048 | tf_op jit(solution)/shard_map/dot_general | solution.py:33
  517.6 26.7 %lru_grad.1 = (bf16[2048,320]{1,0:T(8,128)(2,1)S(1)}, bf16[2048,320]{1,0:T(8,128)(2,1)S(1)}, bf16[2048,320]{1,0:T(8,128)(2,1)}, f32[16,8,320]{2,1,0:T(8,128)S(1)...) custom-call(s32[16]{0:T(128)S(1)} %select_reduce_fusion.3.live_ref, s32[16]{0:T(128)S(1)} %copy-done.28, ...), custom_call_target="tpu_custom_call" | custom-call | flops 1 | bytes 1 | tf_op jit(solution)/shard_map/lru_grad/pallas_call | solution.py:693
  551.8 3.4 collective-permute-start.70
  564.3 7.5 %convolution_convert_fusion.5 = bf16[2048,320]{0,1:T(8,128)(2,1)} fusion(bf16[2048,2048]{1,0:T(8,128)(2,1)} %bitcast.287, bf16[2048,320]{1,0:T(8,128)(2,1)S(1)} %bitcast.318), kind=kOutput, calls=%fused_computation.34 | convolution fusion | flops 2685009920 | bytes 11010048 | tf_op jit(solution)/shard_map/dot_general | solution.py:33
  580.8 7.5 %convolution_convert_fusion.4 = bf16[2048,320]{0,1:T(8,128)(2,1)} fusion(bf16[2048,2048]{1,0:T(8,128)(2,1)} %bitcast.288, bf16[2048,320]{1,0:T(8,128)(2,1)S(1)} %bitcast.311), kind=kOutput, calls=%fused_computation.33 | convolution fusion | flops 2685009920 | bytes 11010048 | tf_op jit(solution)/shard_map/dot_general | solution.py:33
  592.1 3.6 all-to-all-start.3
  627.6 3.8 multiply_convert_fusion
  631.4 3.5 all-to-all-start.2
  638.7 6.4 collective-permute-done.75
  645.1 9.2 %collective-permute-done.76 = bf16[256,2048]{1,0:T(8,128)(2,1)} collective-permute-done((bf16[256,2048]{1,0:T(8,128)(2,1)S(1)}, bf16[256,2048]{1,0:T(8,128)(2,1)}, u32[]{:S(2)}, u32[]{:S(2)}) %collective-permute-start.76) | collective-permute-done | bytes 1048608 | tf_op jit(solution)/shard_map/ppermute | solution.py:46
  673.6 3.4 fusion.18
  678.7 3.5 all-to-all-start.4
  685.6 4.9 all-to-all-done.4
  (664 shorter events, 262.6 us)
Async XLA Ops:
  7.2 47.6 %all-gather.11.cloned.1.call-start = ((), (), s32[]{:S(2)}) async-start(), calls=%async_computation.10 | async-start | bytes 1638400 | tf_op jit(solution)/shard_map/all_gather | solution.py:775
  21.2 33.6 %collective-permute-start.6 = (bf16[256,2048]{1,0:T(8,128)(2,1)S(1)}, bf16[256,2048]{1,0:T(8,128)(2,1)S(1)}, u32[]{:S(2)}, u32[]{:S(2)}) collective-permute-start(bf16[256,2048]{1,0:T(8,128)(2,1)S(1)} %copy-done.5), channel_id=1, source_target_pairs={{0,16},{4,20},{8,24},{12,28},{16,0},{20,4},{24,8},{28,12},{1,17},{... | collective-permute-start | bytes 3145736 | tf_op jit(solution)/shard_map/ppermute | solution.py:46
  23.3 31.5 %collective-permute-start.5 = (bf16[256,2048]{1,0:T(8,128)(2,1)S(1)}, bf16[256,2048]{1,0:T(8,128)(2,1)S(1)}, u32[]{:S(2)}, u32[]{:S(2)}) collective-permute-start(bf16[256,2048]{1,0:T(8,128)(2,1)S(1)} %copy-done.5), channel_id=1, source_target_pairs={{0,8},{4,12},{8,0},{12,4},{16,24},{20,28},{24,16},{28,20},{1,9},{5... | collective-permute-start | bytes 3145736 | tf_op jit(solution)/shard_map/ppermute | solution.py:46
  27.0 27.8 %all-to-all-start = ((bf16[8,2,64,320]{3,2,1,0:T(8,128)(2,1)}), bf16[8,2,64,320]{3,2,1,0:T(8,128)(2,1)}, u32[]{:S(2)}, u32[]{:S(2)}) async-start(bf16[8,2,64,320]{3,2,1,0:T(8,128)(2,1)} %copy.161), calls=%async_computation | async-start | bytes 1572864 | tf_op jit(solution)/shard_map/all_to_all | solution.py:772
  31.2 63.3 %all-gather.15.cloned.1.call-start = ((), (), s32[]{:S(2)}) async-start(), calls=%async_computation.17 | async-start | bytes 1966080 | tf_op jit(solution)/shard_map/all_gather | solution.py:778
  57.0 96.5 %all-gather.17.cloned.1.call-start = ((), (), s32[]{:S(2)}) async-start(), calls=%async_computation.18 | async-start | bytes 1966080 | tf_op jit(solution)/shard_map/all_gather | solution.py:778
  61.9 17.3 %collective-permute-start.9 = (bf16[256,2048]{1,0:T(8,128)(2,1)S(1)}, bf16[256,2048]{1,0:T(8,128)(2,1)}, u32[]{:S(2)}, u32[]{:S(2)}) collective-permute-start(bf16[256,2048]{1,0:T(8,128)(2,1)S(1)} %copy-done.5), channel_id=1, source_target_pairs={{0,4},{4,0},{8,12},{12,8},{16,20},{20,16},{24,28},{28,24},{1,5},{5... | collective-permute-start | bytes 3145736 | tf_op jit(solution)/shard_map/ppermute | solution.py:46
  62.0 17.3 %collective-permute-start.10 = (bf16[256,2048]{1,0:T(8,128)(2,1)S(1)}, bf16[256,2048]{1,0:T(8,128)(2,1)}, u32[]{:S(2)}, u32[]{:S(2)}) collective-permute-start(bf16[256,2048]{1,0:T(8,128)(2,1)S(1)} %collective-permute-done.5.refs_1_), channel_id=1, source_target_pairs={{0,4},{4,0},{8,12},{12,8},{16,20},{20,16},{24,28},{28,24},{1,5},{5... | collective-permute-start | bytes 3145736 | tf_op jit(solution)/shard_map/ppermute | solution.py:46
  62.5 16.8 %collective-permute-start.11 = (bf16[256,2048]{1,0:T(8,128)(2,1)S(1)}, bf16[256,2048]{1,0:T(8,128)(2,1)}, u32[]{:S(2)}, u32[]{:S(2)}) collective-permute-start(bf16[256,2048]{1,0:T(8,128)(2,1)S(1)} %collective-permute-done.6.refs_2_), channel_id=1, source_target_pairs={{0,4},{4,0},{8,12},{12,8},{16,20},{20,16},{24,28},{28,24},{1,5},{5... | collective-permute-start | bytes 3145736 | tf_op jit(solution)/shard_map/ppermute | solution.py:46
  82.2 39.7 %all-to-all-start.1 = ((bf16[8,2,64,768]{3,2,1,0:T(8,128)(2,1)}), bf16[8,2,64,768]{3,2,1,0:T(8,128)(2,1)}, u32[]{:S(2)}, u32[]{:S(2)}) async-start(bf16[8,2,64,768]{3,2,1,0:T(8,128)(2,1)} %copy.172), calls=%async_computation.1 | async-start | bytes 3145728 | tf_op jit(solution)/shard_map/all_to_all | solution.py:772
  86.5 161.8 %all-gather.19.cloned.1.call-start = ((), (), s32[]{:S(2)}) async-start(), calls=%async_computation.19 | async-start | bytes 3932160 | tf_op jit(solution)/shard_map/all_gather | solution.py:778
  124.6 142.6 %all-gather.21.cloned.1.call-start = ((), (), s32[]{:S(2)}) async-start(), calls=%async_computation.20 | async-start | bytes 3932160 | tf_op jit(solution)/shard_map/all_gather | solution.py:778
  124.8 45.4 %collective-permute-start.22 = (bf16[256,2048]{1,0:T(8,128)(2,1)}, bf16[256,2048]{1,0:T(8,128)(2,1)}, u32[]{:S(2)}, u32[]{:S(2)}) collective-permute-start(bf16[256,2048]{1,0:T(8,128)(2,1)} %fusion.20.refs_0_), channel_id=1, source_target_pairs={{0,24},{4,28},{8,16},{12,20},{16,8},{20,12},{24,0},{28,4},{1,25},{... | collective-permute-start | bytes 3145736 | tf_op jit(solution)/shard_map/ppermute | solution.py:46
  127.3 44.9 %collective-permute-start.21 = (bf16[256,2048]{1,0:T(8,128)(2,1)}, bf16[256,2048]{1,0:T(8,128)(2,1)}, u32[]{:S(2)}, u32[]{:S(2)}) collective-permute-start(bf16[256,2048]{1,0:T(8,128)(2,1)} %fusion.20.refs_0_), channel_id=1, source_target_pairs={{0,16},{4,20},{8,24},{12,28},{16,0},{20,4},{24,8},{28,12},{1,17},{... | collective-permute-start | bytes 3145736 | tf_op jit(solution)/shard_map/ppermute | solution.py:46
  127.8 44.4 %collective-permute-start.20 = (bf16[256,2048]{1,0:T(8,128)(2,1)}, bf16[256,2048]{1,0:T(8,128)(2,1)}, u32[]{:S(2)}, u32[]{:S(2)}) collective-permute-start(bf16[256,2048]{1,0:T(8,128)(2,1)} %fusion.20.refs_0_), channel_id=1, source_target_pairs={{0,8},{4,12},{8,0},{12,4},{16,24},{20,28},{24,16},{28,20},{1,9},{5... | collective-permute-start | bytes 3145736 | tf_op jit(solution)/shard_map/ppermute | solution.py:46
  197.6 133.2 %all-gather.13.cloned.1.call-start = ((), (), s32[]{:S(2)}) async-start(), calls=%async_computation.11 | async-start | bytes 3932160 | tf_op jit(solution)/shard_map/all_gather | solution.py:775
  204.6 25.2 %collective-permute-start.25 = (bf16[256,2048]{1,0:T(8,128)(2,1)S(1)}, bf16[256,2048]{1,0:T(8,128)(2,1)S(1)}, u32[]{:S(2)}, u32[]{:S(2)}) collective-permute-start(bf16[256,2048]{1,0:T(8,128)(2,1)S(1)} %pad_maximum_fusion.2), channel_id=1, source_target_pairs={{0,8},{4,12},{8,0},{12,4},{16,24},{20,28},{24,16},{28,20},{1,9},{5... | collective-permute-start | bytes 3145736 | tf_op jit(solution)/shard_map/ppermute | solution.py:46
  207.1 24.9 %collective-permute-start.27 = (bf16[256,2048]{1,0:T(8,128)(2,1)S(1)}, bf16[256,2048]{1,0:T(8,128)(2,1)S(1)}, u32[]{:S(2)}, u32[]{:S(2)}) collective-permute-start(bf16[256,2048]{1,0:T(8,128)(2,1)S(1)} %pad_maximum_fusion.3), channel_id=1, source_target_pairs={{0,16},{4,20},{8,24},{12,28},{16,0},{20,4},{24,8},{28,12},{1,17},{... | collective-permute-start | bytes 3145736 | tf_op jit(solution)/shard_map/ppermute | solution.py:46
  209.9 24.9 %collective-permute-start.31 = (bf16[256,2048]{1,0:T(8,128)(2,1)}, bf16[256,2048]{1,0:T(8,128)(2,1)S(1)}, u32[]{:S(2)}, u32[]{:S(2)}) collective-permute-start(bf16[256,2048]{1,0:T(8,128)(2,1)} %fusion.20.refs_0_), channel_id=1, source_target_pairs={{0,4},{4,0},{8,12},{12,8},{16,20},{20,16},{24,28},{28,24},{1,5},{5... | collective-permute-start | bytes 3145736 | tf_op jit(solution)/shard_map/ppermute | solution.py:46
  209.9 28.5 %collective-permute-start.32 = (bf16[256,2048]{1,0:T(8,128)(2,1)}, bf16[256,2048]{1,0:T(8,128)(2,1)}, u32[]{:S(2)}, u32[]{:S(2)}) collective-permute-start(bf16[256,2048]{1,0:T(8,128)(2,1)} %collective-permute-done.20.refs_1_), channel_id=1, source_target_pairs={{0,4},{4,0},{8,12},{12,8},{16,20},{20,16},{24,28},{28,24},{1,5},{5... | collective-permute-start | bytes 3145736 | tf_op jit(solution)/shard_map/ppermute | solution.py:46
  210.5 27.9 %collective-permute-start.33 = (bf16[256,2048]{1,0:T(8,128)(2,1)}, bf16[256,2048]{1,0:T(8,128)(2,1)}, u32[]{:S(2)}, u32[]{:S(2)}) collective-permute-start(bf16[256,2048]{1,0:T(8,128)(2,1)} %collective-permute-done.21.refs_2_), channel_id=1, source_target_pairs={{0,4},{4,0},{8,12},{12,8},{16,20},{20,16},{24,28},{28,24},{1,5},{5... | collective-permute-start | bytes 3145736 | tf_op jit(solution)/shard_map/ppermute | solution.py:46
  233.0 19.3 %collective-permute-start.30 = (bf16[128,2048]{1,0:T(8,128)(2,1)}, bf16[128,2048]{1,0:T(8,128)(2,1)}, u32[]{:S(2)}, u32[]{:S(2)}) collective-permute-start(bf16[128,2048]{1,0:T(8,128)(2,1)} %fusion.32), channel_id=1, source_target_pairs={{0,16},{4,20},{8,24},{12,28},{16,0},{20,4},{24,8},{28,12},{1,17},{... | collective-permute-start | bytes 1572872 | tf_op jit(solution)/shard_map/ppermute | solution.py:46
  235.8 16.5 %collective-permute-start.29 = (bf16[128,2048]{1,0:T(8,128)(2,1)}, bf16[128,2048]{1,0:T(8,128)(2,1)}, u32[]{:S(2)}, u32[]{:S(2)}) collective-permute-start(bf16[128,2048]{1,0:T(8,128)(2,1)} %fusion.33), channel_id=1, source_target_pairs={{0,8},{4,12},{8,0},{12,4},{16,24},{20,28},{24,16},{28,20},{1,9},{5... | collective-permute-start | bytes 1572872 | tf_op jit(solution)/shard_map/ppermute | solution.py:46
  237.8 199.8 %reduce-scatter.6.cloned.1.call-start = ((), (), s32[]{:S(2)}) async-start(), calls=%async_computation.12 | async-start | bytes 3932160 | tf_op jit(solution)/shard_map/reduce_scatter | solution.py:880
  254.4 23.7 %collective-permute-start.36 = (bf16[256,2048]{1,0:T(8,128)(2,1)S(1)}, bf16[256,2048]{1,0:T(8,128)(2,1)}, u32[]{:S(2)}, u32[]{:S(2)}) collective-permute-start(bf16[256,2048]{1,0:T(8,128)(2,1)S(1)} %multiply_convert_fusion.1.refs_0_), channel_id=1, source_target_pairs={{0,16},{4,20},{8,24},{12,28},{16,0},{20,4},{24,8},{28,12},{1,17},{... | collective-permute-start | bytes 3145736 | tf_op jit(solution)/shard_map/ppermute | solution.py:46
  255.6 23.7 %collective-permute-start.35 = (bf16[256,2048]{1,0:T(8,128)(2,1)S(1)}, bf16[256,2048]{1,0:T(8,128)(2,1)}, u32[]{:S(2)}, u32[]{:S(2)}) collective-permute-start(bf16[256,2048]{1,0:T(8,128)(2,1)S(1)} %multiply_convert_fusion.1.refs_0_), channel_id=1, source_target_pairs={{0,8},{4,12},{8,0},{12,4},{16,24},{20,28},{24,16},{28,20},{1,9},{5... | collective-permute-start | bytes 3145736 | tf_op jit(solution)/shard_map/ppermute | solution.py:46
  256.6 40.5 %collective-permute-start.39 = (bf16[256,2048]{1,0:T(8,128)(2,1)S(1)}, bf16[256,2048]{1,0:T(8,128)(2,1)}, u32[]{:S(2)}, u32[]{:S(2)}) collective-permute-start(bf16[256,2048]{1,0:T(8,128)(2,1)S(1)} %multiply_convert_fusion.1.refs_0_), channel_id=1, source_target_pairs={{0,4},{4,0},{8,12},{12,8},{16,20},{20,16},{24,28},{28,24},{1,5},{5... | collective-permute-start | bytes 3145736 | tf_op jit(solution)/shard_map/ppermute | solution.py:46
  280.3 16.8 %collective-permute-start.40 = (bf16[256,2048]{1,0:T(8,128)(2,1)}, bf16[256,2048]{1,0:T(8,128)(2,1)S(1)}, u32[]{:S(2)}, u32[]{:S(2)}) collective-permute-start(bf16[256,2048]{1,0:T(8,128)(2,1)} %collective-permute-done.35.refs_1_), channel_id=1, source_target_pairs={{0,4},{4,0},{8,12},{12,8},{16,20},{20,16},{24,28},{28,24},{1,5},{5... | collective-permute-start | bytes 3145736 | tf_op jit(solution)/shard_map/ppermute | solution.py:46
  350.9 196.5 %reduce-scatter.8.cloned.1.call-start = ((), (), s32[]{:S(2)}) async-start(), calls=%async_computation.13 | async-start | bytes 7864320 | tf_op jit(solution)/shard_map/reduce_scatter | solution.py:886
  369.4 39.4 %collective-permute-start.46 = (bf16[256,2048]{1,0:T(8,128)(2,1)}, bf16[256,2048]{1,0:T(8,128)(2,1)}, u32[]{:S(2)}, u32[]{:S(2)}) collective-permute-start(bf16[256,2048]{1,0:T(8,128)(2,1)} %pad_maximum_fusion.4), channel_id=1, source_target_pairs={{0,8},{4,12},{8,0},{12,4},{16,24},{20,28},{24,16},{28,20},{1,9},{5... | collective-permute-start | bytes 3145736 | tf_op jit(solution)/shard_map/ppermute | solution.py:46
  379.0 29.8 %collective-permute-start.48 = (bf16[256,2048]{1,0:T(8,128)(2,1)S(1)}, bf16[256,2048]{1,0:T(8,128)(2,1)S(1)}, u32[]{:S(2)}, u32[]{:S(2)}) collective-permute-start(bf16[256,2048]{1,0:T(8,128)(2,1)S(1)} %pad_maximum_fusion.5), channel_id=1, source_target_pairs={{0,16},{4,20},{8,24},{12,28},{16,0},{20,4},{24,8},{28,12},{1,17},{... | collective-permute-start | bytes 3145736 | tf_op jit(solution)/shard_map/ppermute | solution.py:46
  385.7 27.8 %collective-permute-start.52 = (bf16[1024,2048]{1,0:T(8,128)(2,1)}, bf16[1024,2048]{1,0:T(8,128)(2,1)}, u32[]{:S(2)}, u32[]{:S(2)}) collective-permute-start(bf16[1024,2048]{1,0:T(8,128)(2,1)} %convolution_convert_fusion), channel_id=1, source_target_pairs={{0,4},{4,0},{8,12},{12,8},{16,20},{20,16},{24,28},{28,24},{1,5},{5... | collective-permute-start | bytes 12582920 | tf_op jit(solution)/shard_map/ppermute | solution.py:46
  426.9 154.0 %reduce-scatter.10.cloned.1.call-start = ((), (), s32[]{:S(2)}) async-start(), calls=%async_computation.14 | async-start | bytes 1638400 | tf_op jit(solution)/shard_map/reduce_scatter | solution.py:886
  436.6 23.7 %collective-permute-start.54 = (bf16[256,2048]{1,0:T(8,128)(2,1)S(1)}, bf16[256,2048]{1,0:T(8,128)(2,1)}, u32[]{:S(2)}, u32[]{:S(2)}) collective-permute-start(bf16[256,2048]{1,0:T(8,128)(2,1)S(1)} %get-tuple-element.334.refs_0_), channel_id=1, source_target_pairs={{0,16},{4,20},{8,24},{12,28},{16,0},{20,4},{24,8},{28,12},{1,17},{... | collective-permute-start | bytes 3145736 | tf_op jit(solution)/shard_map/ppermute | solution.py:46
  437.2 24.2 %collective-permute-start.53 = (bf16[256,2048]{1,0:T(8,128)(2,1)S(1)}, bf16[256,2048]{1,0:T(8,128)(2,1)}, u32[]{:S(2)}, u32[]{:S(2)}) collective-permute-start(bf16[256,2048]{1,0:T(8,128)(2,1)S(1)} %get-tuple-element.334.refs_0_), channel_id=1, source_target_pairs={{0,8},{4,12},{8,0},{12,4},{16,24},{20,28},{24,16},{28,20},{1,9},{5... | collective-permute-start | bytes 3145736 | tf_op jit(solution)/shard_map/ppermute | solution.py:46
  437.7 38.0 %collective-permute-start.57 = (bf16[256,2048]{1,0:T(8,128)(2,1)S(1)}, bf16[256,2048]{1,0:T(8,128)(2,1)}, u32[]{:S(2)}, u32[]{:S(2)}) collective-permute-start(bf16[256,2048]{1,0:T(8,128)(2,1)S(1)} %get-tuple-element.334.refs_0_), channel_id=1, source_target_pairs={{0,4},{4,0},{8,12},{12,8},{16,20},{20,16},{24,28},{28,24},{1,5},{5... | collective-permute-start | bytes 3145736 | tf_op jit(solution)/shard_map/ppermute | solution.py:46
  477.6 69.8 %collective-permute-start.65 = (bf16[256,2048]{1,0:T(8,128)(2,1)}, bf16[256,2048]{1,0:T(8,128)(2,1)}, u32[]{:S(2)}, u32[]{:S(2)}) collective-permute-start(bf16[256,2048]{1,0:T(8,128)(2,1)} %get-tuple-element.359), channel_id=1, source_target_pairs={{0,24},{4,28},{8,16},{12,20},{16,8},{20,12},{24,0},{28,4},{1,25},{... | collective-permute-start | bytes 3145736 | tf_op jit(solution)/shard_map/ppermute | solution.py:46
  479.4 67.9 %collective-permute-start.66 = (bf16[256,2048]{1,0:T(8,128)(2,1)}, bf16[256,2048]{1,0:T(8,128)(2,1)}, u32[]{:S(2)}, u32[]{:S(2)}) collective-permute-start(bf16[256,2048]{1,0:T(8,128)(2,1)} %get-tuple-element.360), channel_id=1, source_target_pairs={{0,8},{4,12},{8,0},{12,4},{16,24},{20,28},{24,16},{28,20},{1,9},{5... | collective-permute-start | bytes 3145736 | tf_op jit(solution)/shard_map/ppermute | solution.py:46
  479.7 67.7 %collective-permute-start.67 = (bf16[256,2048]{1,0:T(8,128)(2,1)}, bf16[256,2048]{1,0:T(8,128)(2,1)}, u32[]{:S(2)}, u32[]{:S(2)}) collective-permute-start(bf16[256,2048]{1,0:T(8,128)(2,1)} %get-tuple-element.361), channel_id=1, source_target_pairs={{0,16},{4,20},{8,24},{12,28},{16,0},{20,4},{24,8},{28,12},{1,17},{... | collective-permute-start | bytes 3145736 | tf_op jit(solution)/shard_map/ppermute | solution.py:46
  547.4 84.0 %reduce-scatter.12.cloned.1.call-start = ((), (), s32[]{:S(2)}) async-start(), calls=%async_computation.15 | async-start | bytes 1966080 | tf_op jit(solution)/shard_map/reduce_scatter | solution.py:886
  551.8 25.0 %collective-permute-start.70 = (bf16[48,320]{1,0:T(8,128)(2,1)S(1)}, bf16[48,320]{1,0:T(8,128)(2,1)S(1)}, u32[]{:S(2)}, u32[]{:S(2)}) collective-permute-start(bf16[48,320]{1,0:T(8,128)(2,1)S(1)} %reshape.425), channel_id=1, source_target_pairs={{0,3},{1,2},{2,1},{3,0},{4,7},{5,6},{6,5},{7,4},{8,11},{9,10},{10,... | collective-permute-start | bytes 92168 | tf_op jit(solution)/shard_map/ppermute | solution.py:46
  555.2 21.5 %collective-permute-start.69 = (bf16[48,320]{1,0:T(8,128)(2,1)S(1)}, bf16[48,320]{1,0:T(8,128)(2,1)S(1)}, u32[]{:S(2)}, u32[]{:S(2)}) collective-permute-start(bf16[48,320]{1,0:T(8,128)(2,1)S(1)} %reshape.425), channel_id=1, source_target_pairs={{0,2},{1,3},{2,0},{3,1},{4,6},{5,7},{6,4},{7,5},{8,10},{9,11},{10,... | collective-permute-start | bytes 92168 | tf_op jit(solution)/shard_map/ppermute | solution.py:46
  555.4 21.3 %collective-permute-start.68 = (bf16[48,320]{1,0:T(8,128)(2,1)S(1)}, bf16[48,320]{1,0:T(8,128)(2,1)S(1)}, u32[]{:S(2)}, u32[]{:S(2)}) collective-permute-start(bf16[48,320]{1,0:T(8,128)(2,1)S(1)} %reshape.425), channel_id=1, source_target_pairs={{0,1},{1,0},{2,3},{3,2},{4,5},{5,4},{6,7},{7,6},{8,9},{9,8},{10,11... | collective-permute-start | bytes 92168 | tf_op jit(solution)/shard_map/ppermute | solution.py:46
  592.1 39.3 %all-to-all-start.3 = ((bf16[8,2,64,768]{3,2,1,0:T(8,128)(2,1)}), bf16[8,2,64,768]{3,2,1,0:T(8,128)(2,1)S(1)}, u32[]{:S(2)}, u32[]{:S(2)}) async-start(bf16[8,2,64,768]{3,2,1,0:T(8,128)(2,1)} %bitcast.319), calls=%async_computation.7 | async-start | bytes 3145728 | tf_op jit(solution)/shard_map/all_to_all | solution.py:772
  595.7 81.2 %reduce-scatter.14.cloned.1.call-start = ((), (), s32[]{:S(2)}) async-start(), calls=%async_computation.16 | async-start | bytes 2334720 | tf_op jit(solution)/shard_map/reduce_scatter | solution.py:886
  618.8 26.3 %collective-permute-start.75 = (bf16[256,2048]{1,0:T(8,128)(2,1)}, bf16[256,2048]{1,0:T(8,128)(2,1)}, u32[]{:S(2)}, u32[]{:S(2)}) collective-permute-start(bf16[256,2048]{1,0:T(8,128)(2,1)} %pad_maximum_fusion.6), channel_id=1, source_target_pairs={{0,8},{4,12},{8,0},{12,4},{16,24},{20,28},{24,16},{28,20},{1,9},{5... | collective-permute-start | bytes 3145736 | tf_op jit(solution)/shard_map/ppermute | solution.py:46
  626.0 28.3 %collective-permute-start.76 = (bf16[256,2048]{1,0:T(8,128)(2,1)S(1)}, bf16[256,2048]{1,0:T(8,128)(2,1)}, u32[]{:S(2)}, u32[]{:S(2)}) collective-permute-start(bf16[256,2048]{1,0:T(8,128)(2,1)S(1)} %pad_maximum_fusion.7), channel_id=1, source_target_pairs={{0,16},{4,20},{8,24},{12,28},{16,0},{20,4},{24,8},{28,12},{1,17},{... | collective-permute-start | bytes 3145736 | tf_op jit(solution)/shard_map/ppermute | solution.py:46
  631.4 29.4 %all-to-all-start.2 = ((bf16[8,64,320]{2,1,0:T(8,128)(2,1)}), bf16[8,64,320]{2,1,0:T(8,128)(2,1)S(1)}, u32[]{:S(2)}, u32[]{:S(2)}) async-start(bf16[8,64,320]{2,1,0:T(8,128)(2,1)} %bitcast.327), calls=%async_computation.6 | async-start | bytes 786432 | tf_op jit(solution)/shard_map/all_to_all | solution.py:772
  (182 other events, 1378.4 us)
Sparse Core Ops, SparseCore 0:
  10.2 36.2 all-gather.10
  57.1 37.3 all-gather.14
  96.6 39.1 all-gather.16
  137.2 66.3 all-gather.18
  205.0 62.1 all-gather.20
  268.6 62.1 all-gather.12
  351.0 58.8 reduce-scatter.5
  427.0 109.5 reduce-scatter.7
  547.5 33.2 reduce-scatter.9
  592.3 34.6 reduce-scatter.11
  631.6 39.0 reduce-scatter.13

commit v4 on v3

--- a/solution.py
+++ b/solution.py
@@ -229,20 +229,19 @@
             values = (wide * scale * gain_ref[...]).astype(jnp.bfloat16)
         weight_refs, refs = refs[: len(weights)], refs[len(weights) :]
         refs[0][...] = values.reshape(count, chunk, model)
-        products = []
         for weight_ref, out_ref in zip(weight_refs, refs[1:]):
             out = jnp.dot(values, weight_ref[...], preferred_element_type=jnp.float32)
-            products.append(out)
             if not gated:
                 out_ref[...] = out.reshape(count, chunk, out.shape[1])
         if gated:
-            act, bend = gelu_parts(products[0])
-            for out_ref, out in zip(
-                refs[1:], (act, products[1] * gelu_slope(products[0], bend), act * products[1])
-            ):
+            gate, up = out[:, : out.shape[1] // 2], out[:, out.shape[1] // 2 :]
+            act, bend = gelu_parts(gate)
+            for out_ref, out in zip(refs[1:], (act, up * gelu_slope(gate, bend), act * up)):
                 out_ref[...] = out.reshape(count, chunk, out.shape[1]).astype(out_ref.dtype)
 
     widths = [weight.shape[1] for weight in weights]
+    if gated:
+        widths = [widths[0] // 2] * 2
     outs = [shaped((count, rows, model), jnp.bfloat16)] + [shaped((count, rows, w)) for w in widths]
     if gated:
         outs.append(shaped((count, rows, widths[0]), jnp.bfloat16))
@@ -263,12 +262,12 @@
     chunk = top.shape[0] // steps
     ffw, model = down_w.shape
 
-    def kernel(top_ref, down_ref, act_ref, bend_ref, d_gate_ref, d_up_ref):
+    def kernel(top_ref, down_ref, act_ref, bend_ref, out_ref):
         grad = lax.dot_general(
             top_ref[...], down_ref[...], (((1,), (1,)), ((), ())), preferred_element_type=jnp.float32
         )
-        d_gate_ref[...] = (grad * bend_ref[...]).astype(jnp.bfloat16)
-        d_up_ref[...] = (grad * act_ref[...]).astype(jnp.bfloat16)
+        out_ref[:, :ffw] = (grad * bend_ref[...]).astype(jnp.bfloat16)
+        out_ref[:, ffw:] = (grad * act_ref[...]).astype(jnp.bfloat16)
 
     block = pl.BlockSpec((chunk, ffw), lambda i: (i, 0))
     return pl.pallas_call(
@@ -280,8 +279,8 @@
             block,
             block,
         ],
-        out_specs=[block, block],
-        out_shape=[shaped((top.shape[0], ffw), jnp.bfloat16)] * 2,
+        out_specs=pl.BlockSpec((chunk, 2 * ffw), lambda i: (i, 0)),
+        out_shape=shaped((top.shape[0], 2 * ffw), jnp.bfloat16),
         compiler_params=pltpu.CompilerParams(vmem_limit_bytes=VMEM_LIMIT),
         cost_estimate=LIGHT,
         name="ff_backward",
@@ -807,7 +806,7 @@
     vectors = as_wide(small[:, 2 * gate_width : 2 * gate_width + 8]).T
     decay = vectors[7]
     vectors = jnp.concatenate([vectors[:7], -GATE_SCALE * jax.nn.softplus(-decay)[None]], axis=0)
-    ff = jnp.stack([columns(w_gate), columns(w_up)], axis=1)
+    ff = jnp.concatenate([columns(w_gate), columns(w_up)], axis=2)
     top_own = as_low(live_col * as_wide(cotangent))
     x_pieces, ff, top_own = barrier((x_pieces, ff, top_own))
     ff = exchange(ff)
@@ -826,11 +825,8 @@
         return jnp.pad(rows, ((0, 0), (9 - TAPS, 0), (0, 0)))
 
     tails = edges(u_value.reshape(blocks, BLOCK, width)[:, BLOCK - TAPS + 1 :])
-    tails, rec_w, in_w, vectors, ff_gate, ff_up = barrier(
-        (tails, rec_w, in_w, vectors, ff[:, 0], ff[:, 1])
-    )
-    gate_w = gather_columns(ff_gate)
-    up_w = gather_columns(ff_up)
+    tails, rec_w, in_w, vectors, ff = barrier((tails, rec_w, in_w, vectors, ff))
+    ff_w = gather_columns(ff)
     conv_low, keep, drive, rate, slope, into, bent_in, summary = whole(
         lru_forward_kernel,
         (live_count, first, pred),
@@ -862,25 +858,24 @@
     mid_parts, mid_last = scatter_plane(slot_product((gated,), lambda rows: mm(rows, out_w)))
     top_even, mid_last = barrier((top_even, mid_last))
     (top_low,) = stack(plane_all(top_even), "stack_top")
-    mid_parts, top_low, gate_w = barrier((mid_parts, top_low, gate_w))
+    mid_parts, top_low = barrier((mid_parts, top_low))
     resid_mid = resid_in + summed(mid_parts)
     scale_two = lax.rsqrt(jnp.mean(resid_mid * resid_mid, axis=-1, keepdims=True) + NORM_EPSILON)
     own_two = as_low(resid_mid * scale_two * gain_two)
     two_first = plane_first(own_two)
-    two_first, up_w = barrier((two_first, up_w))
+    two_first, ff_w = barrier((two_first, ff_w))
     normed_two, ff_act, ff_bend, hidden = stack(
-        plane_all(plane_second(own_two, two_first)), "ff_forward", None, (gate_w, up_w), True
+        plane_all(plane_second(own_two, two_first)), "ff_forward", None, (ff_w,), True
     )
     grad_down = mm_tn(hidden, top_low, jnp.bfloat16)
     ff_act, ff_bend, grad_down, down_w = barrier((ff_act, ff_bend, grad_down, down_w))
-    d_gate, d_up = ff_backward(top_low, down_w, ff_act, ff_bend)
+    d_ff = ff_backward(top_low, down_w, ff_act, ff_bend)
     two_parts, two_last = scatter_plane(
-        slot_product((d_gate, d_up), lambda one, two: mm_nt(one, gate_w) + mm_nt(two, up_w))
+        slot_product((d_ff,), lambda rows: mm_nt(rows, ff_w))
     )
     down_home = lax.psum_scatter(grad_down, "fsdp", scatter_dimension=0, tiled=True)
-    late_gate, late_up, late_hidden, two_last = barrier((d_gate, d_up, hidden, two_last))
-    grad_gate = mm_tn(normed_two, late_gate, jnp.bfloat16)
-    grad_up = mm_tn(normed_two, late_up, jnp.bfloat16)
+    late_ff, late_hidden, two_last = barrier((d_ff, hidden, two_last))
+    grad_ff = mm_tn(normed_two, late_ff, jnp.bfloat16)
 
     def home_rows(value):
         return lax.psum_scatter(value, "fsdp", scatter_dimension=0, tiled=True)
@@ -892,7 +887,7 @@
     def own_columns(got):
         return as_wide(jnp.swapaxes(got, 0, 1).reshape(chunk, -1))
 
-    ff_pair = by_owner((grad_gate, grad_up)).reshape(z_size * seq_size * 2 * chunk, ffw)
+    ff_pair = by_owner((grad_ff,)).reshape(z_size * seq_size * chunk, 2 * ffw)
     half = count // 2
     mlp_odd = swap(mm(late_hidden[half:], down_w, jnp.bfloat16), "seq", 1)
     mlp_pair = split_pairs(mm(late_hidden[:half], down_w) + as_wide(mlp_odd))
@@ -981,7 +976,7 @@
     d_input, full_rec, full_in, branch_pack, ff_home, out_home = barrier(
         (d_input, full_rec, full_in, branch_pack, ff_home, out_home)
     )
-    ff_got = exchange(ff_home.reshape(seq_size, 2, chunk, ffw))
+    ff_got = exchange(ff_home.reshape(seq_size, chunk, 2 * ffw))
     branch_home = home_rows(branch_pack)
     grad_input = mm_tn(normed_one, d_input, jnp.bfloat16)
     late_input, grad_input = barrier((d_input, grad_input))
@@ -1035,7 +1030,7 @@
     pack, branch_home = barrier((pack.reshape(z_size * pack.shape[1], lanes), branch_home))
     pack, ff_got = barrier((pack, ff_got))
     pack = home_rows(pack)
-    grad_gate_home, grad_up_home = own_columns(ff_got[:, 0]), own_columns(ff_got[:, 1])
+    grad_gate_home, grad_up_home = own_columns(ff_got[..., :ffw]), own_columns(ff_got[..., ffw:])
     grad_gain_two = gain_home(norm_gain2, ((grad_gate_home, w_gate), (grad_up_home, w_up)))
     grad_branch_home = own_columns(exchange(branch_home.reshape(seq_size, chunk, width)))
     grad_input_home = own_columns(exchange(pack[:edge, :width].reshape(seq_size, chunk, width)))

time: 709 us -> 689 us (0.972)
  matrix products: 118 us -> 104 us
    dot_general x32 -> x24, matrix products: 39.4 us -> 35.2 us  [mm_nt(): lax.dot_general(left, right, (((1,), (1,)), ((), ())), preferred_element_...]
    dot_general x8 -> x7, matrix products: 53.6 us -> 49.8 us  [mm_tn(): lax.dot_general(left, right, (((0,), (0,)), ((), ())), preferred_element_...]
    unnamed x271 -> x209, local copies, waits for them, and re-layouts: 23.7 us -> 26.8 us
    all_gather x4 -> x3, waiting for transfers between devices: 16.4 us -> 14.4 us  [gather_columns(): got = lax.all_gather(value, 'fsdp', axis=0, tiled=False)]
  transfers between devices with their start and end apart: 95 -> 94, of which waited for: 36 -> 40; matrix products, arithmetic and copies ran while one was open for 32% -> 30% of each run, Pallas kernels for 20% -> 23%
where the time goes in v4:
time: 689 us; the launch traced here: 680 us
  waiting for transfers between devices  177 us (26%)
  Pallas kernels  155 us (22%)
  matrix products  104 us (15%)
  local copies, waits for them, and re-layouts  87.4 us (13%)
  starting transfers between devices  84.4 us (12%)
  other arithmetic  55.1 us (8%)
  between operations  16.5 us (2%)
    ppermute x79, waiting for transfers between devices, swap(): return lax.ppermute(values, axis, [(i, i ^ flip) for i in range(count)])  151 us
    pallas_call x4, Pallas kernels, whole(): pl.pallas_call(kernel, out_shape=outs, in_specs=specs, out_specs=[pl.Bloc...  67.4 us
    ppermute x79, starting transfers between devices, swap(): return lax.ppermute(values, axis, [(i, i ^ flip) for i in range(count)])  64.2 us
    dot_general x7, matrix products, mm_tn(): lax.dot_general(left, right, (((0,), (0,)), ((), ())), preferred_element_...  49.8 us
    pallas_call x3, Pallas kernels, stack(): pl.pallas_call(kernel, grid=(steps,), in_specs=piece_specs(pieces, steps)...  41.6 us
    dot_general x24, matrix products, mm_nt(): lax.dot_general(left, right, (((1,), (1,)), ((), ())), preferred_element_...  35.2 us
    unnamed x209, local copies, waits for them, and re-layouts  26.8 us
    convert_element_type x20, other arithmetic, as_low(): return values.astype(jnp.bfloat16)  25.1 us
  transfers between devices with their start and end apart: 94, of which 40 were waited for; matrix products, arithmetic and copies ran while one was open for 30% of the time, Pallas kernels for 23%

profile of v4, /device:TPU:0, one launch (start us, length us, event | category | flops | bytes accessed | tf_op | source)
XLA Modules:
  0.0 679.5 jit_solution(4093659356170457909)
XLA Ops:
  27.0 4.2 all-to-all-start
  33.0 10.0 %collective-permute-done.3 = bf16[1,80,344]{1,2,0:T(8,128)(2,1)S(1)} collective-permute-done((bf16[1,80,344]{1,2,0:T(8,128)(2,1)S(1)}, bf16[1,80,344]{1,2,0:T(8,128)(2,1)S(1)}, u32[]{:S(2)}, u32[]{:S(2)}) %collective-permute-start.3) | collective-permute-done | bytes 55072 | tf_op jit(solution)/shard_map/ppermute | solution.py:46
  43.9 10.7 %collective-permute-done.4 = bf16[2,80,344]{1,2,0:T(8,128)(2,1)S(1)} collective-permute-done((bf16[2,80,344]{1,2,0:T(8,128)(2,1)S(1)}, bf16[2,80,344]{1,2,0:T(8,128)(2,1)S(1)}, u32[]{:S(2)}, u32[]{:S(2)}) %collective-permute-start.4) | collective-permute-done | bytes 110112 | tf_op jit(solution)/shard_map/ppermute | solution.py:46
  63.8 9.1 %collective-permute-done.7.refs_3_ = bf16[128,2048]{1,0:T(8,128)(2,1)} collective-permute-done((bf16[128,2048]{1,0:T(8,128)(2,1)S(1)}, bf16[128,2048]{1,0:T(8,128)(2,1)}, u32[]{:S(2)}, u32[]{:S(2)}) %collective-permute-start.7) | collective-permute-done | bytes 524320 | tf_op jit(solution)/shard_map/ppermute | solution.py:46
  80.7 4.3 all-to-all-start.1
  88.1 6.3 all-gather.13.cloned.1.call-done
  97.2 13.0 %norm_one.1 = (bf16[8,256,2048]{2,1,0:T(8,128)(2,1)}, f32[8,256,320]{2,1,0:T(8,128)}) custom-call(bf16[256,2048]{1,0:T(8,128)(2,1)S(1)} %copy-done.5, bf16[256,2048]{1,0:T(8,128)(2,1)S(1)} %collective-permute-done.5.refs_1_, bf16[256,2048]{1,0:T(8,128)(2,1)S(1)} %collective-permute-done.6.refs_2_, bf16[128,2048]{1,0:T(8,128)(2,1)} %collective-permute-done.7.refs_3_, ...), custom_call_target="tpu_custom_call" | custom-call | flops 1 | bytes 1 | tf_op jit(solution)/shard_map/norm_one/pallas_call | solution.py:248
  118.1 3.5 collective-permute-done.15
  127.9 20.2 %lru_forward.1 = (bf16[2048,320]{1,0:T(8,128)(2,1)S(1)}, f32[3,2048,128]{2,1,0:T(8,128)S(1)}, f32[3,2048,128]{2,1,0:T(8,128)}, f32[3,2048,128]{2,1,0:T(8,128)}, ...) custom-call(s32[16]{0:T(128)S(1)} %select_reduce_fusion.3.live_ref, ...), custom_call_target="tpu_custom_call" | custom-call | flops 1 | bytes 1 | tf_op jit(solution)/shard_map/lru_forward/pallas_call | solution.py:692
  152.6 4.1 collective-permute-done.19
  158.2 8.7 %branch_pre.1.ypre_ref = f32[2048,320]{1,0:T(8,128)S(1)} custom-call(bf16[2048,2048]{1,0:T(8,128)(2,1)} %bitcast.243, bf16[2048,320]{1,0:T(8,128)(2,1)S(1)} %bitcast.202), custom_call_target="tpu_custom_call" | custom-call | flops 2684354560 | bytes 11010048 | tf_op jit(solution)/shard_map/branch_pre/pallas_call | solution.py:297
  169.5 19.7 %lru_state.1 = (bf16[2048,320]{1,0:T(8,128)(2,1)S(1)}, f32[3,2048,128]{2,1,0:T(8,128)S(1)}, f32[3,2048,128]{2,1,0:T(8,128)}, f32[3,2048,128]{2,1,0:T(8,128)}, f32[3,2048,128]{2,1,0:T(8,128)}) custom-call(s32[64]{0:T(128)S(1)} %select_reduce_fusion.pos_ref, f32[4,2,3,16,128]{4,3,2,1,0:T(8,128)S(1)} %pad_maximum_fusion.8.all_ref, f32[3,2048,128]{2,1,0:T(8,128)} %copy-done.4, ...), custom_call_target="tpu_custom_call" | custom-call | flops 1 | bytes 1 | tf_op jit(solution)/shard_map/lru_state/pallas_call | solution.py:692
  203.3 19.0 %collective-permute-done.25 = bf16[256,2048]{1,0:T(8,128)(2,1)S(1)} collective-permute-done((bf16[256,2048]{1,0:T(8,128)(2,1)S(1)}, bf16[256,2048]{1,0:T(8,128)(2,1)S(1)}, u32[]{:S(2)}, u32[]{:S(2)}) %collective-permute-start.25) | collective-permute-done | bytes 1048608 | tf_op jit(solution)/shard_map/ppermute | solution.py:46
  232.0 8.7 %stack_top.1 = bf16[8,256,2048]{2,1,0:T(8,128)(2,1)} custom-call(bf16[256,2048]{1,0:T(8,128)(2,1)} %fusion.12.refs_0_, bf16[256,2048]{1,0:T(8,128)(2,1)} %collective-permute-done.20.refs_1_, bf16[256,2048]{1,0:T(8,128)(2,1)} %collective-permute-done.21.refs_2_, bf16[256,2048]{1,0:T(8,128)(2,1)} %collective-permute-done.22.refs_3_, ...), custom_call_target="tpu_custom_call" | custom-call | flops 1 | bytes 1 | tf_op jit(solution)/shard_map/stack_top/pallas_call | solution.py:248
  246.9 8.1 %all-gather.17.cloned.1.call-done = bf16[32,64,1536]{2,1,0:T(8,128)(2,1)} async-done(((bf16[8,64,1536]{2,1,0:T(8,128)(2,1)}), bf16[32,64,1536]{2,1,0:T(8,128)(2,1)}) %all-gather.17.cloned.1.call-update) | async-done | bytes 6291472 | tf_op jit(solution)/shard_map/all_gather | solution.py:777
  255.0 6.1 copy.164
  261.1 7.3 %collective-permute-done.36.refs_2_ = bf16[256,2048]{1,0:T(8,128)(2,1)} collective-permute-done((bf16[256,2048]{1,0:T(8,128)(2,1)S(1)}, bf16[256,2048]{1,0:T(8,128)(2,1)}, u32[]{:S(2)}, u32[]{:S(2)}) %collective-permute-start.36) | collective-permute-done | bytes 1048608 | tf_op jit(solution)/shard_map/ppermute | solution.py:46
  274.6 7.7 %collective-permute-done.37.refs_3_ = bf16[128,2048]{1,0:T(8,128)(2,1)S(1)} collective-permute-done((bf16[128,2048]{1,0:T(8,128)(2,1)S(1)}, bf16[128,2048]{1,0:T(8,128)(2,1)S(1)}, u32[]{:S(2)}, u32[]{:S(2)}) %collective-permute-start.37) | collective-permute-done | bytes 524320 | tf_op jit(solution)/shard_map/ppermute | solution.py:46
  286.7 20.0 %ff_forward.1 = (bf16[8,256,2048]{2,1,0:T(8,128)(2,1)}, f32[8,256,768]{2,1,0:T(8,128)}, f32[8,256,768]{2,1,0:T(8,128)}, bf16[8,256,768]{2,1,0:T(8,128)(2,1)}) custom-call(bf16[256,2048]{1,0:T(8,128)(2,1)S(1)} %multiply_convert_fusion.1.refs_0_, bf16[256,2048]{1,0:T(8,128)(2,1)} %collective-permute-done.35.refs_1_, ...), custom_call_target="tpu_custom_call" | custom-call | flops 1 | bytes 1 | tf_op jit(solution)/shard_map/ff_forward/pallas_call | solution.py:248
  306.7 9.6 %convolution_convert_fusion.2 = bf16[768,2048]{1,0:T(8,128)(2,1)} fusion(bf16[2048,768]{1,0:T(8,128)(2,1)} %bitcast.298, bf16[2048,2048]{1,0:T(8,128)(2,1)S(1)} %bitcast.227), kind=kOutput, calls=%fused_computation.10 | convolution fusion | flops 6444023808 | bytes 14680064 | tf_op jit(solution)/shard_map/dot_general | solution.py:33
  321.0 14.6 %ff_backward.1 = bf16[2048,1536]{1,0:T(8,128)(2,1)} custom-call(bf16[2048,2048]{1,0:T(8,128)(2,1)} %bitcast.224, bf16[768,2048]{1,0:T(8,128)(2,1)S(1)} %copy-done.9, f32[2048,768]{1,0:T(8,128)} %bitcast.257, f32[2048,768]{1,0:T(8,128)} %bitcast.258), custom_call_target="tpu_custom_call" | custom-call | flops 1 | bytes 1 | tf_op jit(solution)/shard_map/ff_backward/pallas_call | solution.py:273
  335.6 5.1 convolution_convert_fusion.9
  355.1 3.1 convolution_add_fusion.12
  358.3 5.2 convolution_convert_fusion.1
  366.8 15.5 %convolution_convert_fusion = bf16[2048,1536]{1,0:T(8,128)(2,1)S(1)} fusion(bf16[2048,2048]{1,0:T(8,128)(2,1)} %bitcast.296, bf16[2048,1536]{1,0:T(8,128)(2,1)S(1)} %copy-done.32), kind=kOutput, calls=%fused_computation.2 | convolution fusion | flops 12888047616 | bytes 20971520 | tf_op jit(solution)/shard_map/dot_general | solution.py:33
  382.3 3.4 copy.165
  385.7 3.6 collective-permute-done.46
  397.7 5.4 fusion.70
  410.2 3.2 multiply_reduce_fusion
  415.3 4.0 fusion.57
  419.9 22.0 %collective-permute-done.54.refs_2_ = bf16[256,2048]{1,0:T(8,128)(2,1)} collective-permute-done((bf16[256,2048]{1,0:T(8,128)(2,1)S(1)}, bf16[256,2048]{1,0:T(8,128)(2,1)}, u32[]{:S(2)}, u32[]{:S(2)}) %collective-permute-start.54) | collective-permute-done | bytes 1048608 | tf_op jit(solution)/shard_map/ppermute | solution.py:46
  446.8 6.7 collective-permute-done.55.refs_3_
  460.1 22.6 %lru_back.1 = (bf16[8,256,2048]{2,1,0:T(8,128)(2,1)}, bf16[8,256,320]{2,1,0:T(8,128)(2,1)}, f32[3,2048,128]{2,1,0:T(8,128)}, f32[3,16,128]{2,1,0:T(8,128)S(1)}) custom-call(bf16[256,2048]{1,0:T(8,128)(2,1)S(1)} %get-tuple-element.310.refs_0_, bf16[256,2048]{1,0:T(8,128)(2,1)} %collective-permute-done.53.refs_1_, ...), custom_call_target="tpu_custom_call" | custom-call | flops 1 | bytes 1 | tf_op jit(solution)/shard_map/lru_back/pallas_call | solution.py:515
  484.0 5.2 collective-permute-done.64
  491.5 7.6 %convolution_convert_fusion.5 = bf16[320,2048]{1,0:T(8,128)(2,1)} fusion(bf16[2048,320]{1,0:T(8,128)(2,1)S(1)} %copy-done.21, bf16[2048,2048]{1,0:T(8,128)(2,1)} %bitcast.297), kind=kOutput, calls=%fused_computation.25 | convolution fusion | flops 2685009920 | bytes 11010048 | tf_op jit(solution)/shard_map/dot_general | solution.py:33
  499.2 26.7 %lru_grad.1 = (bf16[2048,320]{1,0:T(8,128)(2,1)S(1)}, bf16[2048,320]{1,0:T(8,128)(2,1)S(1)}, bf16[2048,320]{1,0:T(8,128)(2,1)}, f32[16,8,320]{2,1,0:T(8,128)S(1)...) custom-call(s32[16]{0:T(128)S(1)} %select_reduce_fusion.3.live_ref, s32[16]{0:T(128)S(1)} %convert_element_type.382.first_ref, ...), custom_call_target="tpu_custom_call" | custom-call | flops 1 | bytes 1 | tf_op jit(solution)/shard_map/lru_grad/pallas_call | solution.py:692
  533.9 3.4 collective-permute-start.70
  544.9 6.4 convolution_convert_fusion.4
  557.2 4.0 reduce-scatter.10.cloned.1.call-done
  561.2 7.4 %convolution_convert_fusion.3 = bf16[2048,320]{0,1:T(8,128)(2,1)} fusion(bf16[2048,2048]{1,0:T(8,128)(2,1)} %bitcast.245, bf16[2048,320]{1,0:T(8,128)(2,1)S(1)} %bitcast.266), kind=kOutput, calls=%fused_computation.23 | convolution fusion | flops 2685009920 | bytes 11010048 | tf_op jit(solution)/shard_map/dot_general | solution.py:33
  572.5 3.6 all-to-all-start.3
  608.0 3.7 multiply_convert_fusion
  611.8 3.5 all-to-all-start.2
  619.1 6.4 collective-permute-done.75
  625.5 9.3 %collective-permute-done.76 = bf16[256,2048]{1,0:T(8,128)(2,1)} collective-permute-done((bf16[256,2048]{1,0:T(8,128)(2,1)S(1)}, bf16[256,2048]{1,0:T(8,128)(2,1)}, u32[]{:S(2)}, u32[]{:S(2)}) %collective-permute-start.76) | collective-permute-done | bytes 1048608 | tf_op jit(solution)/shard_map/ppermute | solution.py:46
  654.0 3.4 fusion.10
  659.1 3.5 all-to-all-start.4
  666.0 4.9 all-to-all-done.4
  (586 shorter events, 249.6 us)
Async XLA Ops:
  7.2 48.3 %all-gather.9.cloned.1.call-start = ((), (), s32[]{:S(2)}) async-start(), calls=%async_computation.10 | async-start | bytes 1638400 | tf_op jit(solution)/shard_map/all_gather | solution.py:774
  21.2 34.3 %collective-permute-start.6 = (bf16[256,2048]{1,0:T(8,128)(2,1)S(1)}, bf16[256,2048]{1,0:T(8,128)(2,1)S(1)}, u32[]{:S(2)}, u32[]{:S(2)}) collective-permute-start(bf16[256,2048]{1,0:T(8,128)(2,1)S(1)} %copy-done.5), channel_id=1, source_target_pairs={{0,16},{4,20},{8,24},{12,28},{16,0},{20,4},{24,8},{28,12},{1,17},{... | collective-permute-start | bytes 3145736 | tf_op jit(solution)/shard_map/ppermute | solution.py:46
  23.3 32.2 %collective-permute-start.5 = (bf16[256,2048]{1,0:T(8,128)(2,1)S(1)}, bf16[256,2048]{1,0:T(8,128)(2,1)S(1)}, u32[]{:S(2)}, u32[]{:S(2)}) collective-permute-start(bf16[256,2048]{1,0:T(8,128)(2,1)S(1)} %copy-done.5), channel_id=1, source_target_pairs={{0,8},{4,12},{8,0},{12,4},{16,24},{20,28},{24,16},{28,20},{1,9},{5... | collective-permute-start | bytes 3145736 | tf_op jit(solution)/shard_map/ppermute | solution.py:46
  27.0 28.5 %all-to-all-start = ((bf16[8,2,64,320]{3,2,1,0:T(8,128)(2,1)}), bf16[8,2,64,320]{3,2,1,0:T(8,128)(2,1)}, u32[]{:S(2)}, u32[]{:S(2)}) async-start(bf16[8,2,64,320]{3,2,1,0:T(8,128)(2,1)} %copy.150), calls=%async_computation | async-start | bytes 1572864 | tf_op jit(solution)/shard_map/all_to_all | solution.py:771
  31.2 63.2 %all-gather.13.cloned.1.call-start = ((), (), s32[]{:S(2)}) async-start(), calls=%async_computation.17 | async-start | bytes 1966080 | tf_op jit(solution)/shard_map/all_gather | solution.py:777
  57.7 93.2 %all-gather.15.cloned.1.call-start = ((), (), s32[]{:S(2)}) async-start(), calls=%async_computation.18 | async-start | bytes 1966080 | tf_op jit(solution)/shard_map/all_gather | solution.py:777
  59.0 14.0 %collective-permute-start.7 = (bf16[128,2048]{1,0:T(8,128)(2,1)S(1)}, bf16[128,2048]{1,0:T(8,128)(2,1)}, u32[]{:S(2)}, u32[]{:S(2)}) collective-permute-start(bf16[128,2048]{1,0:T(8,128)(2,1)S(1)} %slice.331), channel_id=1, source_target_pairs={{0,8},{4,12},{8,0},{12,4},{16,24},{20,28},{24,16},{28,20},{1,9},{5... | collective-permute-start | bytes 1572872 | tf_op jit(solution)/shard_map/ppermute | solution.py:46
  62.1 16.9 %collective-permute-start.9 = (bf16[256,2048]{1,0:T(8,128)(2,1)S(1)}, bf16[256,2048]{1,0:T(8,128)(2,1)}, u32[]{:S(2)}, u32[]{:S(2)}) collective-permute-start(bf16[256,2048]{1,0:T(8,128)(2,1)S(1)} %copy-done.5), channel_id=1, source_target_pairs={{0,4},{4,0},{8,12},{12,8},{16,20},{20,16},{24,28},{28,24},{1,5},{5... | collective-permute-start | bytes 3145736 | tf_op jit(solution)/shard_map/ppermute | solution.py:46
  62.1 16.9 %collective-permute-start.10 = (bf16[256,2048]{1,0:T(8,128)(2,1)S(1)}, bf16[256,2048]{1,0:T(8,128)(2,1)}, u32[]{:S(2)}, u32[]{:S(2)}) collective-permute-start(bf16[256,2048]{1,0:T(8,128)(2,1)S(1)} %collective-permute-done.5.refs_1_), channel_id=1, source_target_pairs={{0,4},{4,0},{8,12},{12,8},{16,20},{20,16},{24,28},{28,24},{1,5},{5... | collective-permute-start | bytes 3145736 | tf_op jit(solution)/shard_map/ppermute | solution.py:46
  62.6 16.4 %collective-permute-start.11 = (bf16[256,2048]{1,0:T(8,128)(2,1)S(1)}, bf16[256,2048]{1,0:T(8,128)(2,1)}, u32[]{:S(2)}, u32[]{:S(2)}) collective-permute-start(bf16[256,2048]{1,0:T(8,128)(2,1)S(1)} %collective-permute-done.6.refs_2_), channel_id=1, source_target_pairs={{0,4},{4,0},{8,12},{12,8},{16,20},{20,16},{24,28},{28,24},{1,5},{5... | collective-permute-start | bytes 3145736 | tf_op jit(solution)/shard_map/ppermute | solution.py:46
  80.7 41.2 %all-to-all-start.1 = ((bf16[8,64,1536]{2,1,0:T(8,128)(2,1)}), bf16[8,64,1536]{2,1,0:T(8,128)(2,1)}, u32[]{:S(2)}, u32[]{:S(2)}) async-start(bf16[8,64,1536]{2,1,0:T(8,128)(2,1)} %copy.161), calls=%async_computation.1 | async-start | bytes 3145728 | tf_op jit(solution)/shard_map/all_to_all | solution.py:771
  85.0 170.0 %all-gather.17.cloned.1.call-start = ((), (), s32[]{:S(2)}) async-start(), calls=%async_computation.19 | async-start | bytes 7864320 | tf_op jit(solution)/shard_map/all_gather | solution.py:777
  121.9 196.7 %all-gather.11.cloned.1.call-start = ((), (), s32[]{:S(2)}) async-start(), calls=%async_computation.11 | async-start | bytes 3932160 | tf_op jit(solution)/shard_map/all_gather | solution.py:774
  122.1 47.3 %collective-permute-start.22 = (bf16[256,2048]{1,0:T(8,128)(2,1)}, bf16[256,2048]{1,0:T(8,128)(2,1)}, u32[]{:S(2)}, u32[]{:S(2)}) collective-permute-start(bf16[256,2048]{1,0:T(8,128)(2,1)} %fusion.12.refs_0_), channel_id=1, source_target_pairs={{0,24},{4,28},{8,16},{12,20},{16,8},{20,12},{24,0},{28,4},{1,25},{... | collective-permute-start | bytes 3145736 | tf_op jit(solution)/shard_map/ppermute | solution.py:46
  124.5 45.0 %collective-permute-start.21 = (bf16[256,2048]{1,0:T(8,128)(2,1)}, bf16[256,2048]{1,0:T(8,128)(2,1)}, u32[]{:S(2)}, u32[]{:S(2)}) collective-permute-start(bf16[256,2048]{1,0:T(8,128)(2,1)} %fusion.12.refs_0_), channel_id=1, source_target_pairs={{0,16},{4,20},{8,24},{12,28},{16,0},{20,4},{24,8},{28,12},{1,17},{... | collective-permute-start | bytes 3145736 | tf_op jit(solution)/shard_map/ppermute | solution.py:46
  125.1 44.5 %collective-permute-start.20 = (bf16[256,2048]{1,0:T(8,128)(2,1)}, bf16[256,2048]{1,0:T(8,128)(2,1)}, u32[]{:S(2)}, u32[]{:S(2)}) collective-permute-start(bf16[256,2048]{1,0:T(8,128)(2,1)} %fusion.12.refs_0_), channel_id=1, source_target_pairs={{0,8},{4,12},{8,0},{12,4},{16,24},{20,28},{24,16},{28,20},{1,9},{5... | collective-permute-start | bytes 3145736 | tf_op jit(solution)/shard_map/ppermute | solution.py:46
  152.5 16.1 %collective-permute-start.18 = (f32[2,3,16,128]{3,2,1,0:T(8,128)S(1)}, f32[2,3,16,128]{3,2,1,0:T(8,128)S(1)}, u32[]{:S(2)}, u32[]{:S(2)}) collective-permute-start(f32[2,3,16,128]{3,2,1,0:T(8,128)S(1)} %get-tuple-element.240), channel_id=1, source_target_pairs={{0,2},{1,3},{2,0},{3,1},{4,6},{5,7},{6,4},{7,5},{8,10},{9,11},{10,... | collective-permute-start | bytes 147464 | tf_op jit(solution)/shard_map/ppermute | solution.py:46
  196.8 25.5 %collective-permute-start.25 = (bf16[256,2048]{1,0:T(8,128)(2,1)S(1)}, bf16[256,2048]{1,0:T(8,128)(2,1)S(1)}, u32[]{:S(2)}, u32[]{:S(2)}) collective-permute-start(bf16[256,2048]{1,0:T(8,128)(2,1)S(1)} %pad_maximum_fusion.1), channel_id=1, source_target_pairs={{0,8},{4,12},{8,0},{12,4},{16,24},{20,28},{24,16},{28,20},{1,9},{5... | collective-permute-start | bytes 3145736 | tf_op jit(solution)/shard_map/ppermute | solution.py:46
  199.3 25.2 %collective-permute-start.27 = (bf16[256,2048]{1,0:T(8,128)(2,1)S(1)}, bf16[256,2048]{1,0:T(8,128)(2,1)S(1)}, u32[]{:S(2)}, u32[]{:S(2)}) collective-permute-start(bf16[256,2048]{1,0:T(8,128)(2,1)S(1)} %pad_maximum_fusion.2), channel_id=1, source_target_pairs={{0,16},{4,20},{8,24},{12,28},{16,0},{20,4},{24,8},{28,12},{1,17},{... | collective-permute-start | bytes 3145736 | tf_op jit(solution)/shard_map/ppermute | solution.py:46
  202.8 25.0 %collective-permute-start.31 = (bf16[256,2048]{1,0:T(8,128)(2,1)}, bf16[256,2048]{1,0:T(8,128)(2,1)S(1)}, u32[]{:S(2)}, u32[]{:S(2)}) collective-permute-start(bf16[256,2048]{1,0:T(8,128)(2,1)} %fusion.12.refs_0_), channel_id=1, source_target_pairs={{0,4},{4,0},{8,12},{12,8},{16,20},{20,16},{24,28},{28,24},{1,5},{5... | collective-permute-start | bytes 3145736 | tf_op jit(solution)/shard_map/ppermute | solution.py:46
  202.8 28.0 %collective-permute-start.32 = (bf16[256,2048]{1,0:T(8,128)(2,1)}, bf16[256,2048]{1,0:T(8,128)(2,1)}, u32[]{:S(2)}, u32[]{:S(2)}) collective-permute-start(bf16[256,2048]{1,0:T(8,128)(2,1)} %collective-permute-done.20.refs_1_), channel_id=1, source_target_pairs={{0,4},{4,0},{8,12},{12,8},{16,20},{20,16},{24,28},{28,24},{1,5},{5... | collective-permute-start | bytes 3145736 | tf_op jit(solution)/shard_map/ppermute | solution.py:46
  203.3 27.5 %collective-permute-start.33 = (bf16[256,2048]{1,0:T(8,128)(2,1)}, bf16[256,2048]{1,0:T(8,128)(2,1)}, u32[]{:S(2)}, u32[]{:S(2)}) collective-permute-start(bf16[256,2048]{1,0:T(8,128)(2,1)} %collective-permute-done.21.refs_2_), channel_id=1, source_target_pairs={{0,4},{4,0},{8,12},{12,8},{16,20},{20,16},{24,28},{28,24},{1,5},{5... | collective-permute-start | bytes 3145736 | tf_op jit(solution)/shard_map/ppermute | solution.py:46
  225.5 15.2 %collective-permute-start.30 = (bf16[128,2048]{1,0:T(8,128)(2,1)}, bf16[128,2048]{1,0:T(8,128)(2,1)}, u32[]{:S(2)}, u32[]{:S(2)}) collective-permute-start(bf16[128,2048]{1,0:T(8,128)(2,1)} %fusion.24), channel_id=1, source_target_pairs={{0,16},{4,20},{8,24},{12,28},{16,0},{20,4},{24,8},{28,12},{1,17},{... | collective-permute-start | bytes 1572872 | tf_op jit(solution)/shard_map/ppermute | solution.py:46
  230.4 189.5 %reduce-scatter.6.cloned.1.call-start = ((), (), s32[]{:S(2)}) async-start(), calls=%async_computation.12 | async-start | bytes 3932160 | tf_op jit(solution)/shard_map/reduce_scatter | solution.py:876
  244.4 24.0 %collective-permute-start.36 = (bf16[256,2048]{1,0:T(8,128)(2,1)S(1)}, bf16[256,2048]{1,0:T(8,128)(2,1)}, u32[]{:S(2)}, u32[]{:S(2)}) collective-permute-start(bf16[256,2048]{1,0:T(8,128)(2,1)S(1)} %multiply_convert_fusion.1.refs_0_), channel_id=1, source_target_pairs={{0,16},{4,20},{8,24},{12,28},{16,0},{20,4},{24,8},{28,12},{1,17},{... | collective-permute-start | bytes 3145736 | tf_op jit(solution)/shard_map/ppermute | solution.py:46
  245.5 24.0 %collective-permute-start.35 = (bf16[256,2048]{1,0:T(8,128)(2,1)S(1)}, bf16[256,2048]{1,0:T(8,128)(2,1)}, u32[]{:S(2)}, u32[]{:S(2)}) collective-permute-start(bf16[256,2048]{1,0:T(8,128)(2,1)S(1)} %multiply_convert_fusion.1.refs_0_), channel_id=1, source_target_pairs={{0,8},{4,12},{8,0},{12,4},{16,24},{20,28},{24,16},{28,20},{1,9},{5... | collective-permute-start | bytes 3145736 | tf_op jit(solution)/shard_map/ppermute | solution.py:46
  246.9 37.8 %collective-permute-start.39 = (bf16[256,2048]{1,0:T(8,128)(2,1)S(1)}, bf16[256,2048]{1,0:T(8,128)(2,1)}, u32[]{:S(2)}, u32[]{:S(2)}) collective-permute-start(bf16[256,2048]{1,0:T(8,128)(2,1)S(1)} %multiply_convert_fusion.1.refs_0_), channel_id=1, source_target_pairs={{0,4},{4,0},{8,12},{12,8},{16,20},{20,16},{24,28},{28,24},{1,5},{5... | collective-permute-start | bytes 3145736 | tf_op jit(solution)/shard_map/ppermute | solution.py:46
  318.6 210.4 %reduce-scatter.8.cloned.1.call-start = ((), (), s32[]{:S(2)}) async-start(), calls=%async_computation.13 | async-start | bytes 7864320 | tf_op jit(solution)/shard_map/reduce_scatter | solution.py:881
  363.4 34.3 %collective-permute-start.52 = (bf16[1024,2048]{1,0:T(8,128)(2,1)}, bf16[1024,2048]{1,0:T(8,128)(2,1)}, u32[]{:S(2)}, u32[]{:S(2)}) collective-permute-start(bf16[1024,2048]{1,0:T(8,128)(2,1)} %convolution_convert_fusion.1), channel_id=1, source_target_pairs={{0,4},{4,0},{8,12},{12,8},{16,20},{20,16},{24,28},{28,24},{1,5},{5... | collective-permute-start | bytes 12582920 | tf_op jit(solution)/shard_map/ppermute | solution.py:46
  363.6 25.6 %collective-permute-start.46 = (bf16[256,2048]{1,0:T(8,128)(2,1)S(1)}, bf16[256,2048]{1,0:T(8,128)(2,1)}, u32[]{:S(2)}, u32[]{:S(2)}) collective-permute-start(bf16[256,2048]{1,0:T(8,128)(2,1)S(1)} %pad_maximum_fusion.3), channel_id=1, source_target_pairs={{0,8},{4,12},{8,0},{12,4},{16,24},{20,28},{24,16},{28,20},{1,9},{5... | collective-permute-start | bytes 3145736 | tf_op jit(solution)/shard_map/ppermute | solution.py:46
  365.3 25.3 %collective-permute-start.48 = (bf16[256,2048]{1,0:T(8,128)(2,1)S(1)}, bf16[256,2048]{1,0:T(8,128)(2,1)}, u32[]{:S(2)}, u32[]{:S(2)}) collective-permute-start(bf16[256,2048]{1,0:T(8,128)(2,1)S(1)} %pad_maximum_fusion.4), channel_id=1, source_target_pairs={{0,16},{4,20},{8,24},{12,28},{16,0},{20,4},{24,8},{28,12},{1,17},{... | collective-permute-start | bytes 3145736 | tf_op jit(solution)/shard_map/ppermute | solution.py:46
  410.1 151.1 %reduce-scatter.10.cloned.1.call-start = ((), (), s32[]{:S(2)}) async-start(), calls=%async_computation.14 | async-start | bytes 1638400 | tf_op jit(solution)/shard_map/reduce_scatter | solution.py:881
  419.3 22.6 %collective-permute-start.54 = (bf16[256,2048]{1,0:T(8,128)(2,1)S(1)}, bf16[256,2048]{1,0:T(8,128)(2,1)}, u32[]{:S(2)}, u32[]{:S(2)}) collective-permute-start(bf16[256,2048]{1,0:T(8,128)(2,1)S(1)} %get-tuple-element.310.refs_0_), channel_id=1, source_target_pairs={{0,16},{4,20},{8,24},{12,28},{16,0},{20,4},{24,8},{28,12},{1,17},{... | collective-permute-start | bytes 3145736 | tf_op jit(solution)/shard_map/ppermute | solution.py:46
  419.3 22.6 %collective-permute-start.53 = (bf16[256,2048]{1,0:T(8,128)(2,1)S(1)}, bf16[256,2048]{1,0:T(8,128)(2,1)}, u32[]{:S(2)}, u32[]{:S(2)}) collective-permute-start(bf16[256,2048]{1,0:T(8,128)(2,1)S(1)} %get-tuple-element.310.refs_0_), channel_id=1, source_target_pairs={{0,8},{4,12},{8,0},{12,4},{16,24},{20,28},{24,16},{28,20},{1,9},{5... | collective-permute-start | bytes 3145736 | tf_op jit(solution)/shard_map/ppermute | solution.py:46
  419.9 34.7 %collective-permute-start.57 = (bf16[256,2048]{1,0:T(8,128)(2,1)S(1)}, bf16[256,2048]{1,0:T(8,128)(2,1)}, u32[]{:S(2)}, u32[]{:S(2)}) collective-permute-start(bf16[256,2048]{1,0:T(8,128)(2,1)S(1)} %get-tuple-element.310.refs_0_), channel_id=1, source_target_pairs={{0,4},{4,0},{8,12},{12,8},{16,20},{20,16},{24,28},{28,24},{1,5},{5... | collective-permute-start | bytes 3145736 | tf_op jit(solution)/shard_map/ppermute | solution.py:46
  456.6 72.4 %collective-permute-start.65 = (bf16[256,2048]{1,0:T(8,128)(2,1)}, bf16[256,2048]{1,0:T(8,128)(2,1)}, u32[]{:S(2)}, u32[]{:S(2)}) collective-permute-start(bf16[256,2048]{1,0:T(8,128)(2,1)} %get-tuple-element.335), channel_id=1, source_target_pairs={{0,24},{4,28},{8,16},{12,20},{16,8},{20,12},{24,0},{28,4},{1,25},{... | collective-permute-start | bytes 3145736 | tf_op jit(solution)/shard_map/ppermute | solution.py:46
  459.3 69.7 %collective-permute-start.66 = (bf16[256,2048]{1,0:T(8,128)(2,1)}, bf16[256,2048]{1,0:T(8,128)(2,1)}, u32[]{:S(2)}, u32[]{:S(2)}) collective-permute-start(bf16[256,2048]{1,0:T(8,128)(2,1)} %get-tuple-element.336), channel_id=1, source_target_pairs={{0,8},{4,12},{8,0},{12,4},{16,24},{20,28},{24,16},{28,20},{1,9},{5... | collective-permute-start | bytes 3145736 | tf_op jit(solution)/shard_map/ppermute | solution.py:46
  459.8 69.1 %collective-permute-start.67 = (bf16[256,2048]{1,0:T(8,128)(2,1)}, bf16[256,2048]{1,0:T(8,128)(2,1)}, u32[]{:S(2)}, u32[]{:S(2)}) collective-permute-start(bf16[256,2048]{1,0:T(8,128)(2,1)} %get-tuple-element.337), channel_id=1, source_target_pairs={{0,16},{4,20},{8,24},{12,28},{16,0},{20,4},{24,8},{28,12},{1,17},{... | collective-permute-start | bytes 3145736 | tf_op jit(solution)/shard_map/ppermute | solution.py:46
  484.0 15.2 %collective-permute-start.63 = (f32[3,16,128]{2,1,0:T(8,128)S(1)}, f32[3,16,128]{2,1,0:T(8,128)S(1)}, u32[]{:S(2)}, u32[]{:S(2)}) collective-permute-start(f32[3,16,128]{2,1,0:T(8,128)S(1)} %get-tuple-element.322), channel_id=1, source_target_pairs={{0,2},{1,3},{2,0},{3,1},{4,6},{5,7},{6,4},{7,5},{8,10},{9,11},{10,... | collective-permute-start | bytes 73736 | tf_op jit(solution)/shard_map/ppermute | solution.py:46
  529.0 82.7 %reduce-scatter.12.cloned.1.call-start = ((), (), s32[]{:S(2)}) async-start(), calls=%async_computation.15 | async-start | bytes 1966080 | tf_op jit(solution)/shard_map/reduce_scatter | solution.py:881
  533.9 21.3 %collective-permute-start.70 = (bf16[48,320]{1,0:T(8,128)(2,1)}, bf16[48,320]{1,0:T(8,128)(2,1)}, u32[]{:S(2)}, u32[]{:S(2)}) collective-permute-start(bf16[48,320]{1,0:T(8,128)(2,1)} %reshape.417), channel_id=1, source_target_pairs={{0,3},{1,2},{2,1},{3,0},{4,7},{5,6},{6,5},{7,4},{8,11},{9,10},{10,... | collective-permute-start | bytes 92168 | tf_op jit(solution)/shard_map/ppermute | solution.py:46
  537.3 17.9 %collective-permute-start.69 = (bf16[48,320]{1,0:T(8,128)(2,1)}, bf16[48,320]{1,0:T(8,128)(2,1)}, u32[]{:S(2)}, u32[]{:S(2)}) collective-permute-start(bf16[48,320]{1,0:T(8,128)(2,1)} %reshape.417), channel_id=1, source_target_pairs={{0,2},{1,3},{2,0},{3,1},{4,6},{5,7},{6,4},{7,5},{8,10},{9,11},{10,... | collective-permute-start | bytes 92168 | tf_op jit(solution)/shard_map/ppermute | solution.py:46
  537.3 17.9 %collective-permute-start.68 = (bf16[48,320]{1,0:T(8,128)(2,1)}, bf16[48,320]{1,0:T(8,128)(2,1)}, u32[]{:S(2)}, u32[]{:S(2)}) collective-permute-start(bf16[48,320]{1,0:T(8,128)(2,1)} %reshape.417), channel_id=1, source_target_pairs={{0,1},{1,0},{2,3},{3,2},{4,5},{5,4},{6,7},{7,6},{8,9},{9,8},{10,11... | collective-permute-start | bytes 92168 | tf_op jit(solution)/shard_map/ppermute | solution.py:46
  572.5 39.3 %all-to-all-start.3 = ((bf16[8,64,1536]{2,1,0:T(8,128)(2,1)}), bf16[8,64,1536]{2,1,0:T(8,128)(2,1)S(1)}, u32[]{:S(2)}, u32[]{:S(2)}) async-start(bf16[8,64,1536]{2,1,0:T(8,128)(2,1)} %bitcast.274), calls=%async_computation.7 | async-start | bytes 3145728 | tf_op jit(solution)/shard_map/all_to_all | solution.py:771
  576.1 81.3 %reduce-scatter.14.cloned.1.call-start = ((), (), s32[]{:S(2)}) async-start(), calls=%async_computation.16 | async-start | bytes 2334720 | tf_op jit(solution)/shard_map/reduce_scatter | solution.py:881
  599.2 26.3 %collective-permute-start.75 = (bf16[256,2048]{1,0:T(8,128)(2,1)}, bf16[256,2048]{1,0:T(8,128)(2,1)}, u32[]{:S(2)}, u32[]{:S(2)}) collective-permute-start(bf16[256,2048]{1,0:T(8,128)(2,1)} %pad_maximum_fusion.5), channel_id=1, source_target_pairs={{0,8},{4,12},{8,0},{12,4},{16,24},{20,28},{24,16},{28,20},{1,9},{5... | collective-permute-start | bytes 3145736 | tf_op jit(solution)/shard_map/ppermute | solution.py:46
  606.5 28.2 %collective-permute-start.76 = (bf16[256,2048]{1,0:T(8,128)(2,1)S(1)}, bf16[256,2048]{1,0:T(8,128)(2,1)}, u32[]{:S(2)}, u32[]{:S(2)}) collective-permute-start(bf16[256,2048]{1,0:T(8,128)(2,1)S(1)} %pad_maximum_fusion.6), channel_id=1, source_target_pairs={{0,16},{4,20},{8,24},{12,28},{16,0},{20,4},{24,8},{28,12},{1,17},{... | collective-permute-start | bytes 3145736 | tf_op jit(solution)/shard_map/ppermute | solution.py:46
  611.8 29.4 %all-to-all-start.2 = ((bf16[8,64,320]{2,1,0:T(8,128)(2,1)}), bf16[8,64,320]{2,1,0:T(8,128)(2,1)S(1)}, u32[]{:S(2)}, u32[]{:S(2)}) async-start(bf16[8,64,320]{2,1,0:T(8,128)(2,1)} %bitcast.282), calls=%async_computation.6 | async-start | bytes 786432 | tf_op jit(solution)/shard_map/all_to_all | solution.py:771
  (150 other events, 1204.3 us)
Sparse Core Ops, SparseCore 0:
  10.2 36.2 all-gather.8
  57.8 36.6 all-gather.12
  96.6 39.1 all-gather.14
  137.2 117.7 all-gather.16
  256.4 62.1 all-gather.10
  320.7 58.8 reduce-scatter.5
  410.2 109.0 reduce-scatter.7
  529.2 31.9 reduce-scatter.9
  572.6 33.9 reduce-scatter.11
  611.9 38.1 reduce-scatter.13

commit v5 on v4

--- a/solution.py
+++ b/solution.py
@@ -212,7 +212,7 @@
     return jnp.concatenate(rows, axis=0)
 
 
-def stack(pieces, name, gain=None, weights=(), gated=False, steps=8):
+def stack(pieces, name, gain=None, weights=(), gated=False, steps=4):
     count = len(pieces)
     halves, flat = piece_halves(pieces), jax.tree.leaves(pieces)
     rows, model = pieces[0].shape
@@ -471,7 +471,7 @@
     lax.fori_loop(0, blocks, block, 0)
 
 
-def lru_back(pieces, out_w, act, bend, keep, steps=8):
+def lru_back(pieces, out_w, act, bend, keep, steps=4):
     count = len(pieces)
     halves, flat = piece_halves(pieces), jax.tree.leaves(pieces)
     rows, model = pieces[0].shape
@@ -1028,7 +1028,7 @@
         axis=1,
     )
     pack, branch_home = barrier((pack.reshape(z_size * pack.shape[1], lanes), branch_home))
-    pack, ff_got = barrier((pack, ff_got))
+    pack, ff_got, down_home = barrier((pack, ff_got, down_home))
     pack = home_rows(pack)
     grad_gate_home, grad_up_home = own_columns(ff_got[..., :ffw]), own_columns(ff_got[..., ffw:])
     grad_gain_two = gain_home(norm_gain2, ((grad_gate_home, w_gate), (grad_up_home, w_up)))

time: 689 us -> 683 us (level)
  Pallas kernels: 155 us -> 148 us
    unnamed x209 -> x211, local copies, waits for them, and re-layouts: 26.8 us -> 26.3 us
  transfers between devices with their start and end apart: 94 -> 94, of which waited for: 40 -> 41; matrix products, arithmetic and copies ran while one was open for 30% -> 30% of each run, Pallas kernels for 23% -> 22%
where the time goes in v5:
time: 683 us; the launch traced here: 674 us
  waiting for transfers between devices  182 us (27%)
  Pallas kernels  148 us (22%)
  matrix products  104 us (15%)
  local copies, waits for them, and re-layouts  87 us (13%)
  starting transfers between devices  82.8 us (12%)
  other arithmetic  53.9 us (8%)
  between operations  16.7 us (2%)
    ppermute x79, waiting for transfers between devices, swap(): return lax.ppermute(values, axis, [(i, i ^ flip) for i in range(count)])  149 us
    pallas_call x4, Pallas kernels, whole(): pl.pallas_call(kernel, out_shape=outs, in_specs=specs, out_specs=[pl.Bloc...  67 us
    ppermute x79, starting transfers between devices, swap(): return lax.ppermute(values, axis, [(i, i ^ flip) for i in range(count)])  62.4 us
    dot_general x7, matrix products, mm_tn(): lax.dot_general(left, right, (((0,), (0,)), ((), ())), preferred_element_...  49.7 us
    pallas_call x3, Pallas kernels, stack(): pl.pallas_call(kernel, grid=(steps,), in_specs=piece_specs(pieces, steps)...  37.9 us
    dot_general x24, matrix products, mm_nt(): lax.dot_general(left, right, (((1,), (1,)), ((), ())), preferred_element_...  35.3 us
    unnamed x211, local copies, waits for them, and re-layouts  26.3 us
    convert_element_type x20, other arithmetic, as_low(): return values.astype(jnp.bfloat16)  25.2 us
  transfers between devices with their start and end apart: 94, of which 41 were waited for; matrix products, arithmetic and copies ran while one was open for 30% of the time, Pallas kernels for 22%

profile of v5, /device:TPU:0, one launch (start us, length us, event | category | flops | bytes accessed | tf_op | source)
XLA Modules:
  0.0 674.2 jit_solution(6526882353801950510)
XLA Ops:
  27.0 4.2 all-to-all-start
  33.0 10.0 %collective-permute-done.3 = bf16[1,80,344]{1,2,0:T(8,128)(2,1)S(1)} collective-permute-done((bf16[1,80,344]{1,2,0:T(8,128)(2,1)S(1)}, bf16[1,80,344]{1,2,0:T(8,128)(2,1)S(1)}, u32[]{:S(2)}, u32[]{:S(2)}) %collective-permute-start.3) | collective-permute-done | bytes 55072 | tf_op jit(solution)/shard_map/ppermute | solution.py:46
  43.9 10.7 %collective-permute-done.4 = bf16[2,80,344]{1,2,0:T(8,128)(2,1)S(1)} collective-permute-done((bf16[2,80,344]{1,2,0:T(8,128)(2,1)S(1)}, bf16[2,80,344]{1,2,0:T(8,128)(2,1)S(1)}, u32[]{:S(2)}, u32[]{:S(2)}) %collective-permute-start.4) | collective-permute-done | bytes 110112 | tf_op jit(solution)/shard_map/ppermute | solution.py:46
  63.8 9.1 %collective-permute-done.7.refs_3_ = bf16[128,2048]{1,0:T(8,128)(2,1)} collective-permute-done((bf16[128,2048]{1,0:T(8,128)(2,1)S(1)}, bf16[128,2048]{1,0:T(8,128)(2,1)}, u32[]{:S(2)}, u32[]{:S(2)}) %collective-permute-start.7) | collective-permute-done | bytes 524320 | tf_op jit(solution)/shard_map/ppermute | solution.py:46
  80.7 4.3 all-to-all-start.1
  88.1 6.4 all-gather.13.cloned.1.call-done
  97.2 11.3 %norm_one.1 = (bf16[8,256,2048]{2,1,0:T(8,128)(2,1)}, f32[8,256,320]{2,1,0:T(8,128)}) custom-call(bf16[256,2048]{1,0:T(8,128)(2,1)S(1)} %copy-done.5, bf16[256,2048]{1,0:T(8,128)(2,1)S(1)} %collective-permute-done.5.refs_1_, bf16[256,2048]{1,0:T(8,128)(2,1)S(1)} %collective-permute-done.6.refs_2_, bf16[128,2048]{1,0:T(8,128)(2,1)} %collective-permute-done.7.refs_3_, ...), custom_call_target="tpu_custom_call" | custom-call | flops 1 | bytes 1 | tf_op jit(solution)/shard_map/norm_one/pallas_call | solution.py:248
  116.4 3.3 collective-permute-done.15
  126.1 19.8 %lru_forward.1 = (bf16[2048,320]{1,0:T(8,128)(2,1)S(1)}, f32[3,2048,128]{2,1,0:T(8,128)S(1)}, f32[3,2048,128]{2,1,0:T(8,128)}, f32[3,2048,128]{2,1,0:T(8,128)}, ...) custom-call(s32[16]{0:T(128)S(1)} %select_reduce_fusion.3.live_ref, ...), custom_call_target="tpu_custom_call" | custom-call | flops 1 | bytes 1 | tf_op jit(solution)/shard_map/lru_forward/pallas_call | solution.py:692
  151.5 3.3 collective-permute-done.19
  156.4 8.7 %branch_pre.1.ypre_ref = f32[2048,320]{1,0:T(8,128)S(1)} custom-call(bf16[2048,2048]{1,0:T(8,128)(2,1)} %bitcast.243, bf16[2048,320]{1,0:T(8,128)(2,1)S(1)} %bitcast.202), custom_call_target="tpu_custom_call" | custom-call | flops 2684354560 | bytes 11010048 | tf_op jit(solution)/shard_map/branch_pre/pallas_call | solution.py:297
  168.6 19.9 %lru_state.1 = (bf16[2048,320]{1,0:T(8,128)(2,1)S(1)}, f32[3,2048,128]{2,1,0:T(8,128)S(1)}, f32[3,2048,128]{2,1,0:T(8,128)}, f32[3,2048,128]{2,1,0:T(8,128)}, f32[3,2048,128]{2,1,0:T(8,128)}) custom-call(s32[64]{0:T(128)S(1)} %select_reduce_fusion.pos_ref, f32[4,2,3,16,128]{4,3,2,1,0:T(8,128)S(1)} %pad_maximum_fusion.8.all_ref, f32[3,2048,128]{2,1,0:T(8,128)} %copy-done.4, ...), custom_call_target="tpu_custom_call" | custom-call | flops 1 | bytes 1 | tf_op jit(solution)/shard_map/lru_state/pallas_call | solution.py:692
  201.8 19.7 %collective-permute-done.25 = bf16[256,2048]{1,0:T(8,128)(2,1)S(1)} collective-permute-done((bf16[256,2048]{1,0:T(8,128)(2,1)S(1)}, bf16[256,2048]{1,0:T(8,128)(2,1)S(1)}, u32[]{:S(2)}, u32[]{:S(2)}) %collective-permute-start.25) | collective-permute-done | bytes 1048608 | tf_op jit(solution)/shard_map/ppermute | solution.py:46
  231.3 6.8 %stack_top.1 = bf16[8,256,2048]{2,1,0:T(8,128)(2,1)} custom-call(bf16[256,2048]{1,0:T(8,128)(2,1)} %fusion.12.refs_0_, bf16[256,2048]{1,0:T(8,128)(2,1)} %collective-permute-done.20.refs_1_, bf16[256,2048]{1,0:T(8,128)(2,1)} %collective-permute-done.21.refs_2_, bf16[256,2048]{1,0:T(8,128)(2,1)} %collective-permute-done.22.refs_3_, ...), custom_call_target="tpu_custom_call" | custom-call | flops 1 | bytes 1 | tf_op jit(solution)/shard_map/stack_top/pallas_call | solution.py:248
  244.9 9.6 %all-gather.17.cloned.1.call-done = bf16[32,64,1536]{2,1,0:T(8,128)(2,1)} async-done(((bf16[8,64,1536]{2,1,0:T(8,128)(2,1)}), bf16[32,64,1536]{2,1,0:T(8,128)(2,1)}) %all-gather.17.cloned.1.call-update) | async-done | bytes 6291472 | tf_op jit(solution)/shard_map/all_gather | solution.py:777
  254.5 6.1 copy.164
  260.6 5.4 collective-permute-done.36.refs_2_
  272.0 7.0 %collective-permute-done.37.refs_3_ = bf16[128,2048]{1,0:T(8,128)(2,1)S(1)} collective-permute-done((bf16[128,2048]{1,0:T(8,128)(2,1)S(1)}, bf16[128,2048]{1,0:T(8,128)(2,1)S(1)}, u32[]{:S(2)}, u32[]{:S(2)}) %collective-permute-start.37) | collective-permute-done | bytes 524320 | tf_op jit(solution)/shard_map/ppermute | solution.py:46
  283.4 19.9 %ff_forward.1 = (bf16[8,256,2048]{2,1,0:T(8,128)(2,1)}, f32[8,256,768]{2,1,0:T(8,128)}, f32[8,256,768]{2,1,0:T(8,128)}, bf16[8,256,768]{2,1,0:T(8,128)(2,1)}) custom-call(bf16[256,2048]{1,0:T(8,128)(2,1)S(1)} %multiply_convert_fusion.1.refs_0_, bf16[256,2048]{1,0:T(8,128)(2,1)} %collective-permute-done.35.refs_1_, ...), custom_call_target="tpu_custom_call" | custom-call | flops 1 | bytes 1 | tf_op jit(solution)/shard_map/ff_forward/pallas_call | solution.py:248
  303.4 9.5 %convolution_convert_fusion.2 = bf16[768,2048]{1,0:T(8,128)(2,1)} fusion(bf16[2048,768]{1,0:T(8,128)(2,1)} %bitcast.298, bf16[2048,2048]{1,0:T(8,128)(2,1)S(1)} %bitcast.227), kind=kOutput, calls=%fused_computation.10 | convolution fusion | flops 6444023808 | bytes 14680064 | tf_op jit(solution)/shard_map/dot_general | solution.py:33
  312.9 5.1 all-gather.11.cloned.1.call-done.down_ref
  320.2 14.5 %ff_backward.1 = bf16[2048,1536]{1,0:T(8,128)(2,1)} custom-call(bf16[2048,2048]{1,0:T(8,128)(2,1)} %bitcast.224, bf16[768,2048]{1,0:T(8,128)(2,1)S(1)} %copy-done.9, f32[2048,768]{1,0:T(8,128)} %bitcast.257, f32[2048,768]{1,0:T(8,128)} %bitcast.258), custom_call_target="tpu_custom_call" | custom-call | flops 1 | bytes 1 | tf_op jit(solution)/shard_map/ff_backward/pallas_call | solution.py:273
  334.7 5.1 convolution_convert_fusion.9
  354.4 3.1 convolution_add_fusion.12
  357.5 5.4 convolution_convert_fusion.1
  366.4 15.5 %convolution_convert_fusion = bf16[2048,1536]{1,0:T(8,128)(2,1)S(1)} fusion(bf16[2048,2048]{1,0:T(8,128)(2,1)} %bitcast.296, bf16[2048,1536]{1,0:T(8,128)(2,1)S(1)} %copy-done.32), kind=kOutput, calls=%fused_computation.2 | convolution fusion | flops 12888047616 | bytes 20971520 | tf_op jit(solution)/shard_map/dot_general | solution.py:33
  381.8 3.3 copy.165
  385.2 3.5 collective-permute-done.46
  397.2 5.4 fusion.70
  409.7 3.2 multiply_reduce_fusion
  414.9 4.0 fusion.57
  419.4 22.1 %collective-permute-done.54.refs_2_ = bf16[256,2048]{1,0:T(8,128)(2,1)} collective-permute-done((bf16[256,2048]{1,0:T(8,128)(2,1)S(1)}, bf16[256,2048]{1,0:T(8,128)(2,1)}, u32[]{:S(2)}, u32[]{:S(2)}) %collective-permute-start.54) | collective-permute-done | bytes 1048608 | tf_op jit(solution)/shard_map/ppermute | solution.py:46
  446.4 6.7 collective-permute-done.55.refs_3_
  459.7 20.0 %lru_back.1 = (bf16[8,256,2048]{2,1,0:T(8,128)(2,1)}, bf16[8,256,320]{2,1,0:T(8,128)(2,1)}, f32[3,2048,128]{2,1,0:T(8,128)}, f32[3,16,128]{2,1,0:T(8,128)S(1)}) custom-call(bf16[256,2048]{1,0:T(8,128)(2,1)S(1)} %get-tuple-element.311.refs_0_, bf16[256,2048]{1,0:T(8,128)(2,1)} %collective-permute-done.53.refs_1_, ...), custom_call_target="tpu_custom_call" | custom-call | flops 1 | bytes 1 | tf_op jit(solution)/shard_map/lru_back/pallas_call | solution.py:515
  481.0 5.1 collective-permute-done.64
  486.2 7.5 %convolution_convert_fusion.5 = bf16[320,2048]{1,0:T(8,128)(2,1)} fusion(bf16[2048,320]{1,0:T(8,128)(2,1)S(1)} %copy-done.21, bf16[2048,2048]{1,0:T(8,128)(2,1)} %bitcast.297), kind=kOutput, calls=%fused_computation.25 | convolution fusion | flops 2685009920 | bytes 11010048 | tf_op jit(solution)/shard_map/dot_general | solution.py:33
  493.8 26.6 %lru_grad.1 = (bf16[2048,320]{1,0:T(8,128)(2,1)S(1)}, bf16[2048,320]{1,0:T(8,128)(2,1)S(1)}, bf16[2048,320]{1,0:T(8,128)(2,1)}, f32[16,8,320]{2,1,0:T(8,128)S(1)...) custom-call(s32[16]{0:T(128)S(1)} %select_reduce_fusion.3.live_ref, s32[16]{0:T(128)S(1)} %convert_element_type.382.first_ref, ...), custom_call_target="tpu_custom_call" | custom-call | flops 1 | bytes 1 | tf_op jit(solution)/shard_map/lru_grad/pallas_call | solution.py:692
  536.9 6.4 convolution_convert_fusion.4
  549.2 6.1 reduce-scatter.10.cloned.1.call-done
  555.3 7.4 %convolution_convert_fusion.3 = bf16[2048,320]{0,1:T(8,128)(2,1)} fusion(bf16[2048,2048]{1,0:T(8,128)(2,1)} %bitcast.245, bf16[2048,320]{1,0:T(8,128)(2,1)S(1)} %bitcast.266), kind=kOutput, calls=%fused_computation.23 | convolution fusion | flops 2685009920 | bytes 11010048 | tf_op jit(solution)/shard_map/dot_general | solution.py:33
  566.6 3.7 all-to-all-start.3
  602.4 3.7 multiply_convert_fusion
  606.2 3.5 all-to-all-start.2
  613.5 6.3 collective-permute-done.75
  619.7 9.4 %collective-permute-done.76 = bf16[256,2048]{1,0:T(8,128)(2,1)} collective-permute-done((bf16[256,2048]{1,0:T(8,128)(2,1)S(1)}, bf16[256,2048]{1,0:T(8,128)(2,1)}, u32[]{:S(2)}, u32[]{:S(2)}) %collective-permute-start.76) | collective-permute-done | bytes 1048608 | tf_op jit(solution)/shard_map/ppermute | solution.py:46
  648.4 3.4 fusion.10
  653.6 3.5 all-to-all-start.4
  660.4 4.9 all-to-all-done.4
  (588 shorter events, 248.1 us)
Async XLA Ops:
  7.2 48.3 %all-gather.9.cloned.1.call-start = ((), (), s32[]{:S(2)}) async-start(), calls=%async_computation.10 | async-start | bytes 1638400 | tf_op jit(solution)/shard_map/all_gather | solution.py:774
  21.2 34.3 %collective-permute-start.6 = (bf16[256,2048]{1,0:T(8,128)(2,1)S(1)}, bf16[256,2048]{1,0:T(8,128)(2,1)S(1)}, u32[]{:S(2)}, u32[]{:S(2)}) collective-permute-start(bf16[256,2048]{1,0:T(8,128)(2,1)S(1)} %copy-done.5), channel_id=1, source_target_pairs={{0,16},{4,20},{8,24},{12,28},{16,0},{20,4},{24,8},{28,12},{1,17},{... | collective-permute-start | bytes 3145736 | tf_op jit(solution)/shard_map/ppermute | solution.py:46
  23.3 32.2 %collective-permute-start.5 = (bf16[256,2048]{1,0:T(8,128)(2,1)S(1)}, bf16[256,2048]{1,0:T(8,128)(2,1)S(1)}, u32[]{:S(2)}, u32[]{:S(2)}) collective-permute-start(bf16[256,2048]{1,0:T(8,128)(2,1)S(1)} %copy-done.5), channel_id=1, source_target_pairs={{0,8},{4,12},{8,0},{12,4},{16,24},{20,28},{24,16},{28,20},{1,9},{5... | collective-permute-start | bytes 3145736 | tf_op jit(solution)/shard_map/ppermute | solution.py:46
  27.0 28.5 %all-to-all-start = ((bf16[8,2,64,320]{3,2,1,0:T(8,128)(2,1)}), bf16[8,2,64,320]{3,2,1,0:T(8,128)(2,1)}, u32[]{:S(2)}, u32[]{:S(2)}) async-start(bf16[8,2,64,320]{3,2,1,0:T(8,128)(2,1)} %copy.150), calls=%async_computation | async-start | bytes 1572864 | tf_op jit(solution)/shard_map/all_to_all | solution.py:771
  31.2 63.2 %all-gather.13.cloned.1.call-start = ((), (), s32[]{:S(2)}) async-start(), calls=%async_computation.17 | async-start | bytes 1966080 | tf_op jit(solution)/shard_map/all_gather | solution.py:777
  57.7 92.1 %all-gather.15.cloned.1.call-start = ((), (), s32[]{:S(2)}) async-start(), calls=%async_computation.18 | async-start | bytes 1966080 | tf_op jit(solution)/shard_map/all_gather | solution.py:777
  59.0 14.0 %collective-permute-start.7 = (bf16[128,2048]{1,0:T(8,128)(2,1)S(1)}, bf16[128,2048]{1,0:T(8,128)(2,1)}, u32[]{:S(2)}, u32[]{:S(2)}) collective-permute-start(bf16[128,2048]{1,0:T(8,128)(2,1)S(1)} %slice.331), channel_id=1, source_target_pairs={{0,8},{4,12},{8,0},{12,4},{16,24},{20,28},{24,16},{28,20},{1,9},{5... | collective-permute-start | bytes 1572872 | tf_op jit(solution)/shard_map/ppermute | solution.py:46
  60.6 13.4 %collective-permute-start.8 = (bf16[128,2048]{1,0:T(8,128)(2,1)S(1)}, bf16[128,2048]{1,0:T(8,128)(2,1)}, u32[]{:S(2)}, u32[]{:S(2)}) collective-permute-start(bf16[128,2048]{1,0:T(8,128)(2,1)S(1)} %slice.332), channel_id=1, source_target_pairs={{0,16},{4,20},{8,24},{12,28},{16,0},{20,4},{24,8},{28,12},{1,17},{... | collective-permute-start | bytes 1572872 | tf_op jit(solution)/shard_map/ppermute | solution.py:46
  62.1 16.9 %collective-permute-start.9 = (bf16[256,2048]{1,0:T(8,128)(2,1)S(1)}, bf16[256,2048]{1,0:T(8,128)(2,1)}, u32[]{:S(2)}, u32[]{:S(2)}) collective-permute-start(bf16[256,2048]{1,0:T(8,128)(2,1)S(1)} %copy-done.5), channel_id=1, source_target_pairs={{0,4},{4,0},{8,12},{12,8},{16,20},{20,16},{24,28},{28,24},{1,5},{5... | collective-permute-start | bytes 3145736 | tf_op jit(solution)/shard_map/ppermute | solution.py:46
  62.1 16.9 %collective-permute-start.10 = (bf16[256,2048]{1,0:T(8,128)(2,1)S(1)}, bf16[256,2048]{1,0:T(8,128)(2,1)}, u32[]{:S(2)}, u32[]{:S(2)}) collective-permute-start(bf16[256,2048]{1,0:T(8,128)(2,1)S(1)} %collective-permute-done.5.refs_1_), channel_id=1, source_target_pairs={{0,4},{4,0},{8,12},{12,8},{16,20},{20,16},{24,28},{28,24},{1,5},{5... | collective-permute-start | bytes 3145736 | tf_op jit(solution)/shard_map/ppermute | solution.py:46
  62.6 16.4 %collective-permute-start.11 = (bf16[256,2048]{1,0:T(8,128)(2,1)S(1)}, bf16[256,2048]{1,0:T(8,128)(2,1)}, u32[]{:S(2)}, u32[]{:S(2)}) collective-permute-start(bf16[256,2048]{1,0:T(8,128)(2,1)S(1)} %collective-permute-done.6.refs_2_), channel_id=1, source_target_pairs={{0,4},{4,0},{8,12},{12,8},{16,20},{20,16},{24,28},{28,24},{1,5},{5... | collective-permute-start | bytes 3145736 | tf_op jit(solution)/shard_map/ppermute | solution.py:46
  80.7 39.4 %all-to-all-start.1 = ((bf16[8,64,1536]{2,1,0:T(8,128)(2,1)}), bf16[8,64,1536]{2,1,0:T(8,128)(2,1)}, u32[]{:S(2)}, u32[]{:S(2)}) async-start(bf16[8,64,1536]{2,1,0:T(8,128)(2,1)} %copy.161), calls=%async_computation.1 | async-start | bytes 3145728 | tf_op jit(solution)/shard_map/all_to_all | solution.py:771
  85.0 169.6 %all-gather.17.cloned.1.call-start = ((), (), s32[]{:S(2)}) async-start(), calls=%async_computation.19 | async-start | bytes 7864320 | tf_op jit(solution)/shard_map/all_gather | solution.py:777
  120.1 198.0 %all-gather.11.cloned.1.call-start = ((), (), s32[]{:S(2)}) async-start(), calls=%async_computation.11 | async-start | bytes 3932160 | tf_op jit(solution)/shard_map/all_gather | solution.py:774
  120.3 47.3 %collective-permute-start.22 = (bf16[256,2048]{1,0:T(8,128)(2,1)}, bf16[256,2048]{1,0:T(8,128)(2,1)}, u32[]{:S(2)}, u32[]{:S(2)}) collective-permute-start(bf16[256,2048]{1,0:T(8,128)(2,1)} %fusion.12.refs_0_), channel_id=1, source_target_pairs={{0,24},{4,28},{8,16},{12,20},{16,8},{20,12},{24,0},{28,4},{1,25},{... | collective-permute-start | bytes 3145736 | tf_op jit(solution)/shard_map/ppermute | solution.py:46
  122.8 45.7 %collective-permute-start.21 = (bf16[256,2048]{1,0:T(8,128)(2,1)}, bf16[256,2048]{1,0:T(8,128)(2,1)}, u32[]{:S(2)}, u32[]{:S(2)}) collective-permute-start(bf16[256,2048]{1,0:T(8,128)(2,1)} %fusion.12.refs_0_), channel_id=1, source_target_pairs={{0,16},{4,20},{8,24},{12,28},{16,0},{20,4},{24,8},{28,12},{1,17},{... | collective-permute-start | bytes 3145736 | tf_op jit(solution)/shard_map/ppermute | solution.py:46
  123.3 45.2 %collective-permute-start.20 = (bf16[256,2048]{1,0:T(8,128)(2,1)}, bf16[256,2048]{1,0:T(8,128)(2,1)}, u32[]{:S(2)}, u32[]{:S(2)}) collective-permute-start(bf16[256,2048]{1,0:T(8,128)(2,1)} %fusion.12.refs_0_), channel_id=1, source_target_pairs={{0,8},{4,12},{8,0},{12,4},{16,24},{20,28},{24,16},{28,20},{1,9},{5... | collective-permute-start | bytes 3145736 | tf_op jit(solution)/shard_map/ppermute | solution.py:46
  151.4 15.4 %collective-permute-start.18 = (f32[2,3,16,128]{3,2,1,0:T(8,128)S(1)}, f32[2,3,16,128]{3,2,1,0:T(8,128)S(1)}, u32[]{:S(2)}, u32[]{:S(2)}) collective-permute-start(f32[2,3,16,128]{3,2,1,0:T(8,128)S(1)} %get-tuple-element.241), channel_id=1, source_target_pairs={{0,2},{1,3},{2,0},{3,1},{4,6},{5,7},{6,4},{7,5},{8,10},{9,11},{10,... | collective-permute-start | bytes 147464 | tf_op jit(solution)/shard_map/ppermute | solution.py:46
  196.0 25.5 %collective-permute-start.25 = (bf16[256,2048]{1,0:T(8,128)(2,1)S(1)}, bf16[256,2048]{1,0:T(8,128)(2,1)S(1)}, u32[]{:S(2)}, u32[]{:S(2)}) collective-permute-start(bf16[256,2048]{1,0:T(8,128)(2,1)S(1)} %pad_maximum_fusion.1), channel_id=1, source_target_pairs={{0,8},{4,12},{8,0},{12,4},{16,24},{20,28},{24,16},{28,20},{1,9},{5... | collective-permute-start | bytes 3145736 | tf_op jit(solution)/shard_map/ppermute | solution.py:46
  198.4 25.2 %collective-permute-start.27 = (bf16[256,2048]{1,0:T(8,128)(2,1)S(1)}, bf16[256,2048]{1,0:T(8,128)(2,1)S(1)}, u32[]{:S(2)}, u32[]{:S(2)}) collective-permute-start(bf16[256,2048]{1,0:T(8,128)(2,1)S(1)} %pad_maximum_fusion.2), channel_id=1, source_target_pairs={{0,16},{4,20},{8,24},{12,28},{16,0},{20,4},{24,8},{28,12},{1,17},{... | collective-permute-start | bytes 3145736 | tf_op jit(solution)/shard_map/ppermute | solution.py:46
  201.2 25.0 %collective-permute-start.31 = (bf16[256,2048]{1,0:T(8,128)(2,1)}, bf16[256,2048]{1,0:T(8,128)(2,1)S(1)}, u32[]{:S(2)}, u32[]{:S(2)}) collective-permute-start(bf16[256,2048]{1,0:T(8,128)(2,1)} %fusion.12.refs_0_), channel_id=1, source_target_pairs={{0,4},{4,0},{8,12},{12,8},{16,20},{20,16},{24,28},{28,24},{1,5},{5... | collective-permute-start | bytes 3145736 | tf_op jit(solution)/shard_map/ppermute | solution.py:46
  201.3 28.8 %collective-permute-start.32 = (bf16[256,2048]{1,0:T(8,128)(2,1)}, bf16[256,2048]{1,0:T(8,128)(2,1)}, u32[]{:S(2)}, u32[]{:S(2)}) collective-permute-start(bf16[256,2048]{1,0:T(8,128)(2,1)} %collective-permute-done.20.refs_1_), channel_id=1, source_target_pairs={{0,4},{4,0},{8,12},{12,8},{16,20},{20,16},{24,28},{28,24},{1,5},{5... | collective-permute-start | bytes 3145736 | tf_op jit(solution)/shard_map/ppermute | solution.py:46
  201.8 28.3 %collective-permute-start.33 = (bf16[256,2048]{1,0:T(8,128)(2,1)}, bf16[256,2048]{1,0:T(8,128)(2,1)}, u32[]{:S(2)}, u32[]{:S(2)}) collective-permute-start(bf16[256,2048]{1,0:T(8,128)(2,1)} %collective-permute-done.21.refs_2_), channel_id=1, source_target_pairs={{0,4},{4,0},{8,12},{12,8},{16,20},{20,16},{24,28},{28,24},{1,5},{5... | collective-permute-start | bytes 3145736 | tf_op jit(solution)/shard_map/ppermute | solution.py:46
  224.6 13.5 %collective-permute-start.30 = (bf16[128,2048]{1,0:T(8,128)(2,1)}, bf16[128,2048]{1,0:T(8,128)(2,1)}, u32[]{:S(2)}, u32[]{:S(2)}) collective-permute-start(bf16[128,2048]{1,0:T(8,128)(2,1)} %fusion.24), channel_id=1, source_target_pairs={{0,16},{4,20},{8,24},{12,28},{16,0},{20,4},{24,8},{28,12},{1,17},{... | collective-permute-start | bytes 1572872 | tf_op jit(solution)/shard_map/ppermute | solution.py:46
  229.5 189.8 %reduce-scatter.6.cloned.1.call-start = ((), (), s32[]{:S(2)}) async-start(), calls=%async_computation.12 | async-start | bytes 3932160 | tf_op jit(solution)/shard_map/reduce_scatter | solution.py:876
  242.6 23.4 %collective-permute-start.36 = (bf16[256,2048]{1,0:T(8,128)(2,1)S(1)}, bf16[256,2048]{1,0:T(8,128)(2,1)}, u32[]{:S(2)}, u32[]{:S(2)}) collective-permute-start(bf16[256,2048]{1,0:T(8,128)(2,1)S(1)} %multiply_convert_fusion.1.refs_0_), channel_id=1, source_target_pairs={{0,16},{4,20},{8,24},{12,28},{16,0},{20,4},{24,8},{28,12},{1,17},{... | collective-permute-start | bytes 3145736 | tf_op jit(solution)/shard_map/ppermute | solution.py:46
  244.0 23.0 %collective-permute-start.35 = (bf16[256,2048]{1,0:T(8,128)(2,1)S(1)}, bf16[256,2048]{1,0:T(8,128)(2,1)}, u32[]{:S(2)}, u32[]{:S(2)}) collective-permute-start(bf16[256,2048]{1,0:T(8,128)(2,1)S(1)} %multiply_convert_fusion.1.refs_0_), channel_id=1, source_target_pairs={{0,8},{4,12},{8,0},{12,4},{16,24},{20,28},{24,16},{28,20},{1,9},{5... | collective-permute-start | bytes 3145736 | tf_op jit(solution)/shard_map/ppermute | solution.py:46
  244.9 36.6 %collective-permute-start.39 = (bf16[256,2048]{1,0:T(8,128)(2,1)S(1)}, bf16[256,2048]{1,0:T(8,128)(2,1)}, u32[]{:S(2)}, u32[]{:S(2)}) collective-permute-start(bf16[256,2048]{1,0:T(8,128)(2,1)S(1)} %multiply_convert_fusion.1.refs_0_), channel_id=1, source_target_pairs={{0,4},{4,0},{8,12},{12,8},{16,20},{20,16},{24,28},{28,24},{1,5},{5... | collective-permute-start | bytes 3145736 | tf_op jit(solution)/shard_map/ppermute | solution.py:46
  318.1 206.0 %reduce-scatter.8.cloned.1.call-start = ((), (), s32[]{:S(2)}) async-start(), calls=%async_computation.13 | async-start | bytes 7864320 | tf_op jit(solution)/shard_map/reduce_scatter | solution.py:881
  362.9 34.4 %collective-permute-start.52 = (bf16[1024,2048]{1,0:T(8,128)(2,1)}, bf16[1024,2048]{1,0:T(8,128)(2,1)}, u32[]{:S(2)}, u32[]{:S(2)}) collective-permute-start(bf16[1024,2048]{1,0:T(8,128)(2,1)} %convolution_convert_fusion.1), channel_id=1, source_target_pairs={{0,4},{4,0},{8,12},{12,8},{16,20},{20,16},{24,28},{28,24},{1,5},{5... | collective-permute-start | bytes 12582920 | tf_op jit(solution)/shard_map/ppermute | solution.py:46
  363.1 25.6 %collective-permute-start.46 = (bf16[256,2048]{1,0:T(8,128)(2,1)S(1)}, bf16[256,2048]{1,0:T(8,128)(2,1)}, u32[]{:S(2)}, u32[]{:S(2)}) collective-permute-start(bf16[256,2048]{1,0:T(8,128)(2,1)S(1)} %pad_maximum_fusion.3), channel_id=1, source_target_pairs={{0,8},{4,12},{8,0},{12,4},{16,24},{20,28},{24,16},{28,20},{1,9},{5... | collective-permute-start | bytes 3145736 | tf_op jit(solution)/shard_map/ppermute | solution.py:46
  364.8 25.3 %collective-permute-start.48 = (bf16[256,2048]{1,0:T(8,128)(2,1)S(1)}, bf16[256,2048]{1,0:T(8,128)(2,1)}, u32[]{:S(2)}, u32[]{:S(2)}) collective-permute-start(bf16[256,2048]{1,0:T(8,128)(2,1)S(1)} %pad_maximum_fusion.4), channel_id=1, source_target_pairs={{0,16},{4,20},{8,24},{12,28},{16,0},{20,4},{24,8},{28,12},{1,17},{... | collective-permute-start | bytes 3145736 | tf_op jit(solution)/shard_map/ppermute | solution.py:46
  409.6 145.7 %reduce-scatter.10.cloned.1.call-start = ((), (), s32[]{:S(2)}) async-start(), calls=%async_computation.14 | async-start | bytes 1638400 | tf_op jit(solution)/shard_map/reduce_scatter | solution.py:881
  418.9 22.6 %collective-permute-start.54 = (bf16[256,2048]{1,0:T(8,128)(2,1)S(1)}, bf16[256,2048]{1,0:T(8,128)(2,1)}, u32[]{:S(2)}, u32[]{:S(2)}) collective-permute-start(bf16[256,2048]{1,0:T(8,128)(2,1)S(1)} %get-tuple-element.311.refs_0_), channel_id=1, source_target_pairs={{0,16},{4,20},{8,24},{12,28},{16,0},{20,4},{24,8},{28,12},{1,17},{... | collective-permute-start | bytes 3145736 | tf_op jit(solution)/shard_map/ppermute | solution.py:46
  418.9 22.6 %collective-permute-start.53 = (bf16[256,2048]{1,0:T(8,128)(2,1)S(1)}, bf16[256,2048]{1,0:T(8,128)(2,1)}, u32[]{:S(2)}, u32[]{:S(2)}) collective-permute-start(bf16[256,2048]{1,0:T(8,128)(2,1)S(1)} %get-tuple-element.311.refs_0_), channel_id=1, source_target_pairs={{0,8},{4,12},{8,0},{12,4},{16,24},{20,28},{24,16},{28,20},{1,9},{5... | collective-permute-start | bytes 3145736 | tf_op jit(solution)/shard_map/ppermute | solution.py:46
  419.4 34.8 %collective-permute-start.57 = (bf16[256,2048]{1,0:T(8,128)(2,1)S(1)}, bf16[256,2048]{1,0:T(8,128)(2,1)}, u32[]{:S(2)}, u32[]{:S(2)}) collective-permute-start(bf16[256,2048]{1,0:T(8,128)(2,1)S(1)} %get-tuple-element.311.refs_0_), channel_id=1, source_target_pairs={{0,4},{4,0},{8,12},{12,8},{16,20},{20,16},{24,28},{28,24},{1,5},{5... | collective-permute-start | bytes 3145736 | tf_op jit(solution)/shard_map/ppermute | solution.py:46
  456.2 67.9 %collective-permute-start.65 = (bf16[256,2048]{1,0:T(8,128)(2,1)}, bf16[256,2048]{1,0:T(8,128)(2,1)}, u32[]{:S(2)}, u32[]{:S(2)}) collective-permute-start(bf16[256,2048]{1,0:T(8,128)(2,1)} %get-tuple-element.336), channel_id=1, source_target_pairs={{0,24},{4,28},{8,16},{12,20},{16,8},{20,12},{24,0},{28,4},{1,25},{... | collective-permute-start | bytes 3145736 | tf_op jit(solution)/shard_map/ppermute | solution.py:46
  458.9 65.2 %collective-permute-start.66 = (bf16[256,2048]{1,0:T(8,128)(2,1)}, bf16[256,2048]{1,0:T(8,128)(2,1)}, u32[]{:S(2)}, u32[]{:S(2)}) collective-permute-start(bf16[256,2048]{1,0:T(8,128)(2,1)} %get-tuple-element.337), channel_id=1, source_target_pairs={{0,8},{4,12},{8,0},{12,4},{16,24},{20,28},{24,16},{28,20},{1,9},{5... | collective-permute-start | bytes 3145736 | tf_op jit(solution)/shard_map/ppermute | solution.py:46
  459.4 64.6 %collective-permute-start.67 = (bf16[256,2048]{1,0:T(8,128)(2,1)}, bf16[256,2048]{1,0:T(8,128)(2,1)}, u32[]{:S(2)}, u32[]{:S(2)}) collective-permute-start(bf16[256,2048]{1,0:T(8,128)(2,1)} %get-tuple-element.338), channel_id=1, source_target_pairs={{0,16},{4,20},{8,24},{12,28},{16,0},{20,4},{24,8},{28,12},{1,17},{... | collective-permute-start | bytes 3145736 | tf_op jit(solution)/shard_map/ppermute | solution.py:46
  524.1 82.0 %reduce-scatter.12.cloned.1.call-start = ((), (), s32[]{:S(2)}) async-start(), calls=%async_computation.15 | async-start | bytes 1966080 | tf_op jit(solution)/shard_map/reduce_scatter | solution.py:881
  526.0 21.3 %collective-permute-start.70 = (bf16[48,320]{1,0:T(8,128)(2,1)}, bf16[48,320]{1,0:T(8,128)(2,1)}, u32[]{:S(2)}, u32[]{:S(2)}) collective-permute-start(bf16[48,320]{1,0:T(8,128)(2,1)} %reshape.417), channel_id=1, source_target_pairs={{0,3},{1,2},{2,1},{3,0},{4,7},{5,6},{6,5},{7,4},{8,11},{9,10},{10,... | collective-permute-start | bytes 92168 | tf_op jit(solution)/shard_map/ppermute | solution.py:46
  527.4 19.8 %collective-permute-start.69 = (bf16[48,320]{1,0:T(8,128)(2,1)}, bf16[48,320]{1,0:T(8,128)(2,1)}, u32[]{:S(2)}, u32[]{:S(2)}) collective-permute-start(bf16[48,320]{1,0:T(8,128)(2,1)} %reshape.417), channel_id=1, source_target_pairs={{0,2},{1,3},{2,0},{3,1},{4,6},{5,7},{6,4},{7,5},{8,10},{9,11},{10,... | collective-permute-start | bytes 92168 | tf_op jit(solution)/shard_map/ppermute | solution.py:46
  529.4 17.8 %collective-permute-start.68 = (bf16[48,320]{1,0:T(8,128)(2,1)}, bf16[48,320]{1,0:T(8,128)(2,1)}, u32[]{:S(2)}, u32[]{:S(2)}) collective-permute-start(bf16[48,320]{1,0:T(8,128)(2,1)} %reshape.417), channel_id=1, source_target_pairs={{0,1},{1,0},{2,3},{3,2},{4,5},{5,4},{6,7},{7,6},{8,9},{9,8},{10,11... | collective-permute-start | bytes 92168 | tf_op jit(solution)/shard_map/ppermute | solution.py:46
  566.6 39.5 %all-to-all-start.3 = ((bf16[8,64,1536]{2,1,0:T(8,128)(2,1)}), bf16[8,64,1536]{2,1,0:T(8,128)(2,1)S(1)}, u32[]{:S(2)}, u32[]{:S(2)}) async-start(bf16[8,64,1536]{2,1,0:T(8,128)(2,1)} %bitcast.274), calls=%async_computation.7 | async-start | bytes 3145728 | tf_op jit(solution)/shard_map/all_to_all | solution.py:771
  570.3 81.5 %reduce-scatter.14.cloned.1.call-start = ((), (), s32[]{:S(2)}) async-start(), calls=%async_computation.16 | async-start | bytes 2334720 | tf_op jit(solution)/shard_map/reduce_scatter | solution.py:881
  593.5 26.3 %collective-permute-start.75 = (bf16[256,2048]{1,0:T(8,128)(2,1)}, bf16[256,2048]{1,0:T(8,128)(2,1)}, u32[]{:S(2)}, u32[]{:S(2)}) collective-permute-start(bf16[256,2048]{1,0:T(8,128)(2,1)} %pad_maximum_fusion.5), channel_id=1, source_target_pairs={{0,8},{4,12},{8,0},{12,4},{16,24},{20,28},{24,16},{28,20},{1,9},{5... | collective-permute-start | bytes 3145736 | tf_op jit(solution)/shard_map/ppermute | solution.py:46
  600.8 28.3 %collective-permute-start.76 = (bf16[256,2048]{1,0:T(8,128)(2,1)S(1)}, bf16[256,2048]{1,0:T(8,128)(2,1)}, u32[]{:S(2)}, u32[]{:S(2)}) collective-permute-start(bf16[256,2048]{1,0:T(8,128)(2,1)S(1)} %pad_maximum_fusion.6), channel_id=1, source_target_pairs={{0,16},{4,20},{8,24},{12,28},{16,0},{20,4},{24,8},{28,12},{1,17},{... | collective-permute-start | bytes 3145736 | tf_op jit(solution)/shard_map/ppermute | solution.py:46
  606.2 30.8 %all-to-all-start.2 = ((bf16[8,64,320]{2,1,0:T(8,128)(2,1)}), bf16[8,64,320]{2,1,0:T(8,128)(2,1)S(1)}, u32[]{:S(2)}, u32[]{:S(2)}) async-start(bf16[8,64,320]{2,1,0:T(8,128)(2,1)} %bitcast.282), calls=%async_computation.6 | async-start | bytes 786432 | tf_op jit(solution)/shard_map/all_to_all | solution.py:771
  (151 other events, 1203.8 us)
Sparse Core Ops, SparseCore 0:
  10.2 36.2 all-gather.8
  57.8 36.6 all-gather.12
  96.6 39.1 all-gather.14
  137.2 117.2 all-gather.16
  255.9 62.0 all-gather.10
  320.2 58.8 reduce-scatter.5
  409.7 109.0 reduce-scatter.7
  524.2 31.0 reduce-scatter.9
  566.8 34.8 reduce-scatter.11
  606.3 38.5 reduce-scatter.13
